TPU v7x, 32 devices: a whole 2x2x4 slice. The times are simulated.
32 devices in a mesh: dp: 2 (over y), ctx: 16 (over z, x, core).
Axes of the slice: x: 2, y: 2, z: 4, core: 2. Of those that a mesh axis runs over, the one named last changes fastest.
Arguments:
- inputs: bfloat16 [4, 2048, 768], P('dp', 'ctx'), may hold values from -6 to 6
- w_query: bfloat16 [768, 768], P(('dp', 'ctx')), may hold values from -0.0546875 to 0.0546875
- w_key: bfloat16 [768, 768], P(('dp', 'ctx')), may hold values from -0.21875 to 0.21875
- w_value: bfloat16 [768, 768], P(('dp', 'ctx')), may hold values from -0.21875 to 0.21875
- w_output: bfloat16 [768, 768], P(('dp', 'ctx')), may hold values from -1.25 to 1.25
- w_gate: bfloat16 [768, 2048], P(('dp', 'ctx')), may hold values from -0.21875 to 0.21875
- w_upper: bfloat16 [768, 2048], P(('dp', 'ctx')), may hold values from -0.21875 to 0.21875
- w_down: bfloat16 [2048, 768], P(('dp', 'ctx')), may hold values from -0.125 to 0.125
- gain_one: bfloat16 [768], P(('dp', 'ctx')), may hold values from 0.099609375 to 1.8984375
- gain_two: bfloat16 [768], P(('dp', 'ctx')), may hold values from 0.099609375 to 1.8984375
- bias_table: bfloat16 [384], P(('dp', 'ctx')), may hold values from -4 to 4
- buckets: int32 [4095], replicated, may hold values from 0 to 31
- cotangent: bfloat16 [4, 2048, 768], P('dp', 'ctx'), may hold values from -6 to 6
Outputs:
- outputs: bfloat16 [4, 2048, 768], P('dp', 'ctx')
- input_grad: float32 [4, 2048, 768], P('dp', 'ctx')
- grad_w_query: float32 [768, 768], P(('dp', 'ctx'))
- grad_w_key: float32 [768, 768], P(('dp', 'ctx'))
- grad_w_value: float32 [768, 768], P(('dp', 'ctx'))
- grad_w_output: float32 [768, 768], P(('dp', 'ctx'))
- grad_w_gate: float32 [768, 2048], P(('dp', 'ctx'))
- grad_w_upper: float32 [768, 2048], P(('dp', 'ctx'))
- grad_w_down: float32 [2048, 768], P(('dp', 'ctx'))
- grad_gain_one: float32 [768], P(('dp', 'ctx'))
- grad_gain_two: float32 [768], P(('dp', 'ctx'))
- grad_bias_table: float32 [384], P(('dp', 'ctx'))
Inputs may be any that keep to these rules, and one draw needn't show every extreme that they name: `buckets`: each entry names a bucket of the bias table.
All inputs are finite; a program needn't handle non-finite values.
Results may differ from a plain program's by a relative error of at most 0.025.
Values may be sent and summed in bfloat16 or wider, within the bound.
No kernel may reach another device: no remote copies, remote signals or barrier semaphores. Data moves between devices by JAX's collectives and lax.ppermute only.
A program may use at most 320 MiB of HBM per device.

v0:
```python
import jax
import jax.numpy as jnp
from jax import lax
from jax.sharding import PartitionSpec as P

H = 12
FF = 2048
BUCKETS = 32


epsilon = 1e-06
exactly = lax.Precision.HIGHEST


def rms_scale(values, gain_vec):
    return (
        values * lax.rsqrt(jnp.mean(values * values, axis=-1, keepdims=True) + epsilon) * gain_vec
    )


def gelu_product(gate_in, up_in):
    return jax.nn.gelu(gate_in, approximate=True) * up_in


def split_heads(matrix, head_count):
    row_count = matrix.shape[0]
    return jnp.transpose(
        matrix.reshape(row_count, head_count, matrix.shape[1] // head_count), (1, 0, 2)
    )


def merge_heads(stacked):
    return jnp.transpose(stacked, (1, 0, 2)).reshape(
        stacked.shape[1], stacked.shape[0] * stacked.shape[2]
    )


def inner_rows(first_op, second_op):
    return lax.dot_general(
        first_op, second_op, (((0,), (0,)), ((), ())), preferred_element_type=jnp.float32
    )


def outer_rows(first_op, second_op):
    return lax.dot_general(
        first_op, second_op, (((1,), (1,)), ((), ())), preferred_element_type=jnp.float32
    )


def spread_bias(offset_bias, query_first, key_first, query_rows, key_cols):
    head_count, offset_count = offset_bias.shape
    seq_length = (offset_count + 1) // 2
    span_width = query_rows + key_cols - 1
    window = lax.dynamic_slice_in_dim(
        offset_bias, key_first - query_first + seq_length - query_rows, span_width, 1
    )
    tiled_rows = jnp.broadcast_to(window[:, None, :], (head_count, query_rows, span_width))
    tiled_rows = jnp.pad(
        tiled_rows.reshape(head_count, query_rows * span_width), ((0, 0), (0, query_rows))
    )
    skewed = tiled_rows.reshape(head_count, query_rows, span_width + 1)[:, :, :key_cols]
    return skewed[:, ::-1, :]


def add_diagonals(offset_grad, score_grad, query_first, key_first):
    head_count, query_rows, key_cols = score_grad.shape
    seq_length = (offset_grad.shape[1] + 1) // 2
    span_width = key_cols + query_rows - 1
    flipped = score_grad.astype(jnp.float32)[:, ::-1, :]
    padded = jnp.pad(flipped, ((0, 0), (0, 0), (0, query_rows))).reshape(
        head_count, query_rows * (span_width + 1)
    )
    skewed = padded[:, : query_rows * span_width].reshape(head_count, query_rows, span_width)
    diag_sums = jnp.sum(skewed, axis=1)
    corner = key_first - query_first + seq_length - query_rows
    window = lax.dynamic_slice_in_dim(offset_grad, corner, span_width, 1)
    return lax.dynamic_update_slice_in_dim(offset_grad, window + diag_sums, corner, 1)


def score_block(query_heads, key_heads, offset_bias, query_first, key_first):
    scores = jnp.einsum("hqd,hkd->hqk", query_heads, key_heads, preferred_element_type=jnp.float32)
    return scores + spread_bias(
        offset_bias, query_first, key_first, query_heads.shape[1], key_heads.shape[1]
    )


def block_grads(
    query_heads,
    key_heads,
    value_heads,
    grad_heads,
    row_lse,
    row_delta,
    offset_bias,
    query_first,
    key_first,
):
    scores = score_block(query_heads, key_heads, offset_bias, query_first, key_first)
    probabilities = jnp.exp(scores - row_lse[:, :, None])
    prob_grad = jnp.einsum(
        "hqd,hkd->hqk", grad_heads, value_heads, preferred_element_type=jnp.float32
    )
    score_grad = (probabilities * (prob_grad - row_delta[:, :, None])).astype(jnp.bfloat16)
    return (probabilities.astype(jnp.bfloat16), score_grad)


def forward_fold(query_heads, offset_bias, query_first, head_count, fold_state, shard_piece):
    key_rows, value_rows = shard_piece
    row_count, model_width = key_rows.shape
    block_rows = 512
    block_count = row_count // block_rows

    def forward_advance(running, block_item):
        running_max, running_sum, weighted = running
        key_block, value_block, number = block_item
        scores = score_block(
            query_heads,
            split_heads(key_block, head_count),
            offset_bias,
            query_first,
            number * block_rows,
        )
        new_max = jnp.maximum(running_max, jnp.max(scores, axis=-1))
        factor = jnp.exp(running_max - new_max)
        weights_block = jnp.exp(scores - new_max[:, :, None])
        running_sum = running_sum * factor + jnp.sum(weights_block, axis=-1)
        weighted = weighted * factor[:, :, None] + jnp.einsum(
            "hqk,hkd->hqd",
            weights_block.astype(jnp.bfloat16),
            split_heads(value_block, head_count),
            preferred_element_type=jnp.float32,
        )
        return ((new_max, running_sum, weighted), None)

    blocks = (
        key_rows.reshape(block_count, block_rows, model_width),
        value_rows.reshape(block_count, block_rows, model_width),
        jnp.arange(block_count, dtype=jnp.int32),
    )
    fold_state, unused = lax.scan(forward_advance, fold_state, blocks)
    return fold_state


def body(
    inputs,
    w_query,
    w_key,
    w_value,
    w_output,
    w_gate,
    w_upper,
    w_down,
    gain_one,
    gain_two,
    bias_table,
    buckets,
    cotangent,
):
    head_count = H
    seq_count, local_rows, model_width = inputs.shape
    seq_length = buckets.shape[0] // 2 + 1
    head_width = model_width // head_count
    query_first = lax.axis_index("ctx") * local_rows
    one_hot = (buckets[:, None] == jnp.arange(BUCKETS, dtype=jnp.int32)[None, :]).astype(
        jnp.bfloat16
    )
    square_zeros = jnp.zeros((model_width, model_width), jnp.float32)
    wide_zeros = jnp.zeros((model_width, FF), jnp.float32)
    gain_zeros = jnp.zeros((model_width,), jnp.float32)
    grad_sums = [
        square_zeros,
        square_zeros,
        square_zeros,
        square_zeros,
        wide_zeros,
        wide_zeros,
        jnp.zeros((FF, model_width), jnp.float32),
        gain_zeros,
        gain_zeros,
    ]
    offset_sums = jnp.zeros((head_count, 2 * seq_length - 1), jnp.float32)
    outputs_list = []
    input_grads = []
    for micro_index in range(seq_count):
        gathered = (
            lax.all_gather(w_query, ("dp", "ctx"), axis=0, tiled=True),
            lax.all_gather(w_key, ("dp", "ctx"), axis=0, tiled=True),
            lax.all_gather(w_value, ("dp", "ctx"), axis=0, tiled=True),
            lax.all_gather(w_output, ("dp", "ctx"), axis=0, tiled=True),
            lax.all_gather(w_gate, ("dp", "ctx"), axis=0, tiled=True),
            lax.all_gather(w_upper, ("dp", "ctx"), axis=0, tiled=True),
            lax.all_gather(w_down, ("dp", "ctx"), axis=0, tiled=True),
            lax.all_gather(gain_one, ("dp", "ctx"), axis=0, tiled=True),
            lax.all_gather(gain_two, ("dp", "ctx"), axis=0, tiled=True),
            lax.all_gather(bias_table, ("dp", "ctx"), axis=0, tiled=True),
        )
        query_w, key_w, value_w, output_w, gate_w, upper_w, down_w, gain_a, gain_b, table_all = (
            gathered
        )
        offset_bias = jnp.transpose(
            jnp.dot(
                one_hot, table_all.reshape(BUCKETS, head_count), preferred_element_type=jnp.float32
            )
        )
        token_rows = inputs[micro_index].astype(jnp.float32)
        normed_low = rms_scale(token_rows, gain_a.astype(jnp.float32)).astype(jnp.bfloat16)
        queries = jnp.dot(normed_low, query_w, preferred_element_type=jnp.float32).astype(
            jnp.bfloat16
        )
        key_rows = jnp.dot(normed_low, key_w, preferred_element_type=jnp.float32).astype(
            jnp.bfloat16
        )
        value_rows = jnp.dot(normed_low, value_w, preferred_element_type=jnp.float32).astype(
            jnp.bfloat16
        )
        query_heads = split_heads(queries, head_count)
        start_state = (
            jnp.full((head_count, local_rows), -1e30, jnp.float32),
            jnp.zeros((head_count, local_rows), jnp.float32),
            jnp.zeros((head_count, local_rows, head_width), jnp.float32),
        )
        running_max, running_sum, weighted = forward_fold(
            query_heads,
            offset_bias,
            query_first,
            head_count,
            start_state,
            (
                lax.all_gather(key_rows, "ctx", axis=0, tiled=True),
                lax.all_gather(value_rows, "ctx", axis=0, tiled=True),
            ),
        )
        row_lse = running_max + jnp.log(running_sum)
        attended = weighted / running_sum[:, :, None]
        context = merge_heads(attended).astype(jnp.bfloat16)
        residual = token_rows + jnp.dot(context, output_w, preferred_element_type=jnp.float32)
        second_low = rms_scale(residual, gain_b.astype(jnp.float32)).astype(jnp.bfloat16)
        gate_pre = jnp.dot(second_low, gate_w, preferred_element_type=jnp.float32)
        up_pre = jnp.dot(second_low, upper_w, preferred_element_type=jnp.float32)
        hidden = gelu_product(gate_pre, up_pre).astype(jnp.bfloat16)
        outputs_list.append(
            (residual + jnp.dot(hidden, down_w, preferred_element_type=jnp.float32)).astype(
                jnp.bfloat16
            )
        )
        gathered = (
            lax.all_gather(w_query, ("dp", "ctx"), axis=0, tiled=True),
            lax.all_gather(w_key, ("dp", "ctx"), axis=0, tiled=True),
            lax.all_gather(w_value, ("dp", "ctx"), axis=0, tiled=True),
            lax.all_gather(w_output, ("dp", "ctx"), axis=0, tiled=True),
            lax.all_gather(w_gate, ("dp", "ctx"), axis=0, tiled=True),
            lax.all_gather(w_upper, ("dp", "ctx"), axis=0, tiled=True),
            lax.all_gather(w_down, ("dp", "ctx"), axis=0, tiled=True),
            lax.all_gather(gain_one, ("dp", "ctx"), axis=0, tiled=True),
            lax.all_gather(gain_two, ("dp", "ctx"), axis=0, tiled=True),
            lax.all_gather(bias_table, ("dp", "ctx"), axis=0, tiled=True),
        )
        query_w, key_w, value_w, output_w, gate_w, upper_w, down_w, gain_a, gain_b, table_all = (
            gathered
        )
        offset_bias = jnp.transpose(
            jnp.dot(
                one_hot, table_all.reshape(BUCKETS, head_count), preferred_element_type=jnp.float32
            )
        )
        down_grad = cotangent[micro_index]
        grad_out = down_grad.astype(jnp.float32)
        hidden_grad = outer_rows(down_grad, down_w)
        unused, gelu_pull = jax.vjp(gelu_product, gate_pre, up_pre)
        gate_grad, up_grad = gelu_pull(hidden_grad)
        gate_low = gate_grad.astype(jnp.bfloat16)
        up_low = up_grad.astype(jnp.bfloat16)
        norm_grad = outer_rows(gate_low, gate_w) + outer_rows(up_low, upper_w)
        unused, norm_pull = jax.vjp(rms_scale, residual, gain_b.astype(jnp.float32))
        residual_part, gain_b_grad = norm_pull(norm_grad)
        residual_grad = grad_out + residual_part
        attn_low = residual_grad.astype(jnp.bfloat16)
        context_low = outer_rows(attn_low, output_w).astype(jnp.bfloat16)
        grad_heads = split_heads(context_low, head_count)
        row_delta = jnp.sum(grad_heads.astype(jnp.float32) * attended, axis=-1)
        initial = (
            jnp.zeros((head_count, local_rows, head_width), jnp.float32),
            jnp.zeros((head_count, 2 * seq_length - 1), jnp.float32),
        )
        keys_all, values_all = (
            lax.all_gather(key_rows, "ctx", axis=0, tiled=True),
            lax.all_gather(value_rows, "ctx", axis=0, tiled=True),
        )
        block_rows = 512
        block_count = seq_length // block_rows

        def body_advance(running, block_item):
            query_grad, offset_grad = running
            key_block, value_block, number = block_item
            key_first = number * block_rows
            key_heads = split_heads(key_block, head_count)
            probs_low, score_grad = block_grads(
                query_heads,
                key_heads,
                split_heads(value_block, head_count),
                grad_heads,
                row_lse,
                row_delta,
                offset_bias,
                query_first,
                key_first,
            )
            query_grad = query_grad + jnp.einsum(
                "hqk,hkd->hqd", score_grad, key_heads, preferred_element_type=jnp.float32
            )
            key_part = jnp.einsum(
                "hqk,hqd->hkd", score_grad, query_heads, preferred_element_type=jnp.float32
            )
            value_part = jnp.einsum(
                "hqk,hqd->hkd", probs_low, grad_heads, preferred_element_type=jnp.float32
            )
            offset_grad = add_diagonals(offset_grad, score_grad, query_first, key_first)
            return (
                (query_grad, offset_grad),
                jnp.concatenate([merge_heads(key_part), merge_heads(value_part)], axis=1),
            )

        blocks = (
            keys_all.reshape(block_count, block_rows, model_width),
            values_all.reshape(block_count, block_rows, model_width),
            jnp.arange(block_count, dtype=jnp.int32),
        )
        (query_grad, offset_grad), key_terms = lax.scan(body_advance, initial, blocks)
        summed = lax.psum_scatter(
            key_terms.reshape(seq_length, 2 * model_width), "ctx", scatter_dimension=0, tiled=True
        )
        key_grad = summed[:, :model_width].astype(jnp.bfloat16)
        value_grad = summed[:, model_width:].astype(jnp.bfloat16)
        query_low = merge_heads(query_grad).astype(jnp.bfloat16)
        offset_sums = offset_sums + offset_grad
        normed_grad = (
            outer_rows(query_low, query_w)
            + outer_rows(key_grad, key_w)
            + outer_rows(value_grad, value_w)
        )
        unused, first_pull = jax.vjp(rms_scale, token_rows, gain_a.astype(jnp.float32))
        token_part, gain_a_grad = first_pull(normed_grad)
        input_grads.append(residual_grad + token_part)
        updates = (
            inner_rows(normed_low, query_low),
            inner_rows(normed_low, key_grad),
            inner_rows(normed_low, value_grad),
            inner_rows(context, attn_low),
            inner_rows(second_low, gate_low),
            inner_rows(second_low, up_low),
            inner_rows(hidden, down_grad),
            gain_a_grad,
            gain_b_grad,
        )
        grad_sums = [earlier + update for earlier, update in zip(grad_sums, updates)]
    table_grad = jnp.transpose(
        jnp.dot(offset_sums, one_hot.astype(jnp.float32), precision=exactly)
    ).reshape(BUCKETS * head_count)
    owned_grads = (
        lax.psum_scatter(grad_sums[0], ("dp", "ctx"), scatter_dimension=0, tiled=True),
        lax.psum_scatter(grad_sums[1], ("dp", "ctx"), scatter_dimension=0, tiled=True),
        lax.psum_scatter(grad_sums[2], ("dp", "ctx"), scatter_dimension=0, tiled=True),
        lax.psum_scatter(grad_sums[3], ("dp", "ctx"), scatter_dimension=0, tiled=True),
        lax.psum_scatter(grad_sums[4], ("dp", "ctx"), scatter_dimension=0, tiled=True),
        lax.psum_scatter(grad_sums[5], ("dp", "ctx"), scatter_dimension=0, tiled=True),
        lax.psum_scatter(grad_sums[6], ("dp", "ctx"), scatter_dimension=0, tiled=True),
        lax.psum_scatter(grad_sums[7], ("dp", "ctx"), scatter_dimension=0, tiled=True),
        lax.psum_scatter(grad_sums[8], ("dp", "ctx"), scatter_dimension=0, tiled=True),
        lax.psum_scatter(table_grad, ("dp", "ctx"), scatter_dimension=0, tiled=True),
    )
    return (
        jnp.stack(outputs_list),
        jnp.stack(input_grads),
        owned_grads[0],
        owned_grads[1],
        owned_grads[2],
        owned_grads[3],
        owned_grads[4],
        owned_grads[5],
        owned_grads[6],
        owned_grads[7],
        owned_grads[8],
        owned_grads[9],
    )


def solution(mesh):
    in_specs = (
        P("dp", "ctx", None),
        P(("dp", "ctx"), None),
        P(("dp", "ctx"), None),
        P(("dp", "ctx"), None),
        P(("dp", "ctx"), None),
        P(("dp", "ctx"), None),
        P(("dp", "ctx"), None),
        P(("dp", "ctx"), None),
        P(("dp", "ctx")),
        P(("dp", "ctx")),
        P(("dp", "ctx")),
        P(),
        P("dp", "ctx", None),
    )
    out_specs = (
        P("dp", "ctx", None),
        P("dp", "ctx", None),
        P(("dp", "ctx"), None),
        P(("dp", "ctx"), None),
        P(("dp", "ctx"), None),
        P(("dp", "ctx"), None),
        P(("dp", "ctx"), None),
        P(("dp", "ctx"), None),
        P(("dp", "ctx"), None),
        P(("dp", "ctx")),
        P(("dp", "ctx")),
        P(("dp", "ctx")),
    )
    return jax.shard_map(body, mesh=mesh, in_specs=in_specs, out_specs=out_specs, check_vma=False)
```

profile of v0, /device:TPU:0, one launch (start us, length us, event | category | flops | bytes accessed | tf_op | source)
XLA Modules:
  0.0 2492.0 jit_solution(17830705981493418291)
XLA Ops:
  12.0 42.1 %all-reduce.13 = (bf16[768]{0:T(1024)(128)(2,1)S(1)}, bf16[384]{0:T(512)(128)(2,1)S(1)}, bf16[768]{0:T(1024)(128)(2,1)S(1)}) all-reduce(bf16[768]{0:T(1024)(128)(2,1)S(1)} %dynamic-update-slice, bf16[384]{0:T(512)(128)(2,1)S(1)} %dynamic-update-slice.1, ...), channel_id=1, replica_groups=mesh['dp'=2,'ctx'=16] {'dp','ctx'}, use_global_device_ids=true, to_apply=%add.6 | all-reduce | flops 1920 | bytes 7680
  55.4 12.3 all-gather.18.cloned.1.call-done
  70.3 53.2 %all-gather.12.cloned.1.call-done = bf16[768,768]{1,0:T(8,128)(2,1)} async-done(((bf16[24,768]{1,0:T(8,128)(2,1)}), bf16[768,768]{1,0:T(8,128)(2,1)}) %all-gather.12.cloned.1.call-update) | async-done | bytes 1179664 | tf_op jit(solution)/shard_map/all_gather | solution.py:187
  132.9 46.5 %all-gather.16.cloned.1.call-done = bf16[768,768]{1,0:T(8,128)(2,1)} async-done(((bf16[24,768]{1,0:T(8,128)(2,1)}), bf16[768,768]{1,0:T(8,128)(2,1)}) %all-gather.16.cloned.1.call-update) | async-done | bytes 1179664 | tf_op jit(solution)/shard_map/all_gather | solution.py:186
  183.0 43.2 %all-gather.20.cloned.1.call-done = bf16[2048,768]{1,0:T(8,128)(2,1)} async-done(((bf16[128,768]{1,0:T(8,128)(2,1)}), bf16[2048,768]{1,0:T(8,128)(2,1)}) %all-gather.20.cloned.1.call-update) | async-done | bytes 3145744 | tf_op jit(solution)/shard_map/all_gather | solution.py:230
  230.9 42.1 %all-gather.30.cloned.1.call-done = bf16[2048,768]{1,0:T(8,128)(2,1)} async-done(((bf16[128,768]{1,0:T(8,128)(2,1)}), bf16[2048,768]{1,0:T(8,128)(2,1)}) %all-gather.30.cloned.1.call-update) | async-done | bytes 3145744 | tf_op jit(solution)/shard_map/all_gather | solution.py:229
  277.6 42.3 %all-gather.32.cloned.1.call-done = bf16[2048,768]{1,0:T(8,128)(2,1)} async-done(((bf16[128,768]{1,0:T(8,128)(2,1)}), bf16[2048,768]{1,0:T(8,128)(2,1)}) %all-gather.32.cloned.1.call-update) | async-done | bytes 3145744 | tf_op jit(solution)/shard_map/all_gather | solution.py:230
  324.7 42.2 %all-gather.14.cloned.1.call-done = bf16[2048,768]{1,0:T(8,128)(2,1)} async-done(((bf16[128,768]{1,0:T(8,128)(2,1)}), bf16[2048,768]{1,0:T(8,128)(2,1)}) %all-gather.14.cloned.1.call-update) | async-done | bytes 3145744 | tf_op jit(solution)/shard_map/all_gather | solution.py:229
  371.5 186.9 %while.76 = (s32[]{:T(128)}, f32[12,128]{1,0:T(8,128)S(1)}, f32[12,128]{1,0:T(8,128)}, f32[12,128,64]{1,2,0:T(8,128)}, bf16[4,512,768]{1,2,0:T(8,128)(2,1)}, /*i...) while((s32[]{:T(128)}, f32[12,128]{1,0:T(8,128)S(1)}, ...), condition=%wide.region_4.5_spmd.clone, body=%wide.region_1.4_spmd.clone.sunk | while | flops 206347776 | bytes 73812416 | solution.py:140
  391.2 22.3 rev.66
  438.0 22.3 rev.66
  484.8 22.4 rev.66
  531.5 22.4 rev.66
  562.7 187.1 %while.77 = (s32[]{:T(128)}, f32[12,128]{1,0:T(8,128)S(1)}, f32[12,128]{1,0:T(8,128)}, f32[12,128,64]{1,2,0:T(8,128)}, bf16[4,512,768]{1,2,0:T(8,128)(2,1)}, /*i...) while((s32[]{:T(128)}, f32[12,128]{1,0:T(8,128)S(1)}, ...), condition=%wide.region_10.11_spmd.clone, body=%wide.region_7.10_spmd.clone.sunk | while | flops 206347776 | bytes 73812416 | solution.py:140
  582.7 22.4 rev.67
  629.5 22.3 rev.67
  676.1 22.3 rev.67
  722.8 22.3 rev.67
  789.3 392.2 %while.79 = (s32[]{:T(128)}, f32[12,128,64]{1,2,0:T(8,128)}, f32[12,4095]{1,0:T(8,128)}, f32[4,512,1536]{2,1,0:T(8,128)}, bf16[4,512,768]{1,2,0:T(8,128)(2,1)}, ...) while((s32[]{:T(128)}, f32[12,128,64]{1,2,0:T(8,128)}, ...), condition=%wide.region_23.24_spmd.clone, body=%wide.region_21.23_spmd.clone.sunk | while | flops 509999616 | bytes 175083536 | solution.py:328
  821.9 22.3 rev.70
  855.7 17.1 rev.71
  916.8 22.3 rev.70
  950.7 17.1 rev.71
  976.6 6.9 reshape.487
  1011.8 22.3 rev.70
  1045.6 17.1 rev.71
  1071.5 6.9 reshape.487
  1106.8 22.3 rev.70
  1140.6 17.1 rev.71
  1184.9 7.5 broadcast.188.clone2.1
  1192.4 380.7 %while.78 = (s32[]{:T(128)}, f32[12,128,64]{1,2,0:T(8,128)}, f32[12,4095]{1,0:T(8,128)}, f32[4,512,1536]{2,1,0:T(8,128)}, bf16[4,512,768]{1,2,0:T(8,128)(2,1)}, ...) while((s32[]{:T(128)}, f32[12,128,64]{1,2,0:T(8,128)}, ...), condition=%wide.region_16.17_spmd.clone, body=%wide.region_14.16_spmd.clone.sunk | while | flops 509999616 | bytes 175083536 | solution.py:328
  1213.7 22.4 rev.68
  1247.6 17.0 rev.69
  1308.7 22.3 rev.68
  1342.5 17.0 rev.69
  1403.5 22.3 rev.68
  1437.3 17.0 rev.69
  1498.3 22.3 rev.68
  1532.1 17.0 rev.69
  1598.6 109.0 %reduce-scatter.10.cloned.1.call-done = f32[128,1536]{1,0:T(8,128)} async-done(((f32[2048,1536]{1,0:T(8,128)}), f32[128,1536]{1,0:T(8,128)}) %reduce-scatter.10.cloned.1.call-update) | async-done | bytes 786448 | tf_op jit(solution)/shard_map/reduce_scatter | solution.py:329
  1726.8 39.7 %all-reduce.12 = (f32[768]{0:T(1024)S(1)}, f32[768]{0:T(1024)S(1)}, f32[384]{0:T(512)S(1)}) all-reduce(f32[768]{0:T(1024)S(1)} %add.461, f32[768]{0:T(1024)S(1)} %copy-done.90, f32[384]{0:T(512)S(1)} %copy-done.91), channel_id=11, replica_groups=mesh['dp'=2,'ctx'=16] {'dp','ctx'}, use_global_device_ids=true, to_apply=%region_35.36.clone | all-reduce | flops 1920 | bytes 15360
  1769.4 42.4 %reduce-scatter.20.cloned.1.call-done = f32[24,768]{1,0:T(8,128)} async-done(((f32[768,768]{1,0:T(8,128)}), f32[24,768]{1,0:T(8,128)}) %reduce-scatter.20.cloned.1.call-update) | async-done | bytes 73744 | tf_op jit(solution)/shard_map/reduce_scatter | solution.py:363
  1811.8 104.6 %reduce-scatter.14.cloned.1.call-done = f32[24,768]{1,0:T(8,128)} async-done(((f32[768,768]{1,0:T(8,128)}), f32[24,768]{1,0:T(8,128)}) %reduce-scatter.14.cloned.1.call-update) | async-done | bytes 73744 | tf_op jit(solution)/shard_map/reduce_scatter | solution.py:360
  1916.4 119.4 %reduce-scatter.24.cloned.1.call-done = f32[24,2048]{1,0:T(8,128)} async-done(((f32[768,2048]{1,0:T(8,128)}), f32[24,2048]{1,0:T(8,128)}) %reduce-scatter.24.cloned.1.call-update) | async-done | bytes 196624 | tf_op jit(solution)/shard_map/reduce_scatter | solution.py:365
  2035.8 120.5 %reduce-scatter.22.cloned.1.call-done = f32[24,2048]{1,0:T(8,128)} async-done(((f32[768,2048]{1,0:T(8,128)}), f32[24,2048]{1,0:T(8,128)}) %reduce-scatter.22.cloned.1.call-update) | async-done | bytes 196624 | tf_op jit(solution)/shard_map/reduce_scatter | solution.py:364
  2156.3 119.9 %reduce-scatter.26.cloned.1.call-done = f32[64,768]{1,0:T(8,128)} async-done(((f32[2048,768]{1,0:T(8,128)}), f32[64,768]{1,0:T(8,128)}) %reduce-scatter.26.cloned.1.call-update) | async-done | bytes 196624 | tf_op jit(solution)/shard_map/reduce_scatter | solution.py:366
  2276.2 105.0 %reduce-scatter.16.cloned.1.call-done = f32[24,768]{1,0:T(8,128)} async-done(((f32[768,768]{1,0:T(8,128)}), f32[24,768]{1,0:T(8,128)}) %reduce-scatter.16.cloned.1.call-update) | async-done | bytes 73744 | tf_op jit(solution)/shard_map/reduce_scatter | solution.py:361
  2381.1 103.8 %reduce-scatter.18.cloned.1.call-done = f32[24,768]{1,0:T(8,128)} async-done(((f32[768,768]{1,0:T(8,128)}), f32[24,768]{1,0:T(8,128)}) %reduce-scatter.18.cloned.1.call-update) | async-done | bytes 73744 | tf_op jit(solution)/shard_map/reduce_scatter | solution.py:362
  (832 shorter events, 747.2 us)
Async XLA Ops:
  7.2 118.9 %copy-start.12 = (bf16[2,128,768]{2,1,0:T(8,128)(2,1)S(1)}, bf16[2,128,768]{2,1,0:T(8,128)(2,1)}, u32[]{:S(2)}) copy-start(bf16[2,128,768]{2,1,0:T(8,128)(2,1)} %param.21) | copy-start | bytes 1179652
  7.2 60.5 %all-gather.18.cloned.1.call-start = ((), (), s32[]{:S(2)}) async-start(), calls=%async_computation.12 | async-start | bytes 1216512 | tf_op jit(solution)/shard_map/all_gather | solution.py:188
  7.9 115.6 %all-gather.12.cloned.1.call-start = ((), (), s32[]{:S(2)}) async-start(), calls=%async_computation.9 | async-start | bytes 1216512 | tf_op jit(solution)/shard_map/all_gather | solution.py:187
  8.7 170.7 %all-gather.16.cloned.1.call-start = ((), (), s32[]{:S(2)}) async-start(), calls=%async_computation.11 | async-start | bytes 1216512 | tf_op jit(solution)/shard_map/all_gather | solution.py:186
  9.4 216.8 %all-gather.20.cloned.1.call-start = ((), (), s32[]{:S(2)}) async-start(), calls=%async_computation.13 | async-start | bytes 3342336 | tf_op jit(solution)/shard_map/all_gather | solution.py:230
  54.2 127.0 %copy-start.75 = (f32[768]{0:T(1024)}, f32[768]{0:T(1024)S(1)}, u32[]{:S(2)}) copy-start(f32[768]{0:T(1024)S(1)} %convert_element_type.254) | copy-start | bytes 9220
  55.3 12.3 copy-start.94
  55.4 72.9 %copy-start.96 = (f32[128]{0:T(128)}, f32[128]{0:T(128)S(1)}, u32[]{:S(2)}) copy-start(f32[128]{0:T(128)S(1)} %get-tuple-element.1287) | copy-start | bytes 1540
  55.4 124.0 %copy-start.85 = (f32[128]{0:T(128)}, f32[128]{0:T(128)S(1)}, u32[]{:S(2)}) copy-start(f32[128]{0:T(128)S(1)} %fusion.120) | copy-start | bytes 1540
  67.7 58.4 %copy-start.33 = (bf16[768,768]{1,0:T(8,128)(2,1)S(1)}, bf16[768,768]{1,0:T(8,128)(2,1)}, u32[]{:S(2)}) copy-start(bf16[768,768]{1,0:T(8,128)(2,1)} %all-gather.18.cloned.1.call-done) | copy-start | bytes 3538948
  70.2 61.8 %copy-start.84 = (s32[4095]{0:T(1024)S(1)}, s32[4095]{0:T(1024)}, u32[]{:S(2)}) copy-start(s32[4095]{0:T(1024)} %param.32) | copy-start | bytes 49144
  70.2 202.8 %all-gather.30.cloned.1.call-start = ((), (), s32[]{:S(2)}) async-start(), calls=%async_computation.18 | async-start | bytes 3342336 | tf_op jit(solution)/shard_map/all_gather | solution.py:229
  70.3 110.9 %copy-start.87 = (f32[128]{0:T(128)}, f32[128]{0:T(128)S(1)}, u32[]{:S(2)}) copy-start(f32[128]{0:T(128)S(1)} %fusion.122) | copy-start | bytes 1540
  126.1 193.9 %all-gather.32.cloned.1.call-start = ((), (), s32[]{:S(2)}) async-start(), calls=%async_computation.19 | async-start | bytes 3342336 | tf_op jit(solution)/shard_map/all_gather | solution.py:230
  127.2 239.6 %all-gather.14.cloned.1.call-start = ((), (), s32[]{:S(2)}) async-start(), calls=%async_computation.10 | async-start | bytes 3342336 | tf_op jit(solution)/shard_map/all_gather | solution.py:229
  128.3 431.3 %all-gather.22.cloned.1.call-start = ((), (), s32[]{:S(2)}) async-start(), calls=%async_computation.14 | async-start | bytes 1216512 | tf_op jit(solution)/shard_map/all_gather | solution.py:189
  129.1 626.7 %all-gather.26.cloned.1.call-start = ((), (), s32[]{:S(2)}) async-start(), calls=%async_computation.16 | async-start | bytes 3244032 | tf_op jit(solution)/shard_map/all_gather | solution.py:191
  129.8 629.5 %all-gather.24.cloned.1.call-start = ((), (), s32[]{:S(2)}) async-start(), calls=%async_computation.15 | async-start | bytes 3244032 | tf_op jit(solution)/shard_map/all_gather | solution.py:190
  130.4 632.4 %all-gather.28.cloned.1.call-start = ((), (), s32[]{:S(2)}) async-start(), calls=%async_computation.17 | async-start | bytes 3244032 | tf_op jit(solution)/shard_map/all_gather | solution.py:192
  131.1 1466.2 %reduce-scatter.12.cloned.1.call-start = ((), (), s32[]{:S(2)}) async-start(), calls=%async_computation.21 | async-start | bytes 13369344 | tf_op jit(solution)/shard_map/reduce_scatter | solution.py:329
  371.5 7.0 copy-start.102
  418.2 7.0 copy-start.102
  465.0 7.0 copy-start.102
  511.8 7.0 copy-start.102
  562.9 7.0 copy-start.104
  609.8 7.0 copy-start.104
  656.5 7.0 copy-start.104
  703.1 7.0 copy-start.104
  781.0 8.2 copy-start.43
  983.5 6.1 copy-start
  1181.5 526.0 %reduce-scatter.10.cloned.1.call-start = ((), (), s32[]{:S(2)}) async-start(), calls=%async_computation.20 | async-start | bytes 13369344 | tf_op jit(solution)/shard_map/reduce_scatter | solution.py:329
  1184.9 7.5 copy-start.11
  1280.4 6.1 copy-start.1
  1470.1 6.1 copy-start.1
  1573.2 238.6 %reduce-scatter.20.cloned.1.call-start = ((), (), s32[]{:S(2)}) async-start(), calls=%async_computation.25 | async-start | bytes 2433024 | tf_op jit(solution)/shard_map/reduce_scatter | solution.py:363
  1576.6 339.8 %reduce-scatter.14.cloned.1.call-start = ((), (), s32[]{:S(2)}) async-start(), calls=%async_computation.22 | async-start | bytes 2433024 | tf_op jit(solution)/shard_map/reduce_scatter | solution.py:360
  1579.5 456.3 %reduce-scatter.24.cloned.1.call-start = ((), (), s32[]{:S(2)}) async-start(), calls=%async_computation.27 | async-start | bytes 6488064 | tf_op jit(solution)/shard_map/reduce_scatter | solution.py:365
  1584.8 571.5 %reduce-scatter.22.cloned.1.call-start = ((), (), s32[]{:S(2)}) async-start(), calls=%async_computation.26 | async-start | bytes 6488064 | tf_op jit(solution)/shard_map/reduce_scatter | solution.py:364
  1591.0 685.2 %reduce-scatter.26.cloned.1.call-start = ((), (), s32[]{:S(2)}) async-start(), calls=%async_computation.28 | async-start | bytes 6488064 | tf_op jit(solution)/shard_map/reduce_scatter | solution.py:366
  1597.3 783.9 %reduce-scatter.16.cloned.1.call-start = ((), (), s32[]{:S(2)}) async-start(), calls=%async_computation.23 | async-start | bytes 2433024 | tf_op jit(solution)/shard_map/reduce_scatter | solution.py:361
  1598.6 112.7 %copy-start.49 = (bf16[128,1536]{1,0:T(8,128)(2,1)}, bf16[128,1536]{1,0:T(8,128)(2,1)S(1)}, u32[]{:S(2)}) copy-start(bf16[128,1536]{1,0:T(8,128)(2,1)S(1)} %convert.11) | copy-start | bytes 1179652
  1711.3 773.7 %reduce-scatter.18.cloned.1.call-start = ((), (), s32[]{:S(2)}) async-start(), calls=%async_computation.24 | async-start | bytes 2433024 | tf_op jit(solution)/shard_map/reduce_scatter | solution.py:362
  1712.1 6.6 copy-start.89
  1712.1 7.9 copy-start.32
  1724.9 43.3 %copy-start.95 = (f32[128]{0:T(128)S(1)}, f32[128]{0:T(128)}, u32[]{:S(2)}) copy-start(f32[128]{0:T(128)} %copy-done.94) | copy-start | bytes 1540
  1724.9 43.3 %copy-start.97 = (f32[128]{0:T(128)S(1)}, f32[128]{0:T(128)}, u32[]{:S(2)}) copy-start(f32[128]{0:T(128)} %copy-done.96) | copy-start | bytes 1540
  1724.9 43.3 %copy-start.42 = (f32[128,768]{1,0:T(8,128)S(1)}, f32[128,768]{1,0:T(8,128)}, u32[]{:S(2)}) copy-start(f32[128,768]{1,0:T(8,128)} %get-tuple-element.1410) | copy-start | bytes 1179652
  1724.9 43.3 %copy-start.45 = (f32[128,768]{1,0:T(8,128)S(1)}, f32[128,768]{1,0:T(8,128)}, u32[]{:S(2)}) copy-start(f32[128,768]{1,0:T(8,128)} %copy-done.43) | copy-start | bytes 1179652
  (150 other events, 269.9 us)
Sparse Core Ops, SparseCore 0:
  10.9 56.7 all-gather.17
  70.6 52.9 all-gather.11
  126.4 52.9 all-gather.15
  182.1 44.1 all-gather.19
  228.9 43.9 all-gather.29
  275.7 44.2 all-gather.31
  322.8 43.9 all-gather.13
  369.7 52.8 all-gather.21
  425.5 57.9 all-gather.25
  486.2 57.8 all-gather.23
  547.0 57.7 all-gather.27
  1181.6 133.7 reduce-scatter.11
  1573.3 134.2 reduce-scatter.9
  1713.2 98.4 reduce-scatter.19
  1818.3 97.9 reduce-scatter.13
  1922.4 113.3 reduce-scatter.23
  2042.8 113.4 reduce-scatter.21
  2162.4 113.7 reduce-scatter.25
  2282.9 98.1 reduce-scatter.15
  2386.8 98.0 reduce-scatter.17
where the time goes:
time: 2520 us; the launch traced here: 2490 us
  waiting for transfers between devices  1110 us (44%)
  local copies, waits for them, and re-layouts  1060 us (42%)
  matrix products  130 us (5%)
  blocking collectives  81.8 us (3%)
  other arithmetic  70.2 us (3%)
  loops' own time  25.5 us (1%)
    rev x16, local copies, waits for them, and re-layouts, spread_bias(): return skewed[:, ::-1, :]  358 us
    rev x8, local copies, waits for them, and re-layouts, add_diagonals(): flipped = score_grad.astype(jnp.float32)[:, ::-1, :]  137 us
    while x256, local copies, waits for them, and re-layouts  123 us
    reduce_scatter x1, waiting for transfers between devices, body(): lax.psum_scatter(grad_sums[4], ('dp', 'ctx'), scatter_dimension=0, tiled=...  121 us
    reduce_scatter x1, waiting for transfers between devices, body(): lax.psum_scatter(grad_sums[6], ('dp', 'ctx'), scatter_dimension=0, tiled=...  120 us
    reduce_scatter x1, waiting for transfers between devices, body(): lax.psum_scatter(grad_sums[5], ('dp', 'ctx'), scatter_dimension=0, tiled=...  119 us
    reduce_scatter x2, waiting for transfers between devices, body(): lax.psum_scatter(key_terms.reshape(seq_length, 2 * model_width), 'ctx', s...  109 us
    reduce_scatter x1, waiting for transfers between devices, body(): lax.psum_scatter(grad_sums[1], ('dp', 'ctx'), scatter_dimension=0, tiled=...  105 us
  transfers between devices with their start and end apart: 20, of which 15 were waited for; matrix products, arithmetic and copies ran while one was open for 33% of the time, Pallas kernels for 0%

commit v1 on v0

v1 whole, which is shorter than its diff:
```python
import functools

import jax
import jax.numpy as jnp
from jax import lax
from jax.experimental import pallas as pl
from jax.experimental.pallas import tpu as pltpu
from jax.sharding import Mesh
from jax.sharding import PartitionSpec as P

H = 12
BUCKETS = 32
GROUPS = 4
CORES = 2
BLOCK = 128

epsilon = 1e-06
exactly = lax.Precision.HIGHEST
bf16 = jnp.bfloat16
f32 = jnp.float32
everyone = ("dp", "a", "z", "x", "c")


def rms_scale(values, gain_vec):
    return (
        values * lax.rsqrt(jnp.mean(values * values, axis=-1, keepdims=True) + epsilon) * gain_vec
    )


def gelu_product(gate_in, up_in):
    return jax.nn.gelu(gate_in, approximate=True) * up_in


def inner_rows(first_op, second_op):
    return lax.dot_general(
        first_op, second_op, (((0,), (0,)), ((), ())), preferred_element_type=f32
    )


def outer_rows(first_op, second_op):
    return lax.dot_general(
        first_op, second_op, (((1,), (1,)), ((), ())), preferred_element_type=f32
    )


def vmem_limit(mib):
    return pltpu.CompilerParams(vmem_limit_bytes=mib * 1024 * 1024)


def project_kernel(heads, token_ref, gain_ref, weight_ref, normed_ref, query_ref, pair_ref):
    rows = token_ref[...].astype(f32)
    scale = lax.rsqrt(jnp.mean(rows * rows, axis=-1, keepdims=True) + epsilon)
    normed = (rows * scale * gain_ref[...]).astype(bf16)
    normed_ref[...] = normed
    width = query_ref.shape[2]
    mixed = jnp.dot(
        normed, weight_ref[:, : 3 * heads * width], preferred_element_type=f32
    ).astype(bf16)
    for k in range(heads):
        query_ref[k] = mixed[:, k * width : (k + 1) * width]
    for k in range(2 * heads):
        pair_ref[k] = mixed[:, (heads + k) * width : (heads + k + 1) * width]


def project(tokens, gain_row, weight, heads, width):
    rows, model = tokens.shape
    tile = 256
    return pl.pallas_call(
        functools.partial(project_kernel, heads),
        grid=(rows // tile,),
        in_specs=[
            pl.BlockSpec((tile, model), lambda i: (i, 0)),
            pl.BlockSpec((1, model), lambda i: (0, 0)),
            pl.BlockSpec(weight.shape, lambda i: (0, 0)),
        ],
        out_specs=[
            pl.BlockSpec((tile, model), lambda i: (i, 0)),
            pl.BlockSpec((heads, tile, width), lambda i: (0, i, 0)),
            pl.BlockSpec((2 * heads, tile, width), lambda i: (0, i, 0)),
        ],
        out_shape=[
            jax.ShapeDtypeStruct((rows, model), bf16),
            jax.ShapeDtypeStruct((heads, rows, width), bf16),
            jax.ShapeDtypeStruct((2 * heads, rows, width), bf16),
        ],
        compiler_params=vmem_limit(40),
        cost_estimate=pl.CostEstimate(
            flops=2 * rows * model * 3 * heads * width,
            bytes_accessed=8 * rows * model,
            transcendentals=0,
        ),
        name="project",
    )(tokens, gain_row, weight)


def skew_rows(vector_ref, table_ref, row_scratch):
    span = vector_ref.shape[-1]
    for r in range(8):
        row_scratch[r : r + 1, :] = pltpu.roll(vector_ref[0], r, 1) if r else vector_ref[0]
    eight = row_scratch[...]
    for group in range(BLOCK // 8):
        turned = pltpu.roll(eight, 8 * group, 1) if group else eight
        table_ref[8 * group : 8 * group + 8, :] = turned[:, BLOCK:span]


def interleave(scratch, own_ref, other_ref, parity):
    for k in range(own_ref.shape[1] // BLOCK):
        rows = slice(k * BLOCK, (k + 1) * BLOCK)
        first = pl.multiple_of((2 * k + parity) * BLOCK, BLOCK)
        second = pl.multiple_of((2 * k + 1 - parity) * BLOCK, BLOCK)
        scratch[pl.ds(first, BLOCK), :] = own_ref[0, rows, :]
        scratch[pl.ds(second, BLOCK), :] = other_ref[0, rows, :]


def attend_kernel(
    tile,
    chunk,
    place_ref,
    query_ref,
    key_own,
    key_other,
    value_own,
    value_other,
    vector_ref,
    context_ref,
    probs_ref,
    kept_ref,
    keys,
    values,
    table,
    scores,
    row_scratch,
):
    head, step = pl.program_id(0), pl.program_id(1)
    first_block, parity = place_ref[0], place_ref[1]
    key_count, width = keys.shape
    blocks = key_count // BLOCK

    @pl.when(step == 0)
    def prepare():
        skew_rows(vector_ref, table, row_scratch)
        interleave(keys, key_own, key_other, parity)
        interleave(values, value_own, value_other, parity)

    query = query_ref[0]
    starts = []
    for sub in range(tile // BLOCK):
        block = 2 * (first_block + step * (tile // BLOCK) + sub) + parity
        starts.append((blocks - 1 - block) * BLOCK)
    lane_max = None
    for part in range(key_count // chunk):
        product = lax.dot_general(
            query,
            keys[part * chunk : (part + 1) * chunk, :],
            (((1,), (1,)), ((), ())),
            preferred_element_type=f32,
        )
        for sub in range(tile // BLOCK):
            rows = slice(sub * BLOCK, (sub + 1) * BLOCK)
            offset = pl.multiple_of(starts[sub] + part * chunk, BLOCK)
            scores[rows, part * chunk : (part + 1) * chunk] = (
                product[rows] + table[:, pl.ds(offset, chunk)]
            )
        piece = scores[:, part * chunk : (part + 1) * chunk]
        for k in range(chunk // BLOCK):
            lanes = piece[:, k * BLOCK : (k + 1) * BLOCK]
            lane_max = lanes if lane_max is None else jnp.maximum(lane_max, lanes)
    row_max = jnp.max(lane_max, axis=-1, keepdims=True)
    lane_sum = jnp.zeros((tile, BLOCK), f32)
    mixed = jnp.zeros((tile, width), f32)
    for part in range(key_count // chunk):
        cols = slice(part * chunk, (part + 1) * chunk)
        weights = jnp.exp(scores[:, cols] - row_max)
        for k in range(chunk // BLOCK):
            lane_sum = lane_sum + weights[:, k * BLOCK : (k + 1) * BLOCK]
        low = weights.astype(bf16)
        probs_ref[0, :, cols] = low
        mixed = mixed + jnp.dot(low, values[cols, :], preferred_element_type=f32)
    inverse = 1.0 / jnp.sum(lane_sum, axis=-1, keepdims=True)
    mixed = mixed * inverse
    kept_ref[0, :, :width] = mixed
    kept_ref[0, :, width:] = jnp.broadcast_to(inverse, (tile, width))
    low = mixed.astype(bf16)
    rows = pl.ds(pl.multiple_of(step * tile, tile), tile)
    for k in range(context_ref.shape[1] // width):

        @pl.when(head == k)
        def store():
            context_ref[rows, k * width : (k + 1) * width] = low


def attend(place, query, own, other, vectors):
    heads, rows, width = query.shape
    own_rows = own.shape[1]
    key_count = 2 * own_rows
    span = vectors.shape[-1]
    tile, chunk = 256, 512
    half = lambda shift: pl.BlockSpec((1, own_rows, width), lambda h, i, s: (h + shift, 0, 0))
    return pl.pallas_call(
        functools.partial(attend_kernel, tile, chunk),
        grid_spec=pltpu.PrefetchScalarGridSpec(
            num_scalar_prefetch=1,
            grid=(heads, rows // tile),
            in_specs=[
                pl.BlockSpec((1, tile, width), lambda h, i, s: (h, i, 0)),
                half(0),
                half(0),
                half(heads),
                half(heads),
                pl.BlockSpec((1, 1, span), lambda h, i, s: (h, 0, 0)),
            ],
            out_specs=[
                pl.BlockSpec((rows, heads * width), lambda h, i, s: (0, 0)),
                pl.BlockSpec((1, tile, key_count), lambda h, i, s: (h, i, 0)),
                pl.BlockSpec((1, tile, 2 * width), lambda h, i, s: (h, i, 0)),
            ],
            scratch_shapes=[
                pltpu.VMEM((key_count, width), bf16),
                pltpu.VMEM((key_count, width), bf16),
                pltpu.VMEM((BLOCK, span - BLOCK), f32),
                pltpu.VMEM((tile, key_count), f32),
                pltpu.VMEM((8, span), f32),
            ],
        ),
        out_shape=[
            jax.ShapeDtypeStruct((rows, heads * width), bf16),
            jax.ShapeDtypeStruct((heads, rows, key_count), bf16),
            jax.ShapeDtypeStruct((heads, rows, 2 * width), f32),
        ],
        compiler_params=vmem_limit(60),
        cost_estimate=pl.CostEstimate(
            flops=16 * heads * rows * key_count * width,
            bytes_accessed=2 * heads * rows * key_count,
            transcendentals=heads * rows * key_count,
        ),
        name="attend",
    )(place, query, own, other, own, other, vectors)


def attend_back_kernel(
    tile,
    chunk,
    place_ref,
    grad_ref,
    kept_ref,
    probs_ref,
    query_ref,
    key_own,
    key_other,
    value_own,
    value_other,
    query_grad_ref,
    own_grad_ref,
    other_grad_ref,
    offset_ref,
    keys,
    values,
    diagonals,
    key_sums,
    value_sums,
    head_grad,
):
    head, step = pl.program_id(0), pl.program_id(1)
    first_block, parity = place_ref[0], place_ref[1]
    key_count, width = keys.shape
    heads = grad_ref.shape[1] // width
    blocks = key_count // BLOCK

    @pl.when(step == 0)
    def prepare():
        interleave(keys, key_own, key_other, parity)
        interleave(values, value_own, value_other, parity)
        diagonals[...] = jnp.zeros_like(diagonals)
        key_sums[...] = jnp.zeros_like(key_sums)
        value_sums[...] = jnp.zeros_like(value_sums)

    for k in range(heads):

        @pl.when(head == k)
        def load():
            head_grad[...] = grad_ref[:, k * width : (k + 1) * width]

    scaled = (head_grad[...].astype(f32) * kept_ref[0, :, width:]).astype(bf16)
    delta = jnp.sum(scaled.astype(f32) * kept_ref[0, :, :width], axis=-1, keepdims=True)
    query_turned = query_ref[0].astype(f32).T.astype(bf16)
    grad_turned = scaled.astype(f32).T.astype(bf16)
    starts = []
    for sub in range(tile // BLOCK):
        block = 2 * (first_block + step * (tile // BLOCK) + sub) + parity
        starts.append((blocks - 1 - block) * BLOCK)
    query_grad = jnp.zeros((tile, width), f32)
    for part in range(key_count // chunk):
        cols = slice(part * chunk, (part + 1) * chunk)
        prob_grad = lax.dot_general(
            scaled, values[cols, :], (((1,), (1,)), ((), ())), preferred_element_type=f32
        )
        low = probs_ref[0, :, cols]
        score_grad = low.astype(f32) * (prob_grad - delta)
        for sub in range(tile // BLOCK):
            rows = slice(sub * BLOCK, (sub + 1) * BLOCK)
            offset = pl.multiple_of(starts[sub] + part * chunk, BLOCK)
            diagonals[:, pl.ds(offset, chunk)] += score_grad[rows]
        score_low = score_grad.astype(bf16)
        query_grad = query_grad + jnp.dot(score_low, keys[cols, :], preferred_element_type=f32)
        key_sums[:, cols] += jnp.dot(query_turned, score_low, preferred_element_type=f32)
        value_sums[:, cols] += jnp.dot(grad_turned, low, preferred_element_type=f32)
    rows = pl.ds(pl.multiple_of(step * tile, tile), tile)
    for k in range(heads):

        @pl.when(head == k)
        def store():
            query_grad_ref[rows, k * width : (k + 1) * width] = query_grad.astype(bf16)

    @pl.when(step == pl.num_programs(1) - 1)
    def finish():
        span = diagonals.shape[1]
        eight = diagonals[0:8, :]
        for group in range(1, BLOCK // 8):
            eight = eight + pltpu.roll(
                diagonals[8 * group : 8 * group + 8, :], span - 8 * group, 1
            )
        total = eight[0:1, :]
        for r in range(1, 8):
            total = total + pltpu.roll(eight[r : r + 1, :], span - r, 1)
        offset_ref[0] = pltpu.roll(total, BLOCK - 1, 1)
        for k in range(heads):

            @pl.when(head == k)
            def store_pairs():
                for sums, shift in ((key_sums, 0), (value_sums, heads)):
                    lanes = slice((shift + k) * width, (shift + k + 1) * width)
                    for b in range(blocks // 2):
                        near = pl.multiple_of((2 * b + parity) * BLOCK, BLOCK)
                        far = pl.multiple_of((2 * b + 1 - parity) * BLOCK, BLOCK)
                        out = slice(b * BLOCK, (b + 1) * BLOCK)
                        own_grad_ref[out, lanes] = sums[:, pl.ds(near, BLOCK)].T
                        other_grad_ref[out, lanes] = sums[:, pl.ds(far, BLOCK)].T.astype(bf16)


def attend_back(place, grad, kept, probs, query, own, other):
    heads, rows, width = query.shape
    own_rows = own.shape[1]
    key_count = 2 * own_rows
    span = key_count * 2
    tile, chunk = 256, 512
    half = lambda shift: pl.BlockSpec((1, own_rows, width), lambda h, i, s: (h + shift, 0, 0))
    return pl.pallas_call(
        functools.partial(attend_back_kernel, tile, chunk),
        grid_spec=pltpu.PrefetchScalarGridSpec(
            num_scalar_prefetch=1,
            grid=(heads, rows // tile),
            in_specs=[
                pl.BlockSpec((tile, heads * width), lambda h, i, s: (i, 0)),
                pl.BlockSpec((1, tile, 2 * width), lambda h, i, s: (h, i, 0)),
                pl.BlockSpec((1, tile, key_count), lambda h, i, s: (h, i, 0)),
                pl.BlockSpec((1, tile, width), lambda h, i, s: (h, i, 0)),
                half(0),
                half(0),
                half(heads),
                half(heads),
            ],
            out_specs=[
                pl.BlockSpec((rows, heads * width), lambda h, i, s: (0, 0)),
                pl.BlockSpec((own_rows, 2 * heads * width), lambda h, i, s: (0, 0)),
                pl.BlockSpec((own_rows, 2 * heads * width), lambda h, i, s: (0, 0)),
                pl.BlockSpec((1, 1, span), lambda h, i, s: (h, 0, 0)),
            ],
            scratch_shapes=[
                pltpu.VMEM((key_count, width), bf16),
                pltpu.VMEM((key_count, width), bf16),
                pltpu.VMEM((BLOCK, span), f32),
                pltpu.VMEM((width, key_count), f32),
                pltpu.VMEM((width, key_count), f32),
                pltpu.VMEM((tile, width), bf16),
            ],
        ),
        out_shape=[
            jax.ShapeDtypeStruct((rows, heads * width), bf16),
            jax.ShapeDtypeStruct((own_rows, 2 * heads * width), f32),
            jax.ShapeDtypeStruct((own_rows, 2 * heads * width), bf16),
            jax.ShapeDtypeStruct((heads, 1, span), f32),
        ],
        compiler_params=vmem_limit(60),
        cost_estimate=pl.CostEstimate(
            flops=32 * heads * rows * key_count * width,
            bytes_accessed=2 * heads * rows * key_count,
            transcendentals=0,
        ),
        name="attend_back",
    )(place, grad, kept, probs, query, own, other, own, other)


def project_back_kernel(
    query_grad_ref,
    own_ref,
    received_ref,
    normed_ref,
    token_ref,
    weight_ref,
    rows_ref,
    weight_grad_ref,
    gain_ref,
    mixed,
):
    step = pl.program_id(0)
    part = query_grad_ref.shape[1]
    mixed[:, :part] = query_grad_ref[...]
    mixed[:, part:] = (own_ref[...] + received_ref[...].astype(f32)).astype(bf16)
    grads = mixed[...]
    normed_grad = lax.dot_general(
        grads,
        weight_ref[:, : 3 * part],
        (((1,), (1,)), ((), ())),
        preferred_element_type=f32,
    )
    rows_ref[...] = normed_grad.astype(bf16)
    tokens = token_ref[...].astype(f32)
    scale = lax.rsqrt(jnp.mean(tokens * tokens, axis=-1, keepdims=True) + epsilon)
    gain = jnp.sum(normed_grad * (tokens * scale), axis=0, keepdims=True)
    update = lax.dot_general(
        normed_ref[...], grads, (((0,), (0,)), ((), ())), preferred_element_type=f32
    )

    @pl.when(step == 0)
    def start():
        weight_grad_ref[...] = update
        gain_ref[...] = gain

    @pl.when(step != 0)
    def more():
        weight_grad_ref[...] += update
        gain_ref[...] += gain


def project_back(query_grad, own, received, normed, tokens, weight):
    rows, model = tokens.shape
    part = query_grad.shape[1]
    tile = 256
    by_rows = lambda size: pl.BlockSpec((tile, size), lambda i: (i, 0))
    whole = lambda shape: pl.BlockSpec(shape, lambda i: (0, 0))
    return pl.pallas_call(
        project_back_kernel,
        grid=(rows // tile,),
        in_specs=[
            by_rows(part),
            by_rows(2 * part),
            by_rows(2 * part),
            by_rows(model),
            by_rows(model),
            whole(weight.shape),
        ],
        out_specs=[by_rows(model), whole((model, 3 * part)), whole((1, model))],
        out_shape=[
            jax.ShapeDtypeStruct((rows, model), bf16),
            jax.ShapeDtypeStruct((model, 3 * part), f32),
            jax.ShapeDtypeStruct((1, model), f32),
        ],
        scratch_shapes=[pltpu.VMEM((tile, 3 * part), bf16)],
        compiler_params=vmem_limit(40),
        cost_estimate=pl.CostEstimate(
            flops=12 * rows * model * part, bytes_accessed=12 * rows * model, transcendentals=0
        ),
        name="project_back",
    )(query_grad, own, received, normed, tokens, weight)


def swap(value, axis):
    return lax.ppermute(value, axis, [(0, 1), (1, 0)])


def pick(pair, index, axis):
    return lax.dynamic_index_in_dim(pair, index, axis, keepdims=False)


def in_order(mine, theirs, index, axis):
    return jnp.where(
        index == 0, jnp.stack([mine, theirs], axis), jnp.stack([theirs, mine], axis)
    )


def halve(value, index, name, axis):
    sent = swap(pick(value, 1 - index, axis), name)
    return (pick(value, index, axis).astype(f32) + sent.astype(f32)).astype(bf16)


def body(
    inputs,
    w_query,
    w_key,
    w_value,
    w_output,
    w_gate,
    w_upper,
    w_down,
    gain_one,
    gain_two,
    bias_table,
    buckets,
    cotangent,
    sizes,
):
    along_dp, along_a = sizes
    z, x, c = lax.axis_index("z"), lax.axis_index("x"), lax.axis_index("c")
    a = lax.axis_index("a")
    seqs, local_rows, model = inputs.shape
    length = buckets.shape[0] // 2 + 1
    width = model // H
    heads = H // GROUPS
    part = heads * width
    weight_rows = w_query.shape[0]
    hidden_units = w_gate.shape[1]

    packed = jnp.concatenate(
        [w_output, w_gate, w_upper, w_down.reshape(weight_rows, hidden_units)], axis=1
    )
    everything = lax.all_gather(packed, everyone, axis=0, tiled=True)

    mine, theirs = pick(inputs, x, 0), swap(pick(inputs, 1 - x, 0), "x")
    near = in_order(mine, theirs, x, 0)
    gathered = jnp.zeros((GROUPS, *near.shape), bf16)
    gathered = lax.dynamic_update_index_in_dim(gathered, near, z, 0)
    for shift in range(1, GROUPS):
        came = lax.ppermute(near, "z", [(i, (i + shift) % GROUPS) for i in range(GROUPS)])
        gathered = lax.dynamic_update_index_in_dim(gathered, came, (z - shift) % GROUPS, 0)
    own_count = GROUPS * 2 * local_rows
    tokens_own = gathered.reshape(own_count, model)

    blocks = [
        jnp.transpose(w.reshape(weight_rows, GROUPS, part), (1, 0, 2))
        for w in (w_query, w_key, w_value)
    ]
    table_column = jnp.pad(bias_table, (0, weight_rows - bias_table.shape[0]))
    extra = jnp.stack([gain_one, gain_two, table_column], axis=1)
    extra = jnp.pad(extra, ((0, 0), (0, BLOCK - extra.shape[1])))
    extra = jnp.broadcast_to(extra[None], (GROUPS, weight_rows, BLOCK))
    columns = lax.all_to_all(jnp.concatenate([*blocks, extra], axis=2), "z", 0, 0, tiled=True)
    columns = in_order(columns, swap(columns, "x"), x, 1)
    if along_a > 1:
        columns = lax.all_gather(columns, "a", axis=0)
    else:
        columns = columns[None]
    dp = lax.axis_index("dp")
    columns = in_order(columns, swap(columns, "dp"), dp, 0)
    columns = in_order(columns, swap(columns, "c"), c, 4)
    columns = columns.reshape(model, 3 * part + BLOCK)
    gain_a = columns[:, 3 * part].astype(f32)
    gain_b = columns[:, 3 * part + 1].astype(f32)
    table = columns[:, 3 * part + 2].reshape(model // weight_rows, weight_rows)
    table = table[:, : bias_table.shape[0]].reshape(BUCKETS, H)
    one_hot = (buckets[:, None] == jnp.arange(BUCKETS, dtype=jnp.int32)[None, :]).astype(bf16)
    own_table = lax.dynamic_slice_in_dim(table, z * heads, heads, 1)
    offset_bias = lax.dot_general(
        own_table, one_hot, (((0,), (1,)), ((), ())), preferred_element_type=f32
    )
    vectors = jnp.pad(offset_bias, ((0, 0), (1, 0))).reshape(heads, 1, 2 * length)

    if along_a > 1:
        tokens_all = lax.all_gather(tokens_own, "a", axis=0, tiled=True)
    else:
        tokens_all = tokens_own
    normed, query, own = project(tokens_all, gain_a.reshape(1, model), columns, heads, width)
    if along_a > 1:
        query = lax.dynamic_slice_in_dim(query, a * own_count, own_count, 1)
        normed = lax.dynamic_slice_in_dim(normed, a * own_count, own_count, 0)
    other = swap(own, "c")
    place = jnp.stack([a * (own_count // BLOCK), c]).astype(jnp.int32)
    context_own, probs, kept = attend(place, query, own, other, vectors)
    context = lax.all_to_all(
        context_own.reshape(GROUPS * 2, local_rows, part), ("z", "x"), 0, 0, tiled=True
    )
    context = jnp.transpose(
        context.reshape(GROUPS, 2, local_rows, part), (1, 2, 0, 3)
    ).reshape(2 * local_rows, model)

    output_w = everything[:, :model]
    gate_w = everything[:, model : model + hidden_units]
    upper_w = everything[:, model + hidden_units : model + 2 * hidden_units]
    down_w = everything[:, model + 2 * hidden_units :].reshape(hidden_units, model)

    token_rows = inputs.reshape(seqs * local_rows, model).astype(f32)
    residual = token_rows + jnp.dot(context, output_w, preferred_element_type=f32)
    second_low = rms_scale(residual, gain_b).astype(bf16)
    gate_pre = jnp.dot(second_low, gate_w, preferred_element_type=f32)
    up_pre = jnp.dot(second_low, upper_w, preferred_element_type=f32)
    hidden = gelu_product(gate_pre, up_pre).astype(bf16)
    outputs = (residual + jnp.dot(hidden, down_w, preferred_element_type=f32)).astype(bf16)

    down_grad = cotangent.reshape(seqs * local_rows, model)
    hidden_grad = outer_rows(down_grad, down_w)
    unused, gelu_pull = jax.vjp(gelu_product, gate_pre, up_pre)
    gate_grad, up_grad = gelu_pull(hidden_grad)
    gate_low = gate_grad.astype(bf16)
    up_low = up_grad.astype(bf16)
    norm_grad = outer_rows(gate_low, gate_w) + outer_rows(up_low, upper_w)
    unused, norm_pull = jax.vjp(rms_scale, residual, gain_b)
    residual_part, gain_b_grad = norm_pull(norm_grad)
    residual_grad = down_grad.astype(f32) + residual_part
    attn_low = residual_grad.astype(bf16)
    context_low = outer_rows(attn_low, output_w).astype(bf16)
    sent = jnp.transpose(
        context_low.reshape(2, local_rows, GROUPS, part), (2, 0, 1, 3)
    ).reshape(GROUPS * 2, local_rows, part)
    context_grad = lax.all_to_all(sent, ("z", "x"), 0, 0, tiled=True).reshape(own_count, part)

    big_grads = jnp.concatenate(
        [
            inner_rows(context, attn_low).astype(bf16),
            inner_rows(second_low, gate_low).astype(bf16),
            inner_rows(second_low, up_low).astype(bf16),
            inner_rows(hidden, down_grad).astype(bf16).reshape(model, hidden_units),
        ],
        axis=1,
    )
    big_owned = lax.psum_scatter(big_grads, everyone, scatter_dimension=0, tiled=True)
    big_owned = big_owned.astype(f32)

    query_grad, own_grad, other_grad, offset_grad = attend_back(
        place, context_grad, kept, probs, query, own, other
    )
    if along_a > 1:
        own_grad = lax.psum_scatter(own_grad, "a", scatter_dimension=0, tiled=True)
        other_grad = lax.psum_scatter(other_grad, "a", scatter_dimension=0, tiled=True)
    received = swap(other_grad, "c")
    rows_grad, weight_grad, gain_a_grad = project_back(
        query_grad, own_grad, received, normed, tokens_own, columns
    )

    rows_grad = rows_grad.reshape(GROUPS, 2, local_rows, model)
    total = pick(rows_grad, z, 0).astype(f32)
    for shift in range(1, GROUPS):
        sent = pick(rows_grad, (z + shift) % GROUPS, 0)
        came = lax.ppermute(sent, "z", [(i, (i + shift) % GROUPS) for i in range(GROUPS)])
        total = total + came.astype(f32)
    from_pair = swap(pick(total, 1 - x, 0).astype(bf16), "x").astype(f32)
    normed_grad = in_order(pick(total, x, 0), from_pair, x, 0).reshape(seqs * local_rows, model)
    scale = lax.rsqrt(jnp.mean(token_rows * token_rows, axis=-1, keepdims=True) + epsilon)
    weighted = normed_grad * gain_a
    inner = jnp.mean(weighted * token_rows, axis=-1, keepdims=True)
    input_grad = residual_grad + scale * weighted - token_rows * (scale * scale * scale * inner)

    table_part = lax.dot_general(
        offset_grad.reshape(heads, 2 * length)[:, : 2 * length - 1],
        one_hot.astype(f32),
        (((1,), (0,)), ((), ())),
        precision=exactly,
    )
    table_grad = lax.dynamic_update_slice_in_dim(
        jnp.zeros((BUCKETS, H), f32), jnp.transpose(table_part), z * heads, 1
    )
    per_owner = bias_table.shape[0]
    table_grad = jnp.pad(
        table_grad.reshape(BUCKETS * H // per_owner, per_owner),
        ((0, 0), (0, weight_rows - per_owner)),
    )
    extra_grad = jnp.stack(
        [gain_a_grad.reshape(model), gain_b_grad, table_grad.reshape(model)], axis=1
    )
    extra_grad = jnp.pad(extra_grad.astype(bf16), ((0, 0), (0, BLOCK - extra_grad.shape[1])))
    terms = jnp.concatenate([weight_grad.astype(bf16), extra_grad], axis=1)
    terms = terms.reshape(along_dp, along_a, GROUPS, 2, CORES, weight_rows, 3 * part + BLOCK)
    terms = halve(terms, c, "c", 4)
    terms = halve(terms, x, "x", 3)
    terms = halve(terms, dp, "dp", 0)
    if along_a > 1:
        terms = lax.psum_scatter(terms, "a", scatter_dimension=0, tiled=True)
    terms = lax.all_to_all(terms[0], "z", 0, 0, tiled=True).astype(f32)
    owned = [
        jnp.transpose(terms[:, :, k * part : (k + 1) * part], (1, 0, 2)).reshape(
            weight_rows, model
        )
        for k in range(3)
    ]
    extras = jnp.sum(terms[:, :, 3 * part : 3 * part + 3], axis=0)
    return (
        outputs.reshape(seqs, local_rows, model),
        input_grad.reshape(seqs, local_rows, model),
        owned[0],
        owned[1],
        owned[2],
        big_owned[:, :model],
        big_owned[:, model : model + hidden_units],
        big_owned[:, model + hidden_units : model + 2 * hidden_units],
        big_owned[:, model + 2 * hidden_units :].reshape(w_down.shape),
        extras[:, 0],
        extras[:, 1],
        extras[:per_owner, 2],
    )


def solution(mesh):
    along_dp, along_ctx = mesh.shape["dp"], mesh.shape["ctx"]
    along_a = along_ctx // (GROUPS * 2 * CORES)
    fine = Mesh(mesh.devices.reshape(along_dp, along_a, GROUPS, 2, CORES), everyone)
    rows = P("dp", ("a", "z", "x", "c"), None)
    owned = P(everyone, None)
    vector = P(everyone)
    in_specs = (rows, *[owned] * 7, *[vector] * 3, P(), rows)
    out_specs = (rows, rows, *[owned] * 7, *[vector] * 3)
    return jax.shard_map(
        functools.partial(body, sizes=(along_dp, along_a)),
        mesh=fine,
        in_specs=in_specs,
        out_specs=out_specs,
        check_vma=False,
    )
```

time: 2520 us -> 372 us (0.15); the launches traced: 2490 us -> 370 us
  local copies, waits for them, and re-layouts: 1060 us -> 59.5 us
  waiting for transfers between devices: 1110 us -> 111 us
  matrix products: 130 us -> 28.6 us
  Pallas kernels: 0 us -> 60.4 us
  other arithmetic: 70.2 us -> 19.8 us
  blocking collectives: 81.8 us -> 49.9 us
  loops' own time: 25.5 us -> 0 us
  starting transfers between devices: 1.02 us -> 26.3 us
    reduce_scatter x9 -> x1, waiting for transfers between devices: 825 us -> 10.7 us  [body(): lax.psum_scatter(big_grads, everyone, scatter_dimension=0, tiled=True)]
    rev x24 -> x0, local copies, waits for them, and re-layouts: 494 us -> none  [the longest x16 358 us: spread_bias(): return skewed[:, ::-1, :]]
    all_gather x11 -> x1, waiting for transfers between devices: 282 us -> 0.01 us  [body(): everything = lax.all_gather(packed, everyone, axis=0, tiled=True)]
    reshape x26 -> x14, local copies, waits for them, and re-layouts: 154 us -> 21.9 us  [the longest x1 6.65 us: body(): everything[:, model + 2 * hidden_units:].reshape(hidden_units, model)]
    while x256 -> x0, local copies, waits for them, and re-layouts: 123 us -> none
    ppermute x0 -> x16, waiting for transfers between devices: none -> 87.7 us  [the longest x3 41.7 us: body(): lax.ppermute(sent, 'z', [(i, (i + shift) % GROUPS) for i in range(GROUPS)])]
    unnamed x2 -> x0, blocking collectives: 81.8 us -> none
    dot_general x72 -> x6, matrix products: 86.5 us -> 11.9 us  [the longest x1 3.39 us: body(): up_pre = jnp.dot(second_low, upper_w, preferred_element_type=f32)]
  transfers between devices with their start and end apart: 20 -> 20, of which waited for: 15 -> 11; matrix products, arithmetic and copies ran while one was open for 33% -> 10% of each run, Pallas kernels for 0% -> 16%
where the time goes in v1:
time: 372 us; the launch traced here: 370 us
  waiting for transfers between devices  111 us (30%)
  Pallas kernels  60.4 us (16%)
  local copies, waits for them, and re-layouts  59.5 us (16%)
  blocking collectives  49.9 us (13%)
  matrix products  28.6 us (8%)
  starting transfers between devices  26.3 us (7%)
  other arithmetic  19.8 us (5%)
  between operations  14.8 us (4%)
    ppermute x3, waiting for transfers between devices, body(): lax.ppermute(sent, 'z', [(i, (i + shift) % GROUPS) for i in range(GROUPS)])  41.7 us
    all_to_all x1, blocking collectives, body(): lax.all_to_all(context_own.reshape(GROUPS * 2, local_rows, part), ('z', '...  34.9 us
    pallas_call x1, Pallas kernels, attend_back(): pl.pallas_call(functools.partial(attend_back_kernel, tile, chunk), grid_s...  30.9 us
    ppermute x3, waiting for transfers between devices, body(): lax.ppermute(near, 'z', [(i, (i + shift) % GROUPS) for i in range(GROUPS)])  26.5 us
    pallas_call x1, Pallas kernels, attend(): pl.pallas_call(functools.partial(attend_kernel, tile, chunk), grid_spec=p...  22.7 us
    ppermute x10, waiting for transfers between devices, swap(): return lax.ppermute(value, axis, [(0, 1), (1, 0)])  19.5 us
    all_to_all x1, blocking collectives, body(): lax.all_to_all(sent, ('z', 'x'), 0, 0, tiled=True).reshape(own_count, part)  15 us
    unnamed x50, local copies, waits for them, and re-layouts  13.3 us
  transfers between devices with their start and end apart: 20, of which 11 were waited for; matrix products, arithmetic and copies ran while one was open for 10% of the time, Pallas kernels for 16%

profile of v1, /device:TPU:0, one launch (start us, length us, event | category | flops | bytes accessed | tf_op | source)
XLA Modules:
  0.0 370.1 jit_solution(4151706075550256012)
XLA Ops:
  8.3 1.7 pad_maximum_fusion.1
  14.9 6.3 %all-to-all-start = ((bf16[4,24,704]{2,1,0:T(8,128)(2,1)}), bf16[4,24,704]{2,1,0:T(8,128)(2,1)S(1)}, u32[]{:S(2)}, u32[]{:S(2)}) async-start(bf16[4,24,704]{2,1,0:T(8,128)(2,1)} %pad_maximum_fusion.2), calls=%async_computation | async-start | bytes 294912 | tf_op jit(solution)/shard_map/all_to_all | solution.py:536
  21.3 1.6 collective-permute-start
  22.8 7.5 %all-to-all-done = bf16[4,24,704]{2,1,0:T(8,128)(2,1)S(1)} async-done(((bf16[4,24,704]{2,1,0:T(8,128)(2,1)}), bf16[4,24,704]{2,1,0:T(8,128)(2,1)S(1)}, u32[]{:S(2)}, u32[]{:S(2)}) %all-to-all-start) | async-done | bytes 135200 | tf_op jit(solution)/shard_map/all_to_all | solution.py:536
  30.3 1.5 collective-permute-start.4
  33.1 1.7 collective-permute-start.2
  34.8 2.1 collective-permute-start.3
  37.2 1.5 collective-permute-start.5
  38.8 7.7 %collective-permute-done.1 = bf16[2,128,768]{2,1,0:T(8,128)(2,1)S(1)} collective-permute-done((bf16[2,128,768]{2,1,0:T(8,128)(2,1)S(1)}, bf16[2,128,768]{2,1,0:T(8,128)(2,1)S(1)}, u32[]{:S(2)}, u32[]{:S(2)}) %collective-permute-start.1) | collective-permute-done | bytes 393248 | tf_op jit(solution)/shard_map/ppermute | solution.py:523
  46.8 18.8 %collective-permute-done.2 = bf16[2,128,768]{2,1,0:T(8,128)(2,1)S(1)} collective-permute-done((bf16[2,128,768]{2,1,0:T(8,128)(2,1)S(1)}, bf16[2,128,768]{2,1,0:T(8,128)(2,1)S(1)}, u32[]{:S(2)}, u32[]{:S(2)}) %collective-permute-start.2) | collective-permute-done | bytes 393248 | tf_op jit(solution)/shard_map/ppermute | solution.py:523
  66.3 2.5 project.1
  72.0 2.4 copy.130
  77.0 2.5 copy.131.key_other.value_other
  79.5 22.7 %attend.1 = (bf16[1024,192]{1,0:T(8,128)(2,1)}, bf16[3,1024,2048]{2,1,0:T(8,128)(2,1)}, f32[3,1024,128]{2,1,0:T(8,128)}) custom-call(s32[2]{0:T(128)} %pad_add_fusion.place_ref, bf16[3,1024,64]{2,1,0:T(8,128)(2,1)} %copy-done.8, bf16[6,1024,64]{2,1,0:T(8,128)(2,1)} %copy-done.5, bf16[6,1024,64]{2,1,0:T(8,128)(2,1)} %copy.131.key_other.value_other, ...), custom_call_target="tpu_custom_call" | custom-call | flops 6442450944 | bytes 12582912 | tf_op jit(solution)/shard_map/attend/pallas_call | solution.py:199
  103.5 34.9 %all_to_all.20 = bf16[8,128,192]{1,2,0:T(8,128)(2,1)S(1)} all-to-all(bf16[8,128,192]{1,2,0:T(8,128)(2,1)S(1)} %copy.133), channel_id=1, replica_groups=mesh['dp'=2,'a'=1,'z'=4,'x'=2,'c'=2] {'z','x'}, dimensions={0} | all-to-all | bytes 786432 | tf_op jit(solution)/shard_map/all_to_all | solution.py:568
  139.6 4.0 %slice.87 = bf16[768,2048]{1,0:T(8,128)(2,1)} slice(bf16[768,6912]{1,0:T(8,128)(2,1)} %all-gather.2.cloned.1.call-done), slice={[0:768], [4864:6912]} | slice | bytes 6291456 | tf_op jit(solution)/shard_map/slice | solution.py:578
  143.6 6.6 %reshape.670 = bf16[2048,768]{1,0:T(8,128)(2,1)} reshape(bf16[768,2048]{1,0:T(8,128)(2,1)} %slice.87) | data formatting | bytes 6291456 | tf_op jit(solution)/shard_map/reshape | solution.py:578
  150.3 2.1 multiply_reduce_fusion.4
  153.8 3.4 fusion.2
  157.6 2.7 fusion.15
  160.3 2.7 convolution_convert_fusion.1
  163.0 2.7 convolution_convert_fusion.2
  166.7 2.5 multiply_reduce_fusion
  169.2 2.8 convolution_convert_fusion
  172.0 6.6 %reshape.683 = bf16[768,2048]{1,0:T(8,128)(2,1)} reshape(bf16[2048,768]{1,0:T(8,128)(2,1)} %convolution_convert_fusion) | data formatting | bytes 6291456 | tf_op jit(solution)/shard_map/reshape | solution.py:610
  178.6 1.8 fusion.24
  180.4 1.5 convolution_convert_fusion.3
  181.9 2.4 copy.148
  184.4 9.1 %pad_maximum_fusion = bf16[768,6912]{1,0:T(8,128)(2,1)} fusion(bf16[768,2048]{1,0:T(8,128)(2,1)} %reshape.683, bf16[768,2048]{1,0:T(8,128)(2,1)} %convolution_convert_fusion.1, bf16[768,2048]{1,0:T(8,128)(2,1)} %convolution_convert_fusion.2, bf16[768,768]{1,0:T(8,128)(2,1)} %copy.148), kind=kLoop, calls=%fused_computation | loop fusion | flops 42467328 | bytes 21233664 | tf_op jit(solution)/shard_map/concatenate | solution.py:605
  193.5 2.5 convolution_convert_fusion.4
  197.3 15.0 %all_to_all.21 = bf16[8,128,192]{1,2,0:T(8,128)(2,1)S(1)} all-to-all(bf16[8,128,192]{1,2,0:T(8,128)(2,1)S(1)} %bitcast.169), channel_id=1, replica_groups=mesh['dp'=2,'a'=1,'z'=4,'x'=2,'c'=2] {'z','x'}, dimensions={0} | all-to-all | bytes 786432 | tf_op jit(solution)/shard_map/all_to_all | solution.py:603
  213.3 30.9 %attend_back.1 = (bf16[1024,192]{1,0:T(8,128)(2,1)}, f32[1024,384]{1,0:T(8,128)}, bf16[1024,384]{1,0:T(8,128)(2,1)}, f32[3,1,4096]{2,1,0:T(1,128)}) custom-call(s32[2]{0:T(128)} %pad_add_fusion.place_ref, bf16[1024,192]{1,0:T(8,128)(2,1)} %bitcast.180, f32[3,1024,128]{2,1,0:T(8,128)} %get-tuple-element.28.kept_ref, ...), custom_call_target="tpu_custom_call" | custom-call | flops 12884901888 | bytes 12582912 | tf_op jit(solution)/shard_map/attend_back/pallas_call | solution.py:347
  245.2 1.7 fusion.32
  252.9 4.4 %project_back.1 = (bf16[1024,768]{1,0:T(8,128)(2,1)S(1)}, f32[768,576]{1,0:T(8,128)S(1)}, f32[1,768]{1,0:T(1,128)S(1)}) custom-call(bf16[1024,192]{1,0:T(8,128)(2,1)S(1)} %copy-done.7, f32[1024,384]{1,0:T(8,128)S(1)} %copy-done.4, bf16[1024,384]{1,0:T(8,128)(2,1)S(1)} %collective-permute-done.8.received_ref, bf16[1024,768]{1,0:T(8,128)(2,1)S(1)} %copy-done.3, ...), custom_call_target="tpu_custom_call" | custom-call | flops 1811939328 | bytes 9437184 | tf_op jit(solution)/shard_map/project_back/pallas_call | solution.py:441
  260.6 1.5 collective-permute-start.11
  266.5 1.7 fusion.19
  268.3 15.4 %collective-permute-done.11 = bf16[2,128,768]{2,1,0:T(8,128)(2,1)S(1)} collective-permute-done((bf16[2,128,768]{2,1,0:T(8,128)(2,1)}, bf16[2,128,768]{2,1,0:T(8,128)(2,1)S(1)}, u32[]{:S(2)}, u32[]{:S(2)}) %collective-permute-start.11) | collective-permute-done | bytes 393248 | tf_op jit(solution)/shard_map/ppermute | solution.py:632
  283.7 26.3 %collective-permute-done.10 = bf16[2,128,768]{2,1,0:T(8,128)(2,1)} collective-permute-done((bf16[2,128,768]{2,1,0:T(8,128)(2,1)S(1)}, bf16[2,128,768]{2,1,0:T(8,128)(2,1)}, u32[]{:S(2)}, u32[]{:S(2)}) %collective-permute-start.10) | collective-permute-done | bytes 393248 | tf_op jit(solution)/shard_map/ppermute | solution.py:632
  310.0 1.4 fusion.26
  311.5 1.5 collective-permute-start.12
  313.9 7.1 %collective-permute-done.12 = bf16[128,768]{1,0:T(8,128)(2,1)S(1)} collective-permute-done((bf16[128,768]{1,0:T(8,128)(2,1)S(1)}, bf16[128,768]{1,0:T(8,128)(2,1)S(1)}, u32[]{:S(2)}, u32[]{:S(2)}) %collective-permute-start.12) | collective-permute-done | bytes 196640 | tf_op jit(solution)/shard_map/ppermute | solution.py:468
  321.3 8.1 %collective-permute-done.14 = bf16[2,1,4,24,704]{4,3,2,1,0:T(8,128)(2,1)S(1)} collective-permute-done((bf16[2,1,4,24,704]{4,3,2,1,0:T(8,128)(2,1)S(1)}, bf16[2,1,4,24,704]{4,3,2,1,0:T(8,128)(2,1)S(1)}, u32[]{:S(2)}, u32[]{:S(2)}) %collective-permute-start.14) | collective-permute-done | bytes 270368 | tf_op jit(solution)/shard_map/ppermute | solution.py:468
  329.5 1.6 collective-permute-start.15
  331.1 3.6 collective-permute-done.15
  335.4 3.3 all-to-all-start.3
  339.9 4.8 %all-to-all-done.3 = bf16[4,24,704]{2,1,0:T(8,128)(2,1)S(1)} async-done(((bf16[4,24,704]{2,1,0:T(8,128)(2,1)}), bf16[4,24,704]{2,1,0:T(8,128)(2,1)S(1)}, u32[]{:S(2)}, u32[]{:S(2)}) %all-to-all-start.3) | async-done | bytes 135200 | tf_op jit(solution)/shard_map/all_to_all | solution.py:666
  348.6 10.7 %reduce-scatter.2.cloned.1.call-done = bf16[24,6912]{1,0:T(8,128)(2,1)} async-done(((bf16[768,6912]{1,0:T(8,128)(2,1)}), bf16[24,6912]{1,0:T(8,128)(2,1)}) %reduce-scatter.2.cloned.1.call-update) | async-done | bytes 331792 | tf_op jit(solution)/shard_map/reduce_scatter | solution.py:614
  359.4 1.8 fusion.51
  (153 shorter events, 45.6 us)
Async XLA Ops:
  7.2 14.1 %copy-start.16 = (bf16[2,128,768]{2,1,0:T(8,128)(2,1)S(1)}, bf16[2,128,768]{2,1,0:T(8,128)(2,1)}, u32[]{:S(2)}) copy-start(bf16[2,128,768]{2,1,0:T(8,128)(2,1)} %param.13) | copy-start | bytes 1179652
  7.2 132.4 %all-gather.2.cloned.1.call-start = ((), (), s32[]{:S(2)}) async-start(), calls=%async_computation.5 | async-start | bytes 10948608 | tf_op jit(solution)/shard_map/all_gather | solution.py:516
  14.9 15.4 %all-to-all-start = ((bf16[4,24,704]{2,1,0:T(8,128)(2,1)}), bf16[4,24,704]{2,1,0:T(8,128)(2,1)S(1)}, u32[]{:S(2)}, u32[]{:S(2)}) async-start(bf16[4,24,704]{2,1,0:T(8,128)(2,1)} %pad_maximum_fusion.2), calls=%async_computation | async-start | bytes 294912 | tf_op jit(solution)/shard_map/all_to_all | solution.py:536
  21.2 338.1 %reduce-scatter.2.cloned.1.call-start = ((), (), s32[]{:S(2)}) async-start(), calls=%async_computation.6 | async-start | bytes 10948608 | tf_op jit(solution)/shard_map/reduce_scatter | solution.py:614
  21.3 10.5 %collective-permute-start = (bf16[128,768]{1,0:T(8,128)(2,1)S(1)}, bf16[128,768]{1,0:T(8,128)(2,1)S(1)}, u32[]{:S(2)}, u32[]{:S(2)}) collective-permute-start(bf16[128,768]{1,0:T(8,128)(2,1)S(1)} %get-tuple-element.56), channel_id=1, source_target_pairs={{0,2},{2,0},{1,3},{3,1},{4,6},{6,4},{5,7},{7,5},{8,10},{10,8},{9,1... | collective-permute-start | bytes 589832 | tf_op jit(solution)/shard_map/ppermute | solution.py:468
  30.3 6.8 %collective-permute-start.4 = (bf16[4,24,704]{2,1,0:T(8,128)(2,1)S(1)}, bf16[4,24,704]{2,1,0:T(8,128)(2,1)S(1)}, u32[]{:S(2)}, u32[]{:S(2)}) collective-permute-start(bf16[4,24,704]{2,1,0:T(8,128)(2,1)S(1)} %all-to-all-done), channel_id=1, source_target_pairs={{0,2},{2,0},{1,3},{3,1},{4,6},{6,4},{5,7},{7,5},{8,10},{10,8},{9,1... | collective-permute-start | bytes 405512 | tf_op jit(solution)/shard_map/ppermute | solution.py:468
  31.9 14.7 %collective-permute-start.1 = (bf16[2,128,768]{2,1,0:T(8,128)(2,1)S(1)}, bf16[2,128,768]{2,1,0:T(8,128)(2,1)S(1)}, u32[]{:S(2)}, u32[]{:S(2)}) collective-permute-start(bf16[2,128,768]{2,1,0:T(8,128)(2,1)S(1)} %maximum_select_fusion.4), channel_id=1, source_target_pairs={{0,4},{4,8},{8,12},{12,0},{1,5},{5,9},{9,13},{13,1},{2,6},{6,10},{... | collective-permute-start | bytes 1179656 | tf_op jit(solution)/shard_map/ppermute | solution.py:523
  33.1 32.5 %collective-permute-start.2 = (bf16[2,128,768]{2,1,0:T(8,128)(2,1)S(1)}, bf16[2,128,768]{2,1,0:T(8,128)(2,1)S(1)}, u32[]{:S(2)}, u32[]{:S(2)}) collective-permute-start(bf16[2,128,768]{2,1,0:T(8,128)(2,1)S(1)} %maximum_select_fusion.4), channel_id=1, source_target_pairs={{0,8},{4,12},{8,0},{12,4},{1,9},{5,13},{9,1},{13,5},{2,10},{6,14},... | collective-permute-start | bytes 1179656 | tf_op jit(solution)/shard_map/ppermute | solution.py:523
  34.8 30.8 %collective-permute-start.3 = (bf16[2,128,768]{2,1,0:T(8,128)(2,1)S(1)}, bf16[2,128,768]{2,1,0:T(8,128)(2,1)S(1)}, u32[]{:S(2)}, u32[]{:S(2)}) collective-permute-start(bf16[2,128,768]{2,1,0:T(8,128)(2,1)S(1)} %maximum_select_fusion.4), channel_id=1, source_target_pairs={{0,12},{4,0},{8,4},{12,8},{1,13},{5,1},{9,5},{13,9},{2,14},{6,2},{... | collective-permute-start | bytes 1179656 | tf_op jit(solution)/shard_map/ppermute | solution.py:523
  37.2 9.4 %collective-permute-start.5 = (bf16[1,4,2,24,704]{4,3,2,1,0:T(8,128)(2,1)S(1)}, bf16[1,4,2,24,704]{4,3,2,1,0:T(8,128)(2,1)S(1)}, u32[]{:S(2)}, u32[]{:S(2)}) collective-permute-start(bf16[1,4,2,24,704]{4,3,2,1,0:T(8,128)(2,1)S(1)} %maximum_select_fusion.5), channel_id=1, source_target_pairs={{0,16},{16,0},{1,17},{17,1},{2,18},{18,2},{3,19},{19,3},{4,20},{20... | collective-permute-start | bytes 811016 | tf_op jit(solution)/shard_map/ppermute | solution.py:468
  46.7 19.1 %collective-permute-start.6 = (bf16[2,1,4,2,24,704]{5,4,3,2,0,1:T(8,128)(2,1)S(1)}, bf16[2,1,4,2,24,704]{5,4,3,2,0,1:T(8,128)(2,1)S(1)}, u32[]{:S(2)}, u32[]{:S(2)}) collective-permute-start(bf16[2,1,4,2,24,704]{5,4,3,2,0,1:T(8,128)(2,1)S(1)} %maximum_select_fusion.2), channel_id=1, source_target_pairs={{0,1},{1,0},{2,3},{3,2},{4,5},{5,4},{6,7},{7,6},{8,9},{9,8},{10,11... | collective-permute-start | bytes 1622024 | tf_op jit(solution)/shard_map/ppermute | solution.py:468
  68.7 1.2 copy-start.2
  69.9 1.1 copy-start.5
  71.1 0.9 copy-start.8
  72.0 3.3 copy-start.23
  74.4 2.6 collective-permute-start.7
  143.6 8.8 %copy-start.15 = (bf16[2,128,768]{2,1,0:T(8,128)(2,1)S(1)}, bf16[2,128,768]{2,1,0:T(8,128)(2,1)}, u32[]{:S(2)}) copy-start(bf16[2,128,768]{2,1,0:T(8,128)(2,1)} %param.25) | copy-start | bytes 1179652
  150.3 2.4 copy-start.9
  152.4 14.3 %copy-start.18 = (f32[256,768]{1,0:T(8,128)}, f32[256,768]{1,0:T(8,128)S(1)}, u32[]{:S(2)}) copy-start(f32[256,768]{1,0:T(8,128)S(1)} %get-tuple-element.64) | copy-start | bytes 2359300
  152.6 5.0 %copy-start.20 = (bf16[768,6912]{1,0:T(8,128)(2,1)S(1)}, bf16[768,6912]{1,0:T(8,128)(2,1)}, u32[]{:S(2)}) copy-start(bf16[768,6912]{1,0:T(8,128)(2,1)} %all-gather.2.cloned.1.call-done) | copy-start | bytes 31850500
  160.3 8.9 %copy-start.13 = (bf16[256,2048]{1,0:T(8,128)(2,1)}, bf16[256,2048]{1,0:T(8,128)(2,1)S(1)}, u32[]{:S(2)}) copy-start(bf16[256,2048]{1,0:T(8,128)(2,1)S(1)} %get-tuple-element.49) | copy-start | bytes 3145732
  178.6 1.8 copy-start.21
  180.4 13.1 %copy-start.11 = (f32[256,768]{1,0:T(8,128)}, f32[256,768]{1,0:T(8,128)S(1)}, u32[]{:S(2)}) copy-start(f32[256,768]{1,0:T(8,128)S(1)} %fusion.24) | copy-start | bytes 2359300
  213.3 31.0 %copy-start.22 = (bf16[768]{0:T(1024)(128)(2,1)S(1)}, bf16[768]{0:T(1024)(128)(2,1)}, u32[]{:S(2)}) copy-start(bf16[768]{0:T(1024)(128)(2,1)} %get-tuple-element.38) | copy-start | bytes 4612
  244.2 4.9 %collective-permute-start.8 = (bf16[1024,384]{1,0:T(8,128)(2,1)}, bf16[1024,384]{1,0:T(8,128)(2,1)S(1)}, u32[]{:S(2)}, u32[]{:S(2)}) collective-permute-start(bf16[1024,384]{1,0:T(8,128)(2,1)} %get-tuple-element.32), channel_id=1, source_target_pairs={{0,1},{1,0},{2,3},{3,2},{4,5},{5,4},{6,7},{7,6},{8,9},{9,8},{10,11... | collective-permute-start | bytes 2359304 | tf_op jit(solution)/shard_map/ppermute | solution.py:468
  249.1 1.4 copy-start.3
  250.5 1.4 copy-start.4
  251.9 1.0 copy-start.7
  257.3 1.3 copy-start
  258.6 1.1 copy-start.6
  258.7 5.2 %copy-start.1 = (f32[768,576]{1,0:T(8,128)S(1)}, f32[768,576]{1,0:T(8,128)}, u32[]{:S(2)}) copy-start(f32[768,576]{1,0:T(8,128)} %copy-done) | copy-start | bytes 5308420
  260.6 23.1 %collective-permute-start.11 = (bf16[2,128,768]{2,1,0:T(8,128)(2,1)}, bf16[2,128,768]{2,1,0:T(8,128)(2,1)S(1)}, u32[]{:S(2)}, u32[]{:S(2)}) collective-permute-start(bf16[2,128,768]{2,1,0:T(8,128)(2,1)} %get-tuple-element.51), channel_id=1, source_target_pairs={{0,12},{4,0},{8,4},{12,8},{1,13},{5,1},{9,5},{13,9},{2,14},{6,2},{... | collective-permute-start | bytes 1179656 | tf_op jit(solution)/shard_map/ppermute | solution.py:632
  262.1 47.9 %collective-permute-start.10 = (bf16[2,128,768]{2,1,0:T(8,128)(2,1)S(1)}, bf16[2,128,768]{2,1,0:T(8,128)(2,1)}, u32[]{:S(2)}, u32[]{:S(2)}) collective-permute-start(bf16[2,128,768]{2,1,0:T(8,128)(2,1)S(1)} %get-tuple-element.52), channel_id=1, source_target_pairs={{0,8},{4,12},{8,0},{12,4},{1,9},{5,13},{9,1},{13,5},{2,10},{6,14},... | collective-permute-start | bytes 1179656 | tf_op jit(solution)/shard_map/ppermute | solution.py:632
  263.1 46.9 %collective-permute-start.9 = (bf16[2,128,768]{2,1,0:T(8,128)(2,1)S(1)}, bf16[2,128,768]{2,1,0:T(8,128)(2,1)}, u32[]{:S(2)}, u32[]{:S(2)}) collective-permute-start(bf16[2,128,768]{2,1,0:T(8,128)(2,1)S(1)} %get-tuple-element.50), channel_id=1, source_target_pairs={{0,4},{4,8},{8,12},{12,0},{1,5},{5,9},{9,13},{13,1},{2,6},{6,10},{... | collective-permute-start | bytes 1179656 | tf_op jit(solution)/shard_map/ppermute | solution.py:632
  264.0 1.2 copy-start.14
  264.0 1.4 copy-start.19
  264.2 2.3 copy-start.10
  264.4 48.7 %collective-permute-start.13 = (bf16[2,1,4,2,24,704]{5,4,2,0,3,1:T(8,128)(2,1)S(1)}, bf16[2,1,4,2,24,704]{5,4,2,0,3,1:T(8,128)(2,1)S(1)}, u32[]{:S(2)}, u32[]{:S(2)}) collective-permute-start(bf16[2,1,4,2,24,704]{5,4,2,0,3,1:T(8,128)(2,1)S(1)} %bitcast.179), channel_id=1, source_target_pairs={{0,1},{1,0},{2,3},{3,2},{4,5},{5,4},{6,7},{7,6},{8,9},{9,8},{10,11... | collective-permute-start | bytes 1622024 | tf_op jit(solution)/shard_map/ppermute | solution.py:468
  311.4 9.5 %copy-start.17 = (bf16[2,128,768]{2,1,0:T(8,128)(2,1)S(1)}, bf16[2,128,768]{2,1,0:T(8,128)(2,1)}, u32[]{:S(2)}) copy-start(bf16[2,128,768]{2,1,0:T(8,128)(2,1)} %param.13) | copy-start | bytes 1179652
  311.5 9.5 %collective-permute-start.12 = (bf16[128,768]{1,0:T(8,128)(2,1)S(1)}, bf16[128,768]{1,0:T(8,128)(2,1)S(1)}, u32[]{:S(2)}, u32[]{:S(2)}) collective-permute-start(bf16[128,768]{1,0:T(8,128)(2,1)S(1)} %fusion.42), channel_id=1, source_target_pairs={{0,2},{2,0},{1,3},{3,1},{4,6},{6,4},{5,7},{7,5},{8,10},{10,8},{9,1... | collective-permute-start | bytes 589832 | tf_op jit(solution)/shard_map/ppermute | solution.py:468
  313.2 16.2 %collective-permute-start.14 = (bf16[2,1,4,24,704]{4,3,2,1,0:T(8,128)(2,1)S(1)}, bf16[2,1,4,24,704]{4,3,2,1,0:T(8,128)(2,1)S(1)}, u32[]{:S(2)}, u32[]{:S(2)}) collective-permute-start(bf16[2,1,4,24,704]{4,3,2,1,0:T(8,128)(2,1)S(1)} %dynamic-slice_bitcast_fusion.3), channel_id=1, source_target_pairs={{0,2},{2,0},{1,3},{3,1},{4,6},{6,4},{5,7},{7,5},{8,10},{10,8},{9,1... | collective-permute-start | bytes 811016 | tf_op jit(solution)/shard_map/ppermute | solution.py:468
  321.0 17.8 %copy-start.12 = (f32[256,768]{1,0:T(8,128)S(1)}, f32[256,768]{1,0:T(8,128)}, u32[]{:S(2)}) copy-start(f32[256,768]{1,0:T(8,128)} %copy-done.11) | copy-start | bytes 2359300
  329.5 5.2 %collective-permute-start.15 = (bf16[1,4,24,704]{3,2,1,0:T(8,128)(2,1)S(1)}, bf16[1,4,24,704]{3,2,1,0:T(8,128)(2,1)S(1)}, u32[]{:S(2)}, u32[]{:S(2)}) collective-permute-start(bf16[1,4,24,704]{3,2,1,0:T(8,128)(2,1)S(1)} %dynamic-slice_bitcast_fusion.5), channel_id=1, source_target_pairs={{0,16},{16,0},{1,17},{17,1},{2,18},{18,2},{3,19},{19,3},{4,20},{20... | collective-permute-start | bytes 405512 | tf_op jit(solution)/shard_map/ppermute | solution.py:468
  335.4 9.3 %all-to-all-start.3 = ((bf16[4,24,704]{2,1,0:T(8,128)(2,1)}), bf16[4,24,704]{2,1,0:T(8,128)(2,1)S(1)}, u32[]{:S(2)}, u32[]{:S(2)}) async-start(bf16[4,24,704]{2,1,0:T(8,128)(2,1)} %fusion.45), calls=%async_computation.3 | async-start | bytes 294912 | tf_op jit(solution)/shard_map/all_to_all | solution.py:666
Sparse Core Ops, SparseCore 0:
  10.9 113.6 all-gather.1
  193.6 165.7 reduce-scatter.1

commit v2 on v1

v2 whole, which is shorter than its diff:
```python
import functools

import jax
import jax.numpy as jnp
from jax import lax
from jax.experimental import pallas as pl
from jax.experimental.pallas import tpu as pltpu
from jax.sharding import Mesh
from jax.sharding import PartitionSpec as P

H = 12
BUCKETS = 32
GROUPS = 4
CORES = 2
BLOCK = 128

epsilon = 1e-06
exactly = lax.Precision.HIGHEST
bf16 = jnp.bfloat16
f32 = jnp.float32
everyone = ("dp", "a", "zh", "zl", "x", "c")
chips = ("dp", "zh", "zl", "x")
PANEL = 256


def rms_scale(values, gain_vec):
    return (
        values * lax.rsqrt(jnp.mean(values * values, axis=-1, keepdims=True) + epsilon) * gain_vec
    )


def vmem_limit(mib):
    return pltpu.CompilerParams(vmem_limit_bytes=mib * 1024 * 1024)


def project_kernel(heads, token_ref, gain_ref, weight_ref, normed_ref, query_ref, pair_ref):
    rows = token_ref[...].astype(f32)
    scale = lax.rsqrt(jnp.mean(rows * rows, axis=-1, keepdims=True) + epsilon)
    normed = (rows * scale * gain_ref[...]).astype(bf16)
    normed_ref[...] = normed
    width = query_ref.shape[2]
    mixed = jnp.dot(
        normed, weight_ref[:, : 3 * heads * width], preferred_element_type=f32
    ).astype(bf16)
    for k in range(heads):
        query_ref[k] = mixed[:, k * width : (k + 1) * width]
        for side in range(2):
            first = (heads * (side + 1) + k) * width
            pair_ref[k, :, side * width : (side + 1) * width] = mixed[:, first : first + width]


def project(tokens, gain_row, weight, heads, width):
    rows, model = tokens.shape
    tile = 256
    return pl.pallas_call(
        functools.partial(project_kernel, heads),
        grid=(rows // tile,),
        in_specs=[
            pl.BlockSpec((tile, model), lambda i: (i, 0)),
            pl.BlockSpec((1, model), lambda i: (0, 0)),
            pl.BlockSpec(weight.shape, lambda i: (0, 0)),
        ],
        out_specs=[
            pl.BlockSpec((tile, model), lambda i: (i, 0)),
            pl.BlockSpec((heads, tile, width), lambda i: (0, i, 0)),
            pl.BlockSpec((heads, tile, 2 * width), lambda i: (0, i, 0)),
        ],
        out_shape=[
            jax.ShapeDtypeStruct((rows, model), bf16),
            jax.ShapeDtypeStruct((heads, rows, width), bf16),
            jax.ShapeDtypeStruct((heads, rows, 2 * width), bf16),
        ],
        compiler_params=vmem_limit(12),
        cost_estimate=pl.CostEstimate(
            flops=2 * rows * model * 3 * heads * width,
            bytes_accessed=8 * rows * model,
            transcendentals=0,
        ),
        name="project",
    )(tokens, gain_row, weight)


def skew_kernel(vector_ref, table_ref, row_scratch):
    span = vector_ref.shape[-1]
    for r in range(8):
        row_scratch[r : r + 1, :] = pltpu.roll(vector_ref[0], r, 1) if r else vector_ref[0]
    eight = row_scratch[...]
    rows = []
    for group in range(BLOCK // 8):
        turned = pltpu.roll(eight, 8 * group, 1) if group else eight
        rows.append(turned[:, BLOCK:span])
    for pair in range(BLOCK // 16):
        both = jnp.concatenate(rows[2 * pair : 2 * pair + 2], axis=0)
        table_ref[0, 16 * pair : 16 * pair + 16, :] = both.astype(bf16)


def skew(vectors):
    heads, unused, span = vectors.shape
    return pl.pallas_call(
        skew_kernel,
        grid=(heads,),
        in_specs=[pl.BlockSpec((1, 1, span), lambda h: (h, 0, 0))],
        out_specs=pl.BlockSpec((1, BLOCK, span - BLOCK), lambda h: (h, 0, 0)),
        out_shape=jax.ShapeDtypeStruct((heads, BLOCK, span - BLOCK), bf16),
        scratch_shapes=[pltpu.VMEM((8, span), f32)],
        compiler_params=vmem_limit(10),
        cost_estimate=pl.CostEstimate(
            flops=0, bytes_accessed=2 * heads * BLOCK * span, transcendentals=0
        ),
        name="skew",
    )(vectors)


def interleave(keys, values, own_ref, other_ref, parity, fill):
    width = keys.shape[1]
    for k in range(own_ref.shape[1] // BLOCK):
        rows = slice(k * BLOCK, (k + 1) * BLOCK)
        for source, spot in ((own_ref, parity), (other_ref, 1 - parity)):
            into = pl.ds(pl.multiple_of((2 * k + spot) * BLOCK, BLOCK), BLOCK)
            keys[into, :] = source[0, rows, :width]
            values[into, :width] = source[0, rows, width:]
            if fill:
                values[into, width:] = jnp.ones((BLOCK, width), bf16)


def table_starts(tile, step, first_block, parity, blocks):
    starts = []
    for sub in range(tile // BLOCK):
        block = 2 * (first_block + step * (tile // BLOCK) + sub) + parity
        starts.append((blocks - 1 - block) * BLOCK)
    return starts


def attend_kernel(
    tile,
    chunk,
    place_ref,
    query_ref,
    pair_own,
    pair_other,
    table,
    context_ref,
    probs_ref,
    kept_ref,
    inverse_ref,
    keys,
    values,
    scores,
):
    head, step = pl.program_id(0), pl.program_id(1)
    first_block, parity = place_ref[0], place_ref[1]
    key_count, width = keys.shape
    blocks = key_count // BLOCK
    subs = tile // BLOCK
    table = table.at[0]

    @pl.when(step == 0)
    def prepare():
        interleave(keys, values, pair_own, pair_other, parity, True)

    query = query_ref[0]
    starts = table_starts(tile, step, first_block, parity, blocks)
    lane_max = None
    for part in range(key_count // chunk):
        cols = slice(part * chunk, (part + 1) * chunk)
        product = lax.dot_general(
            query, keys[cols, :], (((1,), (1,)), ((), ())), preferred_element_type=f32
        )
        pieces = []
        for sub in range(subs):
            rows = slice(sub * BLOCK, (sub + 1) * BLOCK)
            offset = pl.multiple_of(starts[sub] + part * chunk, BLOCK)
            piece = product[rows] + table[:, pl.ds(offset, chunk)].astype(f32)
            scores[rows, cols] = piece
            for k in range(chunk // BLOCK):
                lanes = piece[:, k * BLOCK : (k + 1) * BLOCK]
                top = lanes if k == 0 else jnp.maximum(top, lanes)
            pieces.append(top)
        pieces = jnp.concatenate(pieces, axis=0)
        lane_max = pieces if lane_max is None else jnp.maximum(lane_max, pieces)
    row_max = jnp.max(lane_max, axis=-1, keepdims=True)
    total = jnp.zeros((tile, 2 * width), f32)
    for part in range(key_count // chunk):
        cols = slice(part * chunk, (part + 1) * chunk)
        low = jnp.exp(scores[:, cols] - row_max).astype(bf16)
        probs_ref[0, :, cols] = low
        total = total + jnp.dot(low, values[cols, :], preferred_element_type=f32)
    inverse = 1.0 / total[:, width:]
    value = total[:, :width] * inverse
    kept_ref[0, :, :width] = value
    kept_ref[0, :, width:] = inverse
    turned = value.T.astype(bf16)
    inverse_turned = inverse.T
    for sub in range(subs):
        lanes = slice(sub * BLOCK, (sub + 1) * BLOCK)
        rows = pl.ds(pl.multiple_of(head * width, width), width)
        context_ref[step * subs + sub, rows, :] = turned[:, lanes]
        inverse_ref[0, sub] = inverse_turned[0:1, lanes]


def attend(place, query, own, other, table):
    heads, rows, width = query.shape
    own_rows = own.shape[1]
    key_count = 2 * own_rows
    tile, chunk = 256, 512
    pairs = pl.BlockSpec((1, own_rows, 2 * width), lambda h, i, s: (h, 0, 0))
    return pl.pallas_call(
        functools.partial(attend_kernel, tile, chunk),
        grid_spec=pltpu.PrefetchScalarGridSpec(
            num_scalar_prefetch=1,
            grid=(heads, rows // tile),
            in_specs=[
                pl.BlockSpec((1, tile, width), lambda h, i, s: (h, i, 0)),
                pairs,
                pairs,
                pl.BlockSpec((1, *table.shape[1:]), lambda h, i, s: (h, 0, 0)),
            ],
            out_specs=[
                pl.BlockSpec((rows // BLOCK, heads * width, BLOCK), lambda h, i, s: (0, 0, 0)),
                pl.BlockSpec((1, tile, key_count), lambda h, i, s: (h, i, 0)),
                pl.BlockSpec((1, tile, 2 * width), lambda h, i, s: (h, i, 0)),
                pl.BlockSpec((1, tile // BLOCK, 1, BLOCK), lambda h, i, s: (h, i, 0, 0)),
            ],
            scratch_shapes=[
                pltpu.VMEM((key_count, width), bf16),
                pltpu.VMEM((key_count, 2 * width), bf16),
                pltpu.VMEM((tile, key_count), f32),
            ],
        ),
        out_shape=[
            jax.ShapeDtypeStruct((rows // BLOCK, heads * width, BLOCK), bf16),
            jax.ShapeDtypeStruct((heads, rows, key_count), bf16),
            jax.ShapeDtypeStruct((heads, rows, 2 * width), f32),
            jax.ShapeDtypeStruct((heads, rows // BLOCK, 1, BLOCK), f32),
        ],
        compiler_params=vmem_limit(54),
        cost_estimate=pl.CostEstimate(
            flops=16 * heads * rows * key_count * width,
            bytes_accessed=2 * heads * rows * key_count,
            transcendentals=heads * rows * key_count,
        ),
        name="attend",
    )(place, query, own, other, table)


def attend_back_kernel(
    tile,
    chunk,
    place_ref,
    grad_ref,
    kept_ref,
    inverse_ref,
    probs_ref,
    query_ref,
    pair_own,
    pair_other,
    hot_ref,
    query_grad_ref,
    own_grad_ref,
    other_grad_ref,
    offset_ref,
    keys,
    values,
    diagonals,
    key_sums,
    value_sums,
):
    step = pl.program_id(1)
    first_block, parity = place_ref[0], place_ref[1]
    key_count, width = keys.shape
    blocks = key_count // BLOCK
    subs = tile // BLOCK

    @pl.when(step == 0)
    def prepare():
        interleave(keys, values, pair_own, pair_other, parity, False)
        diagonals[...] = jnp.zeros_like(diagonals)
        key_sums[...] = jnp.zeros_like(key_sums)
        value_sums[...] = jnp.zeros_like(value_sums)

    turned = jnp.concatenate(
        [grad_ref[sub].astype(f32) * inverse_ref[0, sub] for sub in range(subs)], axis=1
    )
    grad_turned = turned.astype(bf16)
    scaled = grad_turned.astype(f32).T
    delta = jnp.sum(scaled * kept_ref[0, :, :width], axis=-1, keepdims=True)
    scaled = scaled.astype(bf16)
    query_turned = query_ref[0].astype(f32).T.astype(bf16)
    starts = table_starts(tile, step, first_block, parity, blocks)
    query_grad = jnp.zeros((tile, width), f32)
    for part in range(key_count // chunk):
        cols = slice(part * chunk, (part + 1) * chunk)
        prob_grad = lax.dot_general(
            scaled, values[cols, :], (((1,), (1,)), ((), ())), preferred_element_type=f32
        )
        low = probs_ref[0, :, cols]
        score_grad = low.astype(f32) * (prob_grad - delta)
        for sub in range(subs):
            rows = slice(sub * BLOCK, (sub + 1) * BLOCK)
            offset = pl.multiple_of(starts[sub] + part * chunk, BLOCK)
            diagonals[:, pl.ds(offset, chunk)] += score_grad[rows]
        score_low = score_grad.astype(bf16)
        query_grad = query_grad + jnp.dot(score_low, keys[cols, :], preferred_element_type=f32)
        key_sums[:, cols] += jnp.dot(query_turned, score_low, preferred_element_type=f32)
        value_sums[:, cols] += jnp.dot(grad_turned, low, preferred_element_type=f32)
    query_grad_ref[0] = query_grad.astype(bf16)

    @pl.when(step == pl.num_programs(1) - 1)
    def finish():
        span = diagonals.shape[1]
        eight = diagonals[0:8, :]
        for group in range(1, BLOCK // 8):
            eight = eight + pltpu.roll(
                diagonals[8 * group : 8 * group + 8, :], span - 8 * group, 1
            )
        total = eight[0:1, :]
        for r in range(1, 8):
            total = total + pltpu.roll(eight[r : r + 1, :], span - r, 1)
        total = pltpu.roll(total, BLOCK - 1, 1)
        bucket_sums = None
        for unused in range(3):
            low = total.astype(bf16)
            total = total - low.astype(f32)
            more = jnp.dot(low, hot_ref[...], preferred_element_type=f32)
            bucket_sums = more if bucket_sums is None else bucket_sums + more
        offset_ref[0] = bucket_sums
        for sums, rows in ((key_sums, slice(0, width)), (value_sums, slice(width, 2 * width))):
            for b in range(blocks // 2):
                near = pl.multiple_of((2 * b + parity) * BLOCK, BLOCK)
                far = pl.multiple_of((2 * b + 1 - parity) * BLOCK, BLOCK)
                lanes = slice(b * BLOCK, (b + 1) * BLOCK)
                own_grad_ref[0, rows, lanes] = sums[:, pl.ds(near, BLOCK)]
                other_grad_ref[0, rows, lanes] = sums[:, pl.ds(far, BLOCK)].astype(bf16)


def attend_back(place, grad, kept, inverse, probs, query, own, other, hot, first, count):
    unused, rows, width = query.shape
    own_rows = own.shape[1]
    key_count = 2 * own_rows
    span = key_count * 2
    tile, chunk = 512, 512
    pairs = pl.BlockSpec((1, own_rows, 2 * width), lambda h, i, s: (h + first, 0, 0))
    return pl.pallas_call(
        functools.partial(attend_back_kernel, tile, chunk),
        grid_spec=pltpu.PrefetchScalarGridSpec(
            num_scalar_prefetch=1,
            grid=(count, rows // tile),
            in_specs=[
                pl.BlockSpec(
                    (tile // BLOCK, width, BLOCK), lambda h, i, s: (i, h + first, 0)
                ),
                pl.BlockSpec((1, tile, 2 * width), lambda h, i, s: (h + first, i, 0)),
                pl.BlockSpec((1, tile // BLOCK, 1, BLOCK), lambda h, i, s: (h + first, i, 0, 0)),
                pl.BlockSpec((1, tile, key_count), lambda h, i, s: (h + first, i, 0)),
                pl.BlockSpec((1, tile, width), lambda h, i, s: (h + first, i, 0)),
                pairs,
                pairs,
                pl.BlockSpec(hot.shape, lambda h, i, s: (0, 0)),
            ],
            out_specs=[
                pl.BlockSpec((1, tile, width), lambda h, i, s: (h, i, 0)),
                pl.BlockSpec((1, 2 * width, own_rows), lambda h, i, s: (h, 0, 0)),
                pl.BlockSpec((1, 2 * width, own_rows), lambda h, i, s: (h, 0, 0)),
                pl.BlockSpec((1, 1, hot.shape[1]), lambda h, i, s: (h, 0, 0)),
            ],
            scratch_shapes=[
                pltpu.VMEM((key_count, width), bf16),
                pltpu.VMEM((key_count, width), bf16),
                pltpu.VMEM((BLOCK, span), f32),
                pltpu.VMEM((width, key_count), f32),
                pltpu.VMEM((width, key_count), f32),
            ],
        ),
        out_shape=[
            jax.ShapeDtypeStruct((count, rows, width), bf16),
            jax.ShapeDtypeStruct((count, 2 * width, own_rows), f32),
            jax.ShapeDtypeStruct((count, 2 * width, own_rows), bf16),
            jax.ShapeDtypeStruct((count, 1, hot.shape[1]), f32),
        ],
        compiler_params=vmem_limit(54),
        cost_estimate=pl.CostEstimate(
            flops=32 * count * rows * key_count * width,
            bytes_accessed=2 * count * rows * key_count,
            transcendentals=0,
        ),
        name="attend_back",
    )(place, grad, kept, inverse, probs, query, own, other, hot)


def project_back_kernel(splits, place_ref, normed_ref, token_ref, weight_ref, *refs):
    extra_ref, given = refs[0], refs[1:-9]
    rows_refs, kept_ref, sent_ref, turned, sums, gains = (*[refs[-9:-5]], *refs[-5:])
    step = pl.program_id(0)
    query_grads = given[: len(splits)]
    owns = given[len(splits) : 2 * len(splits)]
    came = given[2 * len(splits) :]
    heads = sum(splits)
    width = query_grads[0].shape[2]
    part = heads * width
    head = 0
    for k, count in enumerate(splits):
        for h in range(count):
            turned[head * width : (head + 1) * width, :] = (
                query_grads[k][h].astype(f32).T.astype(bf16)
            )
            both = (owns[k][h] + came[k][h].astype(f32)).astype(bf16)
            for side in range(2):
                at = part * (side + 1) + head * width
                turned[at : at + width, :] = both[side * width : (side + 1) * width]
            head += 1
    grads = turned[...]
    normed_grad = lax.dot_general(
        grads,
        weight_ref[:, : 3 * part],
        (((0,), (1,)), ((), ())),
        preferred_element_type=f32,
    )
    low = normed_grad.astype(bf16)
    half, model = low.shape[0] // 2, low.shape[1]
    for k in range(2):

        @pl.when(place_ref[0] == k)
        def store():
            for share in range(2):
                lanes = slice(share * model // 2, (share + 1) * model // 2)
                rows_refs[share][0] = low[k * half : (k + 1) * half, lanes]
                rows_refs[2 + share][0] = low[(1 - k) * half : (2 - k) * half, lanes]

    tokens = token_ref[...].astype(f32)
    scale = lax.rsqrt(jnp.mean(tokens * tokens, axis=-1, keepdims=True) + epsilon)
    gain = jnp.sum(normed_grad * (tokens * scale), axis=0, keepdims=True)
    update = jnp.dot(grads, normed_ref[...], preferred_element_type=f32)

    @pl.when(step == 0)
    def start():
        sums[...] = update
        gains[...] = extra_ref[...]

    @pl.when(step != 0)
    def more():
        sums[...] += update

    gains[0:1, :] += gain

    @pl.when(step == pl.num_programs(0) - 1)
    def finish():
        update = sums[...].T
        extras = jnp.concatenate(
            [gains[...], jnp.zeros((BLOCK - gains.shape[0], model), f32)], axis=0
        ).T
        owners, rows, columns = kept_ref.shape
        for k in range(2):

            @pl.when(place_ref[1] == k)
            def pack():
                for owner in range(owners):
                    for ref, core in ((kept_ref, k), (sent_ref, 1 - k)):
                        at = slice((2 * owner + core) * rows, (2 * owner + core + 1) * rows)
                        ref[owner, :, : 3 * part] = update[at].astype(bf16)
                        ref[owner, :, 3 * part :] = extras[at].astype(bf16)


def project_back(place, query_grads, owns, came, normed, tokens, weight, extra, weight_rows):
    rows, model = tokens.shape
    splits = tuple(value.shape[0] for value in query_grads)
    width = query_grads[0].shape[2]
    part = sum(splits) * width
    tile = 2 * BLOCK
    steps = rows // tile
    by_rows = pl.BlockSpec((tile, model), lambda i, s: (i, 0))
    whole = lambda shape: pl.BlockSpec(shape, lambda i, s: (0, 0))
    pairs = [pl.BlockSpec((count, 2 * width, tile), lambda i, s: (0, 0, i)) for count in splits]
    share = (1, BLOCK, model // 2)
    packed = (model // (2 * weight_rows), weight_rows, 3 * part + BLOCK)
    return pl.pallas_call(
        functools.partial(project_back_kernel, splits),
        grid_spec=pltpu.PrefetchScalarGridSpec(
            num_scalar_prefetch=1,
            grid=(steps,),
            in_specs=[by_rows, by_rows, whole(weight.shape), whole(extra.shape)]
            + [pl.BlockSpec((count, tile, width), lambda i, s: (0, i, 0)) for count in splits]
            + pairs
            + pairs,
            out_specs=[pl.BlockSpec(share, lambda i, s: (i, 0, 0))] * 4
            + [pl.BlockSpec(packed, lambda i, s: (0, 0, 0))] * 2,
            scratch_shapes=[
                pltpu.VMEM((3 * part, tile), bf16),
                pltpu.VMEM((3 * part, model), f32),
                pltpu.VMEM(extra.shape, f32),
            ],
        ),
        out_shape=[jax.ShapeDtypeStruct((steps, *share[1:]), bf16)] * 4
        + [jax.ShapeDtypeStruct(packed, bf16)] * 2,
        compiler_params=vmem_limit(60),
        cost_estimate=pl.CostEstimate(
            flops=12 * rows * model * part, bytes_accessed=12 * rows * model, transcendentals=0
        ),
        name="project_back",
    )(place, normed, tokens, weight, extra, *query_grads, *owns, *came)


def rows_kernel(place_ref, token_ref, residual_ref, gain_ref, *refs):
    terms, grad_ref = refs[:-1], refs[-1]
    per_share = len(terms) // 2
    seqs, local_rows, model = token_ref.shape
    for seq in range(seqs):
        shares = []
        for share in range(2):
            total = jnp.zeros((local_rows, model // 2), f32)
            for shift in range(per_share):
                term = terms[share * per_share + shift][...].astype(f32)
                total = total + jnp.where(place_ref[shift] == seq, term, 0.0)
            shares.append(total)
        weighted = jnp.concatenate(shares, axis=1) * gain_ref[...]
        tokens = token_ref[seq].astype(f32)
        scale = lax.rsqrt(jnp.mean(tokens * tokens, axis=-1, keepdims=True) + epsilon)
        inner = jnp.mean(weighted * tokens, axis=-1, keepdims=True)
        rows = slice(seq * local_rows, (seq + 1) * local_rows)
        grad_ref[seq] = (
            residual_ref[rows] + scale * weighted - tokens * (scale * scale * scale * inner)
        )


def rows_stage(place, tokens, residual_grad, gain_row, terms):
    whole = lambda array: pl.BlockSpec(array.shape, lambda i, s: (0,) * array.ndim)
    given = (tokens, residual_grad, gain_row, *terms)
    return pl.pallas_call(
        rows_kernel,
        grid_spec=pltpu.PrefetchScalarGridSpec(
            num_scalar_prefetch=1,
            grid=(1,),
            in_specs=[whole(array) for array in given],
            out_specs=whole(tokens),
        ),
        out_shape=jax.ShapeDtypeStruct(tokens.shape, f32),
        compiler_params=vmem_limit(16),
        cost_estimate=pl.CostEstimate(
            flops=20 * tokens.size, bytes_accessed=16 * tokens.size, transcendentals=0
        ),
        name="rows_stage",
    )(place, *given)


def output_kernel(context_ref, token_ref, gain_ref, *refs):
    weights, (residual_ref, normed_ref) = refs[:-2], refs[-2:]
    seqs, local_rows, model = token_ref.shape
    groups = context_ref.shape[0] // seqs
    part = context_ref.shape[1]
    for seq in range(seqs):
        rows = slice(seq * local_rows, (seq + 1) * local_rows)
        for p, weight_ref in enumerate(weights):
            lanes = slice(p * PANEL, (p + 1) * PANEL)
            weight = weight_ref[...].reshape(model, PANEL)
            total = token_ref[seq, :, lanes].astype(f32)
            for group in range(groups):
                total = total + lax.dot_general(
                    context_ref[seq * groups + group],
                    weight[group * part : (group + 1) * part],
                    (((0,), (0,)), ((), ())),
                    preferred_element_type=f32,
                )
            residual_ref[rows, lanes] = total
    normed_ref[...] = rms_scale(residual_ref[...], gain_ref[...]).astype(bf16)


def output_stage(context, tokens, gain_row, everything, shape):
    seqs, local_rows, model = tokens.shape
    whole = lambda array: pl.BlockSpec(array.shape, lambda i: (0,) * array.ndim)
    return pl.pallas_call(
        output_kernel,
        grid=(1,),
        in_specs=[whole(context), whole(tokens), whole(gain_row)] + shape.output_specs(),
        out_specs=[pl.BlockSpec((seqs * local_rows, model), lambda i: (0, 0))] * 2,
        out_shape=[
            jax.ShapeDtypeStruct((seqs * local_rows, model), f32),
            jax.ShapeDtypeStruct((seqs * local_rows, model), bf16),
        ],
        compiler_params=vmem_limit(60),
        cost_estimate=pl.CostEstimate(
            flops=2 * seqs * local_rows * model * model,
            bytes_accessed=2 * model * model,
            transcendentals=0,
        ),
        name="output_stage",
    )(context, tokens, gain_row, *[everything] * len(shape.output_specs()))


def hidden_kernel(
    shape, place_ref, normed_own, normed_other, down_own, down_other, gate_w, upper_w, *refs
):
    panels = shape.model // PANEL
    down_w = refs[:panels]
    out_own, out_other, norm_own, norm_other = refs[panels : panels + 4]
    grad_refs, (normed, downs, outs, norms) = refs[panels + 4 : -4], refs[-4:]
    step = pl.program_id(0)
    x, dp = place_ref[0], place_ref[1]
    half = normed_own.shape[0]

    @pl.when(step == 0)
    def gather():
        normed[:half] = normed_own[...]
        normed[half:] = normed_other[...]
        downs[:half] = down_own[...]
        downs[half:] = down_other[...]

    rows, grad = normed[...], downs[...]
    gate = gate_w[...].reshape(shape.model, PANEL)
    upper = upper_w[...].reshape(shape.model, PANEL)
    gate_pre = jnp.dot(rows, gate, preferred_element_type=f32)
    up_pre = jnp.dot(rows, upper, preferred_element_type=f32)
    hidden_grad = None
    for p in range(panels):
        product = lax.dot_general(
            grad[:, p * PANEL : (p + 1) * PANEL],
            down_w[p][...].reshape(PANEL, PANEL),
            (((1,), (1,)), ((), ())),
            preferred_element_type=f32,
        )
        hidden_grad = product if hidden_grad is None else hidden_grad + product
    slope = 0.7978845608028654
    square = gate_pre * gate_pre
    bend = jnp.tanh(slope * gate_pre * (1.0 + 0.044715 * square))
    share = 0.5 * (1.0 + bend)
    curved = gate_pre * share
    hidden = (curved * up_pre).astype(bf16)
    steep = share + 0.5 * gate_pre * (1.0 - bend * bend) * (
        slope * (1.0 + 3.0 * 0.044715 * square)
    )
    gate_low = (hidden_grad * up_pre * steep).astype(bf16)
    up_low = (hidden_grad * curved).astype(bf16)
    across = (((1,), (1,)), ((), ()))
    norm_part = lax.dot_general(gate_low, gate, across, preferred_element_type=f32)
    norm_part += lax.dot_general(up_low, upper, across, preferred_element_type=f32)

    @pl.when(step == 0)
    def first():
        norms[...] = norm_part

    @pl.when(step != 0)
    def later():
        norms[...] += norm_part

    along = (((0,), (0,)), ((), ()))
    for p in range(panels):
        lanes = slice(p * PANEL, (p + 1) * PANEL)
        product = jnp.dot(
            hidden, down_w[p][...].reshape(PANEL, PANEL), preferred_element_type=f32
        )

        @pl.when(step == 0)
        def first_out():
            outs[:, lanes] = product

        @pl.when(step != 0)
        def later_out():
            outs[:, lanes] += product

        shape.store_down(
            grad_refs,
            step,
            p,
            lax.dot_general(hidden, grad[:, lanes], along, preferred_element_type=f32),
            x,
            dp,
        )
    for side, low in enumerate((gate_low, up_low)):
        shape.store_side(
            grad_refs,
            step,
            side,
            lax.dot_general(rows, low, along, preferred_element_type=f32),
            x,
            dp,
        )

    @pl.when(step == shape.steps - 1)
    def finish():
        out_own[...] = outs[:half]
        out_other[...] = outs[half:].astype(bf16)
        norm_own[...] = norms[:half]
        norm_other[...] = norms[half:].astype(bf16)


class PackedWeights:
    def __init__(self, model, hidden_half, pieces):
        self.model, self.pieces = model, pieces
        self.side = model // pieces
        self.deep = hidden_half // pieces
        self.steps = hidden_half // PANEL
        self.panels = model // PANEL
        self.side_rows = 2 * self.steps * self.side
        self.grad_rows = self.side_rows + self.panels * self.deep

    def side_spec(self, shift):
        return pl.BlockSpec((self.pieces, self.side, PANEL), lambda j: (0, j + shift, 0))

    def down_specs(self):
        if self.pieces == 1:
            first = self.side_rows // PANEL
            each = self.deep // PANEL
            return [
                pl.BlockSpec((1, PANEL, PANEL), lambda j, p=p: (0, first + p * each + j, 0))
                for p in range(self.panels)
            ]
        first = self.side_rows // self.deep
        some = self.pieces // self.steps
        return [
            pl.BlockSpec((some, self.deep, PANEL), lambda j, p=p: (j, first + p, 0))
            for p in range(self.panels)
        ]

    def output_specs(self):
        first = self.grad_rows // self.side
        return [
            pl.BlockSpec((self.pieces, self.side, PANEL), lambda j, p=p: (0, first + p, 0))
            for p in range(self.panels)
        ]

    def grad_shapes(self):
        if self.pieces == 1:
            return [(1, self.grad_rows, PANEL)]
        side = self.steps * self.side
        first = (self.pieces // 2, side + self.deep, PANEL)
        second = (self.pieces // 2, side + (self.panels - 1) * self.deep, PANEL)
        return [first, first, second, second]

    def store_side(self, refs, step, side, value, x, dp):
        low = value.astype(bf16).reshape(self.pieces, self.side, PANEL)
        if self.pieces == 1:
            start = pl.multiple_of((step + side * self.steps) * self.side, 16)
            refs[0][:, pl.ds(start, self.side), :] = low
            return
        rows = pl.ds(pl.multiple_of(step * self.side, 16), self.side)
        half = self.pieces // 2
        if side:
            for k in range(2):

                @pl.when(dp == k)
                def store_upper():
                    refs[2][:, rows, :] = low[k * half : (k + 1) * half]
                    refs[3][:, rows, :] = low[(1 - k) * half : (2 - k) * half]
        else:
            pairs = low.reshape(half, 2, self.side, PANEL)
            for k in range(2):

                @pl.when(x == k)
                def store_gate():
                    refs[0][:, rows, :] = pairs[:, k]
                    refs[1][:, rows, :] = pairs[:, 1 - k]

    def store_down(self, refs, step, p, value, x, dp):
        low = value.astype(bf16)
        if self.pieces == 1:
            start = pl.multiple_of(self.side_rows + p * self.deep + step * PANEL, PANEL)
            refs[0][0, pl.ds(start, PANEL), :] = low
            return
        some = self.pieces // self.steps
        first = self.steps * self.side
        if p == 0:
            pairs = low.reshape(some // 2, 2, self.deep, PANEL)
            spots = pl.ds(step * (some // 2), some // 2)
            for k in range(2):

                @pl.when(x == k)
                def store_first():
                    refs[0][spots, first : first + self.deep, :] = pairs[:, k]
                    refs[1][spots, first : first + self.deep, :] = pairs[:, 1 - k]
        else:
            pieces = low.reshape(some, self.deep, PANEL)
            per_half = self.steps // 2
            spots = pl.ds((step % per_half) * some, some)
            first += (p - 1) * self.deep
            for slot, mine in ((2, step // per_half == dp), (3, step // per_half != dp)):

                @pl.when(mine)
                def store_other():
                    refs[slot][spots, first : first + self.deep, :] = pieces


def hidden_stage(place, normed, normed_other, down, down_other, everything, shape):
    half, model = normed.shape
    whole = pl.BlockSpec((half, model), lambda j, s: (0, 0))
    with_place = lambda spec: pl.BlockSpec(
        spec.block_shape, lambda j, s, spec=spec: spec.index_map(j)
    )
    grads = shape.grad_shapes()
    weights = [shape.side_spec(0), shape.side_spec(shape.steps)] + shape.down_specs()
    return pl.pallas_call(
        functools.partial(hidden_kernel, shape),
        grid_spec=pltpu.PrefetchScalarGridSpec(
            num_scalar_prefetch=1,
            grid=(shape.steps,),
            in_specs=[whole] * 4 + [with_place(spec) for spec in weights],
            out_specs=[whole] * 4 + [pl.BlockSpec(size, lambda j, s: (0, 0, 0)) for size in grads],
            scratch_shapes=[
                pltpu.VMEM((2 * half, model), bf16),
                pltpu.VMEM((2 * half, model), bf16),
                pltpu.VMEM((2 * half, model), f32),
                pltpu.VMEM((2 * half, model), f32),
            ],
        ),
        out_shape=[
            jax.ShapeDtypeStruct((half, model), f32),
            jax.ShapeDtypeStruct((half, model), bf16),
            jax.ShapeDtypeStruct((half, model), f32),
            jax.ShapeDtypeStruct((half, model), bf16),
        ]
        + [jax.ShapeDtypeStruct(size, bf16) for size in grads],
        compiler_params=vmem_limit(60),
        cost_estimate=pl.CostEstimate(
            flops=18 * 2 * half * model * shape.steps * PANEL,
            bytes_accessed=12 * model * shape.steps * PANEL,
            transcendentals=0,
        ),
        name="hidden_stage",
    )(place, normed, normed_other, down, down_other, *[everything] * (2 + shape.panels))


def output_back_kernel(norm_own, norm_other, residual_ref, down_ref, gain_ref, context_ref, *refs):
    weights = refs[:-4]
    rows_ref, gain_grad_ref, context_grad_ref, weight_grad_ref = refs[-4:]
    residual, gain = residual_ref[...], gain_ref[...]
    norm_grad = norm_own[...] + norm_other[...].astype(f32)
    scale = lax.rsqrt(jnp.mean(residual * residual, axis=-1, keepdims=True) + epsilon)
    gain_grad_ref[...] = jnp.sum(norm_grad * (residual * scale), axis=0, keepdims=True)
    weighted = norm_grad * gain
    inner = jnp.mean(weighted * residual, axis=-1, keepdims=True)
    rows_grad = (
        down_ref[...].astype(f32)
        + scale * weighted
        - residual * (scale * scale * scale * inner)
    )
    rows_ref[...] = rows_grad
    low = rows_grad.astype(bf16)
    blocks, part, local_rows = context_ref.shape
    seqs = rows_grad.shape[0] // local_rows
    groups = blocks // seqs
    model = residual.shape[1]
    for group in range(groups):
        columns = slice(group * part, (group + 1) * part)
        product = None
        for p, weight_ref in enumerate(weights):
            more = lax.dot_general(
                weight_ref[...].reshape(model, PANEL)[columns],
                low[:, p * PANEL : (p + 1) * PANEL],
                (((1,), (1,)), ((), ())),
                preferred_element_type=f32,
            )
            product = more if product is None else product + more
        turned = product.astype(bf16)
        total = None
        for seq in range(seqs):
            rows = slice(seq * local_rows, (seq + 1) * local_rows)
            context_grad_ref[seq * groups + group] = turned[:, rows]
            more = jnp.dot(
                context_ref[seq * groups + group], low[rows], preferred_element_type=f32
            )
            total = more if total is None else total + more
        weight_grad_ref[columns, :] = total.astype(bf16)


def output_back(norm_own, norm_other, residual, down, gain_row, context, everything, shape):
    rows, model = residual.shape
    whole = lambda array: pl.BlockSpec(array.shape, lambda i: (0,) * array.ndim)
    given = (norm_own, norm_other, residual, down, gain_row, context)
    out_shape = [
        jax.ShapeDtypeStruct((rows, model), f32),
        jax.ShapeDtypeStruct((1, model), f32),
        jax.ShapeDtypeStruct(context.shape, bf16),
        jax.ShapeDtypeStruct((model, model), bf16),
    ]
    return pl.pallas_call(
        output_back_kernel,
        grid=(1,),
        in_specs=[whole(array) for array in given] + shape.output_specs(),
        out_specs=[whole(array) for array in out_shape],
        out_shape=out_shape,
        compiler_params=vmem_limit(60),
        cost_estimate=pl.CostEstimate(
            flops=4 * rows * model * model, bytes_accessed=4 * model * model, transcendentals=0
        ),
        name="output_back",
    )(*given, *[everything] * shape.panels)


def owned_kernel(part, term_ref, *refs):
    groups, rows, columns = term_ref.shape
    model = refs[0].shape[1]
    total = None
    for group in range(groups):
        term = term_ref[group].astype(f32)
        for k in range(3):
            first = model + k * part
            refs[k][:, group * part : (group + 1) * part] = term[:, first : first + part]
        total = term if total is None else total + term
    refs[3][...] = total[:, :model]
    extras = total[:, model + 3 * part :]
    short = jnp.zeros((BLOCK - rows, BLOCK), f32)
    refs[4][...] = jnp.concatenate([extras, short], axis=0).T[:8]


def owned_stage(terms, model, part):
    groups, rows, columns = terms.shape
    whole = lambda array: pl.BlockSpec(array.shape, lambda i: (0,) * array.ndim)
    out_shape = [jax.ShapeDtypeStruct((rows, model), f32)] * 4 + [
        jax.ShapeDtypeStruct((8, BLOCK), f32)
    ]
    return pl.pallas_call(
        functools.partial(owned_kernel, part),
        grid=(1,),
        in_specs=[whole(terms)],
        out_specs=[whole(array) for array in out_shape],
        out_shape=out_shape,
        compiler_params=vmem_limit(16),
        cost_estimate=pl.CostEstimate(
            flops=terms.size, bytes_accessed=4 * terms.size, transcendentals=0
        ),
        name="owned_stage",
    )(terms)


def swap(value, axis):
    return lax.ppermute(value, axis, [(0, 1), (1, 0)])


def pick(pair, index, axis):
    return lax.dynamic_index_in_dim(pair, index, axis, keepdims=False)


def in_order(mine, theirs, index, axis):
    return jnp.where(
        index == 0, jnp.stack([mine, theirs], axis), jnp.stack([theirs, mine], axis)
    )


def plus(mine, came):
    return (mine.astype(f32) + came.astype(f32)).astype(bf16)


def halve(value, index, name, axis):
    return plus(pick(value, index, axis), swap(pick(value, 1 - index, axis), name))


def turn(value, shift):
    count = 2 * 2
    return lax.ppermute(value, ("zh", "zl"), [(i, (i + shift) % count) for i in range(count)])


def exchange(value, axes, index, axis):
    count = value.shape[axis]
    result = value
    for mask in range(1, count):
        came = lax.ppermute(
            pick(value, index ^ mask, axis), axes, [(i, i ^ mask) for i in range(count)]
        )
        result = lax.dynamic_update_index_in_dim(result, came, index ^ mask, axis)
    return result


def columns_in_panels(weight):
    rows, cols = weight.shape
    return jnp.transpose(weight.reshape(rows, cols // PANEL, PANEL), (1, 0, 2)).reshape(
        rows * cols // PANEL, PANEL
    )


def own_half(weight, each, c):
    rows, cols = weight.shape
    return pick(weight.reshape(rows, cols // (2 * each), 2, each), c, 2).reshape(rows, cols // 2)


def body(
    inputs,
    w_query,
    w_key,
    w_value,
    w_output,
    w_gate,
    w_upper,
    w_down,
    gain_one,
    gain_two,
    bias_table,
    buckets,
    cotangent,
    sizes,
):
    along_dp, along_a = sizes
    dp, a, x, c = (lax.axis_index(name) for name in ("dp", "a", "x", "c"))
    zh, zl = lax.axis_index("zh"), lax.axis_index("zl")
    z, group = 2 * zh + zl, 2 * zl + x
    depth = 4
    seqs, local_rows, model = inputs.shape
    length = buckets.shape[0] // 2 + 1
    width = model // H
    heads = H // GROUPS
    part = heads * width
    weight_rows, hidden_units = w_gate.shape
    each = w_down.shape[0]
    own_count = depth * 2 * local_rows
    token_count = seqs * local_rows

    column = jnp.zeros((depth, local_rows, model), bf16)
    column = lax.dynamic_update_index_in_dim(column, pick(inputs, zh, 0), z, 0)
    for shift in range(1, depth):
        arriving = turn(pick(inputs, (z + shift) % depth // 2, 0), shift)
        column = lax.dynamic_update_index_in_dim(column, arriving, (z - shift) % depth, 0)
    tokens_own = in_order(column, swap(column, "x"), x, 1).reshape(own_count, model)

    blocks = [
        jnp.transpose(w.reshape(weight_rows, GROUPS, part), (1, 0, 2))
        for w in (w_query, w_key, w_value)
    ]
    table_column = jnp.pad(bias_table, (0, weight_rows - bias_table.shape[0]))
    extra = jnp.stack([gain_one, gain_two, table_column], axis=1)
    extra = jnp.pad(extra, ((0, 0), (0, BLOCK - extra.shape[1])))
    extra = jnp.broadcast_to(extra[None], (GROUPS, weight_rows, BLOCK))
    columns = lax.all_to_all(
        jnp.concatenate([*blocks, extra], axis=2), ("zl", "x"), 0, 0, tiled=True
    )
    columns = in_order(columns, swap(columns, "zh"), zh, 0)
    if along_a > 1:
        columns = lax.all_gather(columns, "a", axis=0)
    columns = in_order(columns, swap(columns, "dp"), dp, 0)
    columns = in_order(columns, swap(columns, "c"), c, columns.ndim - 2)
    columns = columns.reshape(model, 3 * part + BLOCK)
    gain_a = columns[:, 3 * part].astype(f32).reshape(1, model)
    gain_b = columns[:, 3 * part + 1].astype(f32).reshape(1, model)
    table = columns[:, 3 * part + 2].reshape(model // weight_rows, weight_rows)
    table = table[:, : bias_table.shape[0]].reshape(BUCKETS, H)
    padded = jnp.pad(buckets, (0, 1), constant_values=BLOCK)
    hot = (padded[:, None] == jnp.arange(BLOCK, dtype=jnp.int32)[None, :]).astype(bf16)
    own_table = lax.dynamic_slice_in_dim(table, group * heads, heads, 1)
    own_table = jnp.pad(own_table, ((0, BLOCK - BUCKETS), (0, 0)))
    ahead = jnp.pad(buckets, (1, 0), constant_values=BLOCK)
    hot_ahead = (ahead[None, :] == jnp.arange(BLOCK, dtype=jnp.int32)[:, None]).astype(bf16)
    vectors = lax.dot_general(
        own_table, hot_ahead, (((0,), (0,)), ((), ())), preferred_element_type=f32
    ).reshape(heads, 1, 2 * length)

    if along_a == 1:
        sent = [own_half(w, each, 1 - c) for w in (w_gate, w_upper)] + [w_output]
        came = swap(jnp.concatenate(sent, axis=1), "c")
        kept = [own_half(w, each, c) for w in (w_gate, w_upper)] + [w_output]
        both = in_order(jnp.concatenate(kept, axis=1), came, c, 0).reshape(2 * weight_rows, -1)
        packed = jnp.concatenate(
            [
                columns_in_panels(both[:, :hidden_units]),
                columns_in_panels(w_down),
                columns_in_panels(both[:, hidden_units:]),
            ],
            axis=0,
        )
        pieces = along_dp * depth * 2
        everything = lax.all_gather(packed, chips, axis=0, tiled=True)
        everything = everything.reshape(pieces, packed.shape[0], PANEL)
    else:
        pieces = 1
        gate_all, upper_all, down_all, output_all = (
            lax.all_gather(w, everyone, axis=0, tiled=True)
            for w in (w_gate, w_upper, w_down, w_output)
        )
        down_half = pick(down_all.reshape(-1, 2, each, model), c, 1).reshape(-1, model)
        everything = jnp.concatenate(
            [
                columns_in_panels(own_half(gate_all, each, c)),
                columns_in_panels(own_half(upper_all, each, c)),
                columns_in_panels(down_half),
                columns_in_panels(output_all),
            ],
            axis=0,
        )[None]
    shape = PackedWeights(model, hidden_units // 2, pieces)

    if along_a > 1:
        tokens_all = lax.all_gather(tokens_own, "a", axis=0, tiled=True)
    else:
        tokens_all = tokens_own
    normed, query, own = project(tokens_all, gain_a, columns, heads, width)
    if along_a > 1:
        query = lax.dynamic_slice_in_dim(query, a * own_count, own_count, 1)
        normed = lax.dynamic_slice_in_dim(normed, a * own_count, own_count, 0)
    other = swap(own, "c")
    biases = skew(vectors)
    place = jnp.stack([a * (own_count // BLOCK), c]).astype(jnp.int32)
    context_own, probs, kept, inverse = attend(place, query, own, other, biases)
    owners = ("zh", "zl", "x")
    context = lax.all_to_all(context_own, owners, 0, 0, tiled=True)

    down_grad = cotangent.reshape(token_count, model)
    down_other = swap(down_grad, "c")
    residual, second = output_stage(context, inputs, gain_b, everything, shape)
    second_other = swap(second, "c")
    sides_place = jnp.stack([x, dp]).astype(jnp.int32)
    out_own, out_other, norm_own, norm_other, *big_grads = hidden_stage(
        sides_place, second, second_other, down_grad, down_other, everything, shape
    )
    norm_came = swap(norm_other, "c")
    out_came = swap(out_other, "c")
    outputs = (residual + out_own + out_came.astype(f32)).astype(bf16)
    residual_grad, gain_b_grad, context_sent, output_grad = output_back(
        norm_own, norm_came, residual, down_grad, gain_b, context, everything, shape
    )
    context_grad = lax.all_to_all(context_sent, owners, 0, 0, tiled=True)
    if along_a == 1:
        first_terms, first_sent, second_terms, second_sent = big_grads
        first_came = swap(first_sent, "x")
        second_came = swap(second_sent, "dp")
    output_terms = output_grad.reshape(
        along_dp, along_a, 2, GROUPS, CORES, weight_rows, model
    )
    output_terms = halve(output_terms, c, "c", 4)

    if along_a == 1:
        context_grad, first_came, second_came = lax.optimization_barrier(
            (context_grad, first_came, second_came)
        )
        first_terms = plus(first_terms, first_came).reshape(along_dp, depth, -1, PANEL)
        second_terms = plus(second_terms, second_came).reshape(depth, 2, -1, PANEL)
        first_terms, second_terms, context_grad, output_terms = lax.optimization_barrier(
            (first_terms, second_terms, context_grad, output_terms)
        )
        first_came = swap(pick(first_terms, 1 - dp, 0), "dp")
        second_came = swap(pick(second_terms, 1 - x, 1), "x")
    output_came = swap(pick(output_terms, 1 - dp, 0), "dp")

    query_grads, owns, came, offset_grads = [], [], [], []
    for first, count in ((0, 1), (1, heads - 1)):
        query_grad, own_grad, other_grad, offset_grad = attend_back(
            place, context_grad, kept, inverse, probs, query, own, other, hot, first, count
        )
        if along_a > 1:
            own_grad, other_grad = (
                lax.psum_scatter(value, "a", scatter_dimension=2, tiled=True)
                for value in (own_grad, other_grad)
            )
        elif first == 0:
            first_came, second_came, output_came, query_grad, own_grad, other_grad, offset_grad = (
                lax.optimization_barrier(
                    (
                        first_came,
                        second_came,
                        output_came,
                        query_grad,
                        own_grad,
                        other_grad,
                        offset_grad,
                    )
                )
            )
            terms = jnp.concatenate(
                [
                    plus(pick(first_terms, dp, 0), first_came),
                    plus(pick(second_terms, x, 1), second_came),
                ],
                axis=1,
            )
            output_terms = plus(pick(output_terms, dp, 0), output_came)
            terms, output_terms, context_grad = lax.optimization_barrier(
                (terms, output_terms, context_grad)
            )
            column_came = [
                turn(pick(terms, (z + shift) % depth, 0), shift) for shift in range(1, depth)
            ]
        else:
            *column_came, query_grad, own_grad, other_grad, offset_grad = (
                lax.optimization_barrier(
                    (*column_came, query_grad, own_grad, other_grad, offset_grad)
                )
            )
        query_grads.append(query_grad)
        owns.append(own_grad)
        came.append(swap(other_grad, "c"))
        offset_grads.append(offset_grad)
    if along_a > 1:
        output_terms = plus(pick(output_terms, dp, 0), output_came)
    per_owner = bias_table.shape[0]
    bucket_sums = jnp.concatenate(offset_grads, axis=0)[:, 0, :BUCKETS]
    spot = jnp.arange(model, dtype=jnp.int32)
    entry = spot // weight_rows * per_owner + spot % weight_rows
    entry = jnp.where(spot % weight_rows < per_owner, entry, -1)
    spread = (entry[None, :] // H == jnp.arange(BUCKETS, dtype=jnp.int32)[:, None]).astype(bf16)
    table_rows = jnp.dot(bucket_sums.astype(bf16), spread, preferred_element_type=f32)
    own_heads = group * heads + jnp.arange(heads, dtype=jnp.int32)
    table_row = jnp.sum(
        jnp.where(entry[None, :] % H == own_heads[:, None], table_rows, 0.0), axis=0
    )
    extra = jnp.stack(
        [jnp.zeros((model,), f32), gain_b_grad.reshape(model), table_row]
        + [jnp.zeros((model,), f32)] * 5
    )
    core_place = jnp.stack([x, c]).astype(jnp.int32)
    *rows_grads, mixed, sent_c = project_back(
        core_place, query_grads, owns, came, normed, tokens_own, columns, extra, weight_rows
    )

    by_owner = (along_dp, along_a, 2, GROUPS, weight_rows, mixed.shape[2])
    mixed, sent_c, sent = mixed.reshape(by_owner), sent_c.reshape(by_owner), rows_grads[2:]
    came_x = [swap(value, "x") for value in sent]
    came_c = swap(sent_c, "c")
    mixed = plus(mixed, came_c)
    sent_dp, mixed, came_x[0] = lax.optimization_barrier(
        (pick(mixed, 1 - dp, 0), pick(mixed, dp, 0), came_x[0])
    )
    came_dp = swap(sent_dp, "dp")
    arrived = []

    def along_column(k):
        share = plus(rows_grads[k], came_x[k])
        return [pick(share, (z + shift) % depth, 0) for shift in range(depth)]

    def turned(parts):
        return [part if shift == 0 else turn(part, shift) for shift, part in enumerate(parts)]

    *parts, came_dp = lax.optimization_barrier((*along_column(0), came_dp))
    arrived += turned(parts)
    mixed = jnp.concatenate([output_terms, plus(mixed, came_dp)], axis=4)
    sent_zh, mixed, came_x[1] = lax.optimization_barrier(
        (pick(mixed, 1 - zh, 1), pick(mixed, zh, 1), came_x[1])
    )
    came_zh = swap(sent_zh, "zh")
    *parts, came_zh = lax.optimization_barrier((*along_column(1), came_zh))
    arrived += turned(parts)
    mixed = plus(mixed, came_zh)
    if along_a > 1:
        mixed = lax.psum_scatter(mixed, "a", scatter_dimension=0, tiled=True)
    *early, terms_owned = lax.optimization_barrier((*arrived[:depth], mixed[0]))
    arrived = early + arrived[depth:]
    terms_owned = lax.all_to_all(terms_owned, ("zl", "x"), 0, 0, tiled=True)
    origins = jnp.stack([(z - shift) % depth // 2 for shift in range(depth)]).astype(jnp.int32)
    input_grad = rows_stage(origins, inputs, residual_grad, gain_a, arrived)

    if along_a == 1:
        total = pick(terms, z, 0).astype(f32)
        for arriving in column_came:
            total = total + arriving.astype(f32)
        side, deep = shape.steps * shape.side, shape.deep
        sides = jnp.concatenate([total[:side], total[side + deep : 2 * side + deep]], axis=0)
        sides = sides.astype(bf16).reshape(-1, 2, weight_rows, PANEL)
        sides = in_order(pick(sides, c, 1), swap(pick(sides, 1 - c, 1), "c"), c, 0)
        sides = sides.reshape(2, 2, shape.steps, weight_rows, PANEL)
        sides = jnp.transpose(
            sides.reshape(2, 2, shape.steps, weight_rows, PANEL // each, each), (1, 3, 2, 4, 0, 5)
        ).reshape(2, weight_rows, hidden_units)
        gate_owned, upper_owned = sides[0].astype(f32), sides[1].astype(f32)
        down_owned = jnp.transpose(
            jnp.concatenate([total[side : side + deep], total[2 * side + deep :]], axis=0).reshape(
                shape.panels, each, PANEL
            ),
            (1, 0, 2),
        ).reshape(each, model)
    else:
        side = shape.steps * model
        gate_half, upper_half = (
            jnp.transpose(
                big_grads[0][0, k * side : (k + 1) * side].reshape(shape.steps, model, PANEL),
                (1, 0, 2),
            ).reshape(model, -1, 1, each)
            for k in range(2)
        )
        down_half = jnp.transpose(
            big_grads[0][0, 2 * side :].reshape(shape.panels, -1, PANEL), (1, 0, 2)
        ).reshape(-1, 1, each, model)
        zero = jnp.zeros_like
        gate_owned, upper_owned = (
            lax.psum_scatter(
                in_order(half, zero(half), c, 2).reshape(model, hidden_units),
                everyone,
                scatter_dimension=0,
                tiled=True,
            ).astype(f32)
            for half in (gate_half, upper_half)
        )
        down_owned = lax.psum_scatter(
            in_order(down_half, zero(down_half), c, 1).reshape(hidden_units, model),
            everyone,
            scatter_dimension=0,
            tiled=True,
        ).astype(f32)

    *owned, extras = owned_stage(terms_owned, model, part)
    return (
        outputs.reshape(seqs, local_rows, model),
        input_grad,
        *owned,
        gate_owned,
        upper_owned,
        down_owned,
        extras[0, :weight_rows],
        extras[1, :weight_rows],
        extras[2, :per_owner],
    )


def solution(mesh):
    along_dp, along_ctx = mesh.shape["dp"], mesh.shape["ctx"]
    along_a = along_ctx // (4 * 2 * CORES)
    fine = Mesh(mesh.devices.reshape(along_dp, along_a, 2, 2, 2, CORES), everyone)
    rows = P("dp", ("a", "zh", "zl", "x", "c"), None)
    owned = P(everyone, None)
    vector = P(everyone)
    in_specs = (rows, *[owned] * 7, *[vector] * 3, P(), rows)
    out_specs = (rows, rows, *[owned] * 7, *[vector] * 3)
    return jax.shard_map(
        functools.partial(body, sizes=(along_dp, along_a)),
        mesh=fine,
        in_specs=in_specs,
        out_specs=out_specs,
        check_vma=False,
    )
```

time: 372 us -> 335 us (0.901)
  blocking collectives: 49.9 us -> 0 us
  Pallas kernels: 60.4 us -> 99.8 us
  local copies, waits for them, and re-layouts: 59.5 us -> 24.2 us
  starting transfers between devices: 26.3 us -> 60.3 us
  matrix products: 28.6 us -> 0.61 us
  waiting for transfers between devices: 111 us -> 118 us
  other arithmetic: 19.8 us -> 15.9 us
    ppermute x10 -> x24, waiting for transfers between devices: 19.5 us -> 79.8 us  [swap(): return lax.ppermute(value, axis, [(0, 1), (1, 0)])]
    ppermute x6 -> x12, waiting for transfers between devices: 68.3 us -> 14.9 us  [turn(): lax.ppermute(value, ('zh', 'zl'), [(i, (i + shift) % count) for i in rang...]
    all_to_all x2 -> x0, blocking collectives: 49.9 us -> none  [the longest x1 34.9 us: body(): lax.all_to_all(context_own.reshape(GROUPS * 2, local_rows, part), ('z', '...]
    pallas_call x1 -> x7, Pallas kernels: 4.39 us -> 49 us  [the longest x1 25.8 us: hidden_stage(): pl.pallas_call(functools.partial(hidden_kernel, shape), grid_spec=pltpu.P...]
    dot_general x14 -> x2, matrix products: 28.6 us -> 0.61 us  [the longest x1 0.47 us: body(): lax.dot_general(own_table, hot_ahead, (((0,), (0,)), ((), ())), preferred...]
    reshape x10, local copies, waits for them, and re-layouts: 19.3 us -> 3.6 us  [the longest x2 2.27 us: own_half(): weight.reshape(rows, cols // (2 * each), 2, each)]
    ppermute x6 -> x12, starting transfers between devices: 8.03 us -> 23.5 us  [turn(): lax.ppermute(value, ('zh', 'zl'), [(i, (i + shift) % count) for i in rang...]
    all_to_all x2 -> x4, starting transfers between devices: 9.65 us -> 22.7 us  [the longest x1 12.4 us: body(): context = lax.all_to_all(context_own, owners, 0, 0, tiled=True)]
  transfers between devices with their start and end apart: 20 -> 41, of which waited for: 11 -> 20; matrix products, arithmetic and copies ran while one was open for 10% -> 6% of each run, Pallas kernels for 16% -> 19%
where the time goes in v2:
time: 335 us; the launch traced here: 334 us
  waiting for transfers between devices  118 us (35%)
  Pallas kernels  99.8 us (30%)
  starting transfers between devices  60.3 us (18%)
  local copies, waits for them, and re-layouts  24.2 us (7%)
  other arithmetic  15.9 us (5%)
  between operations  15.3 us (5%)
    ppermute x24, waiting for transfers between devices, swap(): return lax.ppermute(value, axis, [(0, 1), (1, 0)])  79.8 us
    pallas_call x2, Pallas kernels, attend_back(): pl.pallas_call(functools.partial(attend_back_kernel, tile, chunk), grid_s...  28.2 us
    pallas_call x1, Pallas kernels, hidden_stage(): pl.pallas_call(functools.partial(hidden_kernel, shape), grid_spec=pltpu.P...  25.8 us
    ppermute x12, starting transfers between devices, turn(): lax.ppermute(value, ('zh', 'zl'), [(i, (i + shift) % count) for i in rang...  23.5 us
    all_to_all x1, waiting for transfers between devices, body(): context = lax.all_to_all(context_own, owners, 0, 0, tiled=True)  20.1 us
    pallas_call x1, Pallas kernels, attend(): pl.pallas_call(functools.partial(attend_kernel, tile, chunk), grid_spec=p...  19.9 us
    ppermute x12, waiting for transfers between devices, turn(): lax.ppermute(value, ('zh', 'zl'), [(i, (i + shift) % count) for i in rang...  14.9 us
    ppermute x24, starting transfers between devices, swap(): return lax.ppermute(value, axis, [(0, 1), (1, 0)])  14.1 us
  transfers between devices with their start and end apart: 41, of which 20 were waited for; matrix products, arithmetic and copies ran while one was open for 6% of the time, Pallas kernels for 19%

profile of v2, /device:TPU:0, one launch (start us, length us, event | category | flops | bytes accessed | tf_op | source)
XLA Modules:
  0.0 334.5 jit_solution(9517017613632417543)
XLA Ops:
  9.5 2.5 dynamic-slice_reduce_fusion.2
  15.5 3.0 collective-permute-start
  18.5 2.6 collective-permute-start.1
  21.1 1.3 collective-permute-start.2
  23.8 3.3 all-to-all-start
  27.2 11.3 %collective-permute-done.1 = bf16[128,768]{1,0:T(8,128)(2,1)S(1)} collective-permute-done((bf16[128,768]{1,0:T(8,128)(2,1)S(1)}, bf16[128,768]{1,0:T(8,128)(2,1)S(1)}, u32[]{:S(2)}, u32[]{:S(2)}) %collective-permute-start.1) | collective-permute-done | bytes 196640 | tf_op jit(solution)/shard_map/ppermute | solution.py:946
  38.5 2.3 all-to-all-done
  40.9 1.5 collective-permute-start.3
  42.4 8.7 %collective-permute-done.4 = bf16[4,24,704]{2,1,0:T(8,128)(2,1)S(1)} collective-permute-done((bf16[4,24,704]{2,1,0:T(8,128)(2,1)S(1)}, bf16[4,24,704]{2,1,0:T(8,128)(2,1)S(1)}, u32[]{:S(2)}, u32[]{:S(2)}) %collective-permute-start.4) | collective-permute-done | bytes 135200 | tf_op jit(solution)/shard_map/ppermute | solution.py:923
  51.1 1.6 collective-permute-start.5
  52.7 12.6 %collective-permute-done.5 = bf16[2,4,24,704]{3,2,1,0:T(8,128)(2,1)S(1)} collective-permute-done((bf16[2,4,24,704]{3,2,1,0:T(8,128)(2,1)S(1)}, bf16[2,4,24,704]{3,2,1,0:T(8,128)(2,1)S(1)}, u32[]{:S(2)}, u32[]{:S(2)}) %collective-permute-start.5) | collective-permute-done | bytes 270368 | tf_op jit(solution)/shard_map/ppermute | solution.py:923
  68.1 2.7 project.1
  74.6 2.0 skew.1.table
  76.6 1.6 copy-done.4
  79.1 19.9 %attend.1 = (bf16[8,192,128]{2,1,0:T(8,128)(2,1)}, bf16[3,1024,2048]{2,1,0:T(8,128)(2,1)}, f32[3,1024,128]{2,1,0:T(8,128)}, f32[3,8,1,128]{3,2,1,0:T(1,128)}) custom-call(s32[2]{0:T(128)} %pad_add_fusion.place_ref, bf16[3,1024,64]{2,1,0:T(8,128)(2,1)} %copy-done.6, bf16[3,1024,128]{2,1,0:T(8,128)(2,1)} %copy-done.7, bf16[3,1024,128]{2,1,0:T(8,128)(2,1)} %copy-done.17, ...), custom_call_target="tpu_custom_call" | custom-call | flops 6442450944 | bytes 12582912 | tf_op jit(solution)/shard_map/attend/pallas_call | solution.py:207
  99.0 12.4 %all-to-all-start.1 = ((bf16[8,192,128]{2,1,0:T(8,128)(2,1)}), bf16[8,192,128]{2,1,0:T(8,128)(2,1)S(1)}, u32[]{:S(2)}, u32[]{:S(2)}) async-start(bf16[8,192,128]{2,1,0:T(8,128)(2,1)} %get-tuple-element.99), calls=%async_computation.1 | async-start | bytes 786432 | tf_op jit(solution)/shard_map/all_to_all | solution.py:1088
  112.2 20.1 %all-to-all-done.1.context_ref = bf16[8,192,128]{2,1,0:T(8,128)(2,1)S(1)} async-done(((bf16[8,192,128]{2,1,0:T(8,128)(2,1)}), bf16[8,192,128]{2,1,0:T(8,128)(2,1)S(1)}, u32[]{:S(2)}, u32[]{:S(2)}) %all-to-all-start.1) | async-done | bytes 393248 | tf_op jit(solution)/shard_map/all_to_all | solution.py:1088
  133.3 3.2 output_stage.1
  137.0 1.3 collective-permute-done.9.normed_other
  139.1 25.8 %hidden_stage.1 = (f32[256,768]{1,0:T(8,128)}, bf16[256,768]{1,0:T(8,128)(2,1)}, f32[256,768]{1,0:T(8,128)}, bf16[256,768]{1,0:T(8,128)(2,1)}, bf16[8,256,256]{2...) custom-call(s32[2]{0:T(128)} %pad_add_fusion.1.place_ref, ...), custom_call_target="tpu_custom_call" | custom-call | flops 7247757312 | bytes 9437184 | tf_op jit(solution)/shard_map/hidden_stage/pallas_call | solution.py:788
  165.0 1.5 collective-permute-start.13
  167.9 4.8 %output_back.1 = (f32[256,768]{1,0:T(8,128)}, f32[1,768]{1,0:T(1,128)}, bf16[8,192,128]{2,1,0:T(8,128)(2,1)}, bf16[768,768]{1,0:T(8,128)(2,1)}) custom-call(f32[256,768]{1,0:T(8,128)} %get-tuple-element.104.norm_own, bf16[256,768]{1,0:T(8,128)(2,1)} %copy-done.24, f32[256,768]{1,0:T(8,128)} %get-tuple-element.100.residual_ref, bf16[256,768]{1,0:T(8,128)(2,1)} %bitcast.179, ...), custom_call_target="tpu_custom_call" | custom-call | flops 603979776 | bytes 2359296 | tf_op jit(solution)/shard_map/output_back/pallas_call | solution.py:872
  172.8 3.5 %all-to-all-start.2 = ((bf16[8,192,128]{2,1,0:T(8,128)(2,1)}), bf16[8,192,128]{2,1,0:T(8,128)(2,1)S(1)}, u32[]{:S(2)}, u32[]{:S(2)}) async-start(bf16[8,192,128]{2,1,0:T(8,128)(2,1)} %get-tuple-element.110), calls=%async_computation.2 | async-start | bytes 786432 | tf_op jit(solution)/shard_map/all_to_all | solution.py:1104
  177.5 2.8 fusion.hot_ref
  182.2 12.3 %collective-permute-done.13 = bf16[8,256,256]{2,1,0:T(8,128)(2,1)} collective-permute-done((bf16[8,256,256]{2,1,0:T(8,128)(2,1)}, bf16[8,256,256]{2,1,0:T(8,128)(2,1)}, u32[]{:S(2)}, u32[]{:S(2)}) %collective-permute-start.13) | collective-permute-done | bytes 1048608 | tf_op jit(solution)/shard_map/ppermute | solution.py:923
  194.9 2.6 collective-permute-done.14
  198.6 1.9 add_convert_fusion.1
  203.5 1.5 collective-permute-start.16
  205.6 10.7 %attend_back.2 = (bf16[1,1024,64]{2,1,0:T(8,128)(2,1)}, f32[1,128,1024]{2,1,0:T(8,128)}, bf16[1,128,1024]{2,1,0:T(8,128)(2,1)}, f32[1,1,128]{2,1,0:T(1,128)}) custom-call(s32[2]{0:T(128)} %pad_add_fusion.place_ref, bf16[8,192,128]{2,1,0:T(8,128)(2,1)} %copy-done.12, f32[3,1024,128]{2,1,0:T(8,128)} %get-tuple-element.122.kept_ref, ...), custom_call_target="tpu_custom_call" | custom-call | flops 4294967296 | bytes 4194304 | tf_op jit(solution)/shard_map/attend_back/pallas_call | solution.py:343
  216.3 6.5 %collective-permute-done.18 = bf16[1,2,4,24,768]{4,3,2,1,0:T(8,128)(2,1)S(1)} collective-permute-done((bf16[1,2,4,24,768]{4,3,2,1,0:T(8,128)(2,1)S(1)}, bf16[1,2,4,24,768]{4,3,2,1,0:T(8,128)(2,1)S(1)}, u32[]{:S(2)}, u32[]{:S(2)}) %collective-permute-start.18) | collective-permute-done | bytes 294944 | tf_op jit(solution)/shard_map/ppermute | solution.py:923
  224.6 2.0 collective-permute-start.20
  226.5 1.9 collective-permute-start.21
  228.4 17.5 %attend_back.3 = (bf16[2,1024,64]{2,1,0:T(8,128)(2,1)}, f32[2,128,1024]{2,1,0:T(8,128)}, bf16[2,128,1024]{2,1,0:T(8,128)(2,1)}, f32[2,1,128]{2,1,0:T(1,128)}) custom-call(s32[2]{0:T(128)} %pad_add_fusion.place_ref, bf16[8,192,128]{2,1,0:T(8,128)(2,1)} %copy-done.12, f32[3,1024,128]{2,1,0:T(8,128)} %get-tuple-element.122.kept_ref, ...), custom_call_target="tpu_custom_call" | custom-call | flops 8589934592 | bytes 8388608 | tf_op jit(solution)/shard_map/attend_back/pallas_call | solution.py:343
  247.1 1.9 add_convert_fusion.4
  249.9 10.4 %project_back.1 = (bf16[4,128,384]{2,1,0:T(8,128)(2,1)}, bf16[4,128,384]{2,1,0:T(8,128)(2,1)}, bf16[4,128,384]{2,1,0:T(8,128)(2,1)}, bf16[4,128,384]{2,1,0:T(8,1...) custom-call(s32[2]{0:T(128)} %pad_add_fusion.3.place_ref, bf16[1024,768]{1,0:T(8,128)(2,1)} %copy-done.5, ...), custom_call_target="tpu_custom_call" | custom-call | flops 1811939328 | bytes 9437184 | tf_op jit(solution)/shard_map/project_back/pallas_call | solution.py:475
  261.3 1.5 collective-permute-start.25
  263.8 9.5 %collective-permute-done.25 = bf16[4,128,384]{2,1,0:T(8,128)(2,1)S(1)} collective-permute-done((bf16[4,128,384]{2,1,0:T(8,128)(2,1)S(1)}, bf16[4,128,384]{2,1,0:T(8,128)(2,1)S(1)}, u32[]{:S(2)}, u32[]{:S(2)}) %collective-permute-start.25) | collective-permute-done | bytes 393248 | tf_op jit(solution)/shard_map/ppermute | solution.py:923
  273.2 1.5 collective-permute-start.26
  274.9 6.5 %collective-permute-done.26 = bf16[1,2,4,24,704]{4,3,2,1,0:T(8,128)(2,1)S(1)} collective-permute-done((bf16[1,2,4,24,704]{4,3,2,1,0:T(8,128)(2,1)S(1)}, bf16[1,2,4,24,704]{4,3,2,1,0:T(8,128)(2,1)S(1)}, u32[]{:S(2)}, u32[]{:S(2)}) %collective-permute-start.26) | collective-permute-done | bytes 270368 | tf_op jit(solution)/shard_map/ppermute | solution.py:923
  281.4 5.8 %collective-permute-start.27 = (bf16[128,384]{1,0:T(8,128)(2,1)S(1)}, bf16[128,384]{1,0:T(8,128)(2,1)S(1)}, u32[]{:S(2)}, u32[]{:S(2)}) collective-permute-start(bf16[128,384]{1,0:T(8,128)(2,1)S(1)} %get-tuple-element.153), channel_id=1, source_target_pairs={{0,4},{4,8},{8,12},{12,0},{1,5},{5,9},{9,13},{13,1},{2,6},{6,10},{... | collective-permute-start | bytes 294920 | tf_op jit(solution)/shard_map/ppermute | solution.py:946
  287.2 2.4 collective-permute-start.29
  290.5 17.1 %collective-permute-done.31 = bf16[1,4,24,1472]{3,2,1,0:T(8,128)(2,1)S(1)} collective-permute-done((bf16[1,4,24,1472]{3,2,1,0:T(8,128)(2,1)S(1)}, bf16[1,4,24,1472]{3,2,1,0:T(8,128)(2,1)S(1)}, u32[]{:S(2)}, u32[]{:S(2)}) %collective-permute-start.31) | collective-permute-done | bytes 282656 | tf_op jit(solution)/shard_map/ppermute | solution.py:923
  308.4 3.5 %all-to-all-start.3 = ((bf16[4,24,1472]{2,1,0:T(8,128)(2,1)}), bf16[4,24,1472]{2,1,0:T(8,128)(2,1)S(1)}, u32[]{:S(2)}, u32[]{:S(2)}) async-start(bf16[4,24,1472]{2,1,0:T(8,128)(2,1)} %fusion.13), calls=%async_computation.3 | async-start | bytes 589824 | tf_op jit(solution)/shard_map/all_to_all | solution.py:1229
  313.1 2.0 collective-permute-start.32
  315.1 1.6 collective-permute-start.33
  320.3 1.6 collective-permute-done.32.refs_5_
  321.9 1.9 collective-permute-done.33.refs_6_
  323.7 2.0 rows_stage.1
  (239 shorter events, 41.0 us)
Async XLA Ops:
  7.2 126.1 %all-gather.2.cloned.1.call-start = ((), (), s32[]{:S(2)}) async-start(), calls=%async_computation.4 | async-start | bytes 6266880 | tf_op jit(solution)/shard_map/all_gather | solution.py:1055
  12.6 1.5 collective-permute-start.8
  15.5 11.7 %collective-permute-start = (bf16[128,768]{1,0:T(8,128)(2,1)S(1)}, bf16[128,768]{1,0:T(8,128)(2,1)S(1)}, u32[]{:S(2)}, u32[]{:S(2)}) collective-permute-start(bf16[128,768]{1,0:T(8,128)(2,1)S(1)} %get-tuple-element.209), channel_id=1, source_target_pairs={{0,4},{4,8},{8,12},{12,0},{1,5},{5,9},{9,13},{13,1},{2,6},{6,10},{... | collective-permute-start | bytes 589832 | tf_op jit(solution)/shard_map/ppermute | solution.py:946
  18.5 20.0 %collective-permute-start.1 = (bf16[128,768]{1,0:T(8,128)(2,1)S(1)}, bf16[128,768]{1,0:T(8,128)(2,1)S(1)}, u32[]{:S(2)}, u32[]{:S(2)}) collective-permute-start(bf16[128,768]{1,0:T(8,128)(2,1)S(1)} %get-tuple-element.208), channel_id=1, source_target_pairs={{0,8},{4,12},{8,0},{12,4},{1,9},{5,13},{9,1},{13,5},{2,10},{6,14},... | collective-permute-start | bytes 589832 | tf_op jit(solution)/shard_map/ppermute | solution.py:946
  21.1 19.8 %collective-permute-start.2 = (bf16[128,768]{1,0:T(8,128)(2,1)S(1)}, bf16[128,768]{1,0:T(8,128)(2,1)S(1)}, u32[]{:S(2)}, u32[]{:S(2)}) collective-permute-start(bf16[128,768]{1,0:T(8,128)(2,1)S(1)} %get-tuple-element.207), channel_id=1, source_target_pairs={{0,12},{4,0},{8,4},{12,8},{1,13},{5,1},{9,5},{13,9},{2,14},{6,2},{... | collective-permute-start | bytes 589832 | tf_op jit(solution)/shard_map/ppermute | solution.py:946
  23.8 17.1 %all-to-all-start = ((bf16[4,24,704]{2,1,0:T(8,128)(2,1)}), bf16[4,24,704]{2,1,0:T(8,128)(2,1)S(1)}, u32[]{:S(2)}, u32[]{:S(2)}) async-start(bf16[4,24,704]{2,1,0:T(8,128)(2,1)} %pad_maximum_fusion.6), calls=%async_computation | async-start | bytes 294912 | tf_op jit(solution)/shard_map/all_to_all | solution.py:1018
  40.9 10.2 %collective-permute-start.4 = (bf16[4,24,704]{2,1,0:T(8,128)(2,1)S(1)}, bf16[4,24,704]{2,1,0:T(8,128)(2,1)S(1)}, u32[]{:S(2)}, u32[]{:S(2)}) collective-permute-start(bf16[4,24,704]{2,1,0:T(8,128)(2,1)S(1)} %all-to-all-done), channel_id=1, source_target_pairs={{0,8},{8,0},{1,9},{9,1},{2,10},{10,2},{3,11},{11,3},{4,12},{12,4},... | collective-permute-start | bytes 405512 | tf_op jit(solution)/shard_map/ppermute | solution.py:923
  40.9 25.3 %collective-permute-start.3 = (bf16[4,128,768]{2,1,0:T(8,128)(2,1)S(1)}, bf16[4,128,768]{2,1,0:T(8,128)(2,1)S(1)}, u32[]{:S(2)}, u32[]{:S(2)}) collective-permute-start(bf16[4,128,768]{2,1,0:T(8,128)(2,1)S(1)} %bitcast_dynamic-update-slice_fusion), channel_id=1, source_target_pairs={{0,2},{2,0},{1,3},{3,1},{4,6},{6,4},{5,7},{7,5},{8,10},{10,8},{9,1... | collective-permute-start | bytes 2359304 | tf_op jit(solution)/shard_map/ppermute | solution.py:923
  51.1 14.3 %collective-permute-start.5 = (bf16[2,4,24,704]{3,2,1,0:T(8,128)(2,1)S(1)}, bf16[2,4,24,704]{3,2,1,0:T(8,128)(2,1)S(1)}, u32[]{:S(2)}, u32[]{:S(2)}) collective-permute-start(bf16[2,4,24,704]{3,2,1,0:T(8,128)(2,1)S(1)} %maximum_select_fusion.5), channel_id=1, source_target_pairs={{0,16},{16,0},{1,17},{17,1},{2,18},{18,2},{3,19},{19,3},{4,20},{20... | collective-permute-start | bytes 811016 | tf_op jit(solution)/shard_map/ppermute | solution.py:923
  65.5 2.1 collective-permute-start.6
  72.9 5.4 %collective-permute-start.7 = (bf16[3,1024,128]{2,1,0:T(8,128)(2,1)S(1)}, bf16[3,1024,128]{2,1,0:T(8,128)(2,1)S(1)}, u32[]{:S(2)}, u32[]{:S(2)}) collective-permute-start(bf16[3,1024,128]{2,1,0:T(8,128)(2,1)S(1)} %get-tuple-element.98.pair_own), channel_id=1, source_target_pairs={{0,1},{1,0},{2,3},{3,2},{4,5},{5,4},{6,7},{7,6},{8,9},{9,8},{10,11... | collective-permute-start | bytes 2359304 | tf_op jit(solution)/shard_map/ppermute | solution.py:923
  79.1 32.3 %copy-start.11 = (bf16[2,128,768]{2,1,0:T(8,128)(2,1)S(1)}, bf16[2,128,768]{2,1,0:T(8,128)(2,1)}, u32[]{:S(2)}) copy-start(bf16[2,128,768]{2,1,0:T(8,128)(2,1)} %param.25) | copy-start | bytes 1179652
  99.0 33.3 %all-to-all-start.1 = ((bf16[8,192,128]{2,1,0:T(8,128)(2,1)}), bf16[8,192,128]{2,1,0:T(8,128)(2,1)S(1)}, u32[]{:S(2)}, u32[]{:S(2)}) async-start(bf16[8,192,128]{2,1,0:T(8,128)(2,1)} %get-tuple-element.99), calls=%async_computation.1 | async-start | bytes 786432 | tf_op jit(solution)/shard_map/all_to_all | solution.py:1088
  111.4 25.6 %collective-permute-start.10 = (bf16[256,768]{1,0:T(8,128)(2,1)S(1)}, bf16[256,768]{1,0:T(8,128)(2,1)S(1)}, u32[]{:S(2)}, u32[]{:S(2)}) collective-permute-start(bf16[256,768]{1,0:T(8,128)(2,1)S(1)} %bitcast.180), channel_id=1, source_target_pairs={{0,1},{1,0},{2,3},{3,2},{4,5},{5,4},{6,7},{7,6},{8,9},{9,8},{10,11... | collective-permute-start | bytes 1179656 | tf_op jit(solution)/shard_map/ppermute | solution.py:923
  136.4 1.9 collective-permute-start.9
  164.9 2.3 collective-permute-start.12
  165.0 29.4 %collective-permute-start.13 = (bf16[8,256,256]{2,1,0:T(8,128)(2,1)}, bf16[8,256,256]{2,1,0:T(8,128)(2,1)}, u32[]{:S(2)}, u32[]{:S(2)}) collective-permute-start(bf16[8,256,256]{2,1,0:T(8,128)(2,1)} %get-tuple-element.111), channel_id=1, source_target_pairs={{0,2},{2,0},{1,3},{3,1},{4,6},{6,4},{5,7},{7,5},{8,10},{10,8},{9,1... | collective-permute-start | bytes 3145736 | tf_op jit(solution)/shard_map/ppermute | solution.py:923
  166.5 31.0 %collective-permute-start.14 = (bf16[8,320,256]{2,1,0:T(8,128)(2,1)}, bf16[8,320,256]{2,1,0:T(8,128)(2,1)S(1)}, u32[]{:S(2)}, u32[]{:S(2)}) collective-permute-start(bf16[8,320,256]{2,1,0:T(8,128)(2,1)} %get-tuple-element.112), channel_id=1, source_target_pairs={{0,16},{16,0},{1,17},{17,1},{2,18},{18,2},{3,19},{19,3},{4,20},{20... | collective-permute-start | bytes 3932168 | tf_op jit(solution)/shard_map/ppermute | solution.py:923
  172.8 22.1 %all-to-all-start.2 = ((bf16[8,192,128]{2,1,0:T(8,128)(2,1)}), bf16[8,192,128]{2,1,0:T(8,128)(2,1)S(1)}, u32[]{:S(2)}, u32[]{:S(2)}) async-start(bf16[8,192,128]{2,1,0:T(8,128)(2,1)} %get-tuple-element.110), calls=%async_computation.2 | async-start | bytes 786432 | tf_op jit(solution)/shard_map/all_to_all | solution.py:1104
  177.5 3.4 %collective-permute-start.15 = (bf16[2,1,2,4,24,768]{5,4,3,2,1,0:T(8,128)(2,1)S(1)}, bf16[2,1,2,4,24,768]{5,4,3,2,1,0:T(8,128)(2,1)}, u32[]{:S(2)}, u32[]{:S(2)}) collective-permute-start(bf16[2,1,2,4,24,768]{5,4,3,2,1,0:T(8,128)(2,1)S(1)} %dynamic-slice_bitcast_fusion.1), channel_id=1, source_target_pairs={{0,1},{1,0},{2,3},{3,2},{4,5},{5,4},{6,7},{7,6},{8,9},{9,8},{10,11... | collective-permute-start | bytes 1769480 | tf_op jit(solution)/shard_map/ppermute | solution.py:923
  202.2 20.7 %collective-permute-start.17 = (bf16[4,320,256]{2,1,0:T(8,128)(2,1)}, bf16[4,320,256]{2,1,0:T(8,128)(2,1)}, u32[]{:S(2)}, u32[]{:S(2)}) collective-permute-start(bf16[4,320,256]{2,1,0:T(8,128)(2,1)} %dynamic-slice_bitcast_fusion), channel_id=1, source_target_pairs={{0,2},{2,0},{1,3},{3,1},{4,6},{6,4},{5,7},{7,5},{8,10},{10,8},{9,1... | collective-permute-start | bytes 1966088 | tf_op jit(solution)/shard_map/ppermute | solution.py:923
  203.5 19.3 %collective-permute-start.16 = (bf16[4,256,256]{2,1,0:T(8,128)(2,1)}, bf16[4,256,256]{2,1,0:T(8,128)(2,1)S(1)}, u32[]{:S(2)}, u32[]{:S(2)}) collective-permute-start(bf16[4,256,256]{2,1,0:T(8,128)(2,1)} %dynamic-slice_bitcast_fusion.2), channel_id=1, source_target_pairs={{0,16},{16,0},{1,17},{17,1},{2,18},{18,2},{3,19},{19,3},{4,20},{20... | collective-permute-start | bytes 1572872 | tf_op jit(solution)/shard_map/ppermute | solution.py:923
  205.0 42.1 %collective-permute-start.11 = (bf16[256,768]{1,0:T(8,128)(2,1)}, bf16[256,768]{1,0:T(8,128)(2,1)}, u32[]{:S(2)}, u32[]{:S(2)}) collective-permute-start(bf16[256,768]{1,0:T(8,128)(2,1)} %get-tuple-element.103), channel_id=1, source_target_pairs={{0,1},{1,0},{2,3},{3,2},{4,5},{5,4},{6,7},{7,6},{8,9},{9,8},{10,11... | collective-permute-start | bytes 1179656 | tf_op jit(solution)/shard_map/ppermute | solution.py:923
  205.0 17.8 %collective-permute-start.18 = (bf16[1,2,4,24,768]{4,3,2,1,0:T(8,128)(2,1)S(1)}, bf16[1,2,4,24,768]{4,3,2,1,0:T(8,128)(2,1)S(1)}, u32[]{:S(2)}, u32[]{:S(2)}) collective-permute-start(bf16[1,2,4,24,768]{4,3,2,1,0:T(8,128)(2,1)S(1)} %dynamic-slice_bitcast_fusion.8), channel_id=1, source_target_pairs={{0,16},{16,0},{1,17},{17,1},{2,18},{18,2},{3,19},{19,3},{4,20},{20... | collective-permute-start | bytes 884744 | tf_op jit(solution)/shard_map/ppermute | solution.py:923
  224.5 21.5 %collective-permute-start.19 = (bf16[576,256]{1,0:T(8,128)(2,1)S(1)}, bf16[576,256]{1,0:T(8,128)(2,1)S(1)}, u32[]{:S(2)}, u32[]{:S(2)}) collective-permute-start(bf16[576,256]{1,0:T(8,128)(2,1)S(1)} %get-tuple-element.192), channel_id=1, source_target_pairs={{0,4},{4,8},{8,12},{12,0},{1,5},{5,9},{9,13},{13,1},{2,6},{6,10},{... | collective-permute-start | bytes 884744 | tf_op jit(solution)/shard_map/ppermute | solution.py:946
  224.6 21.6 %collective-permute-start.20 = (bf16[576,256]{1,0:T(8,128)(2,1)S(1)}, bf16[576,256]{1,0:T(8,128)(2,1)S(1)}, u32[]{:S(2)}, u32[]{:S(2)}) collective-permute-start(bf16[576,256]{1,0:T(8,128)(2,1)S(1)} %get-tuple-element.191), channel_id=1, source_target_pairs={{0,8},{4,12},{8,0},{12,4},{1,9},{5,13},{9,1},{13,5},{2,10},{6,14},... | collective-permute-start | bytes 884744 | tf_op jit(solution)/shard_map/ppermute | solution.py:946
  226.5 20.6 %copy-start.10 = (f32[256,768]{1,0:T(8,128)S(1)}, f32[256,768]{1,0:T(8,128)}, u32[]{:S(2)}) copy-start(f32[256,768]{1,0:T(8,128)} %get-tuple-element.100.residual_ref) | copy-start | bytes 2359300
  226.5 20.6 %copy-start.18 = (f32[256,768]{1,0:T(8,128)S(1)}, f32[256,768]{1,0:T(8,128)}, u32[]{:S(2)}) copy-start(f32[256,768]{1,0:T(8,128)} %get-tuple-element.102) | copy-start | bytes 2359300
  226.5 19.6 %collective-permute-start.21 = (bf16[576,256]{1,0:T(8,128)(2,1)S(1)}, bf16[576,256]{1,0:T(8,128)(2,1)S(1)}, u32[]{:S(2)}, u32[]{:S(2)}) collective-permute-start(bf16[576,256]{1,0:T(8,128)(2,1)S(1)} %get-tuple-element.190), channel_id=1, source_target_pairs={{0,12},{4,0},{8,4},{12,8},{1,13},{5,1},{9,5},{13,9},{2,14},{6,2},{... | collective-permute-start | bytes 884744 | tf_op jit(solution)/shard_map/ppermute | solution.py:946
  246.1 3.7 %collective-permute-start.23 = (bf16[2,128,1024]{2,1,0:T(8,128)(2,1)}, bf16[2,128,1024]{2,1,0:T(8,128)(2,1)}, u32[]{:S(2)}, u32[]{:S(2)}) collective-permute-start(bf16[2,128,1024]{2,1,0:T(8,128)(2,1)} %get-tuple-element.145), channel_id=1, source_target_pairs={{0,1},{1,0},{2,3},{3,2},{4,5},{5,4},{6,7},{7,6},{8,9},{9,8},{10,11... | collective-permute-start | bytes 1572872 | tf_op jit(solution)/shard_map/ppermute | solution.py:923
  247.1 2.8 collective-permute-start.22
  249.9 11.0 %copy-start.26 = (bf16[576,256]{1,0:T(8,128)(2,1)S(1)}, bf16[576,256]{1,0:T(8,128)(2,1)}, u32[]{:S(2)}) copy-start(bf16[576,256]{1,0:T(8,128)(2,1)} %copy-done.25) | copy-start | bytes 884740
  249.9 11.0 %copy-start.28 = (bf16[576,256]{1,0:T(8,128)(2,1)S(1)}, bf16[576,256]{1,0:T(8,128)(2,1)}, u32[]{:S(2)}) copy-start(bf16[576,256]{1,0:T(8,128)(2,1)} %copy-done.27) | copy-start | bytes 884740
  260.3 3.2 collective-permute-start.24
  261.2 51.6 %collective-permute-start.35 = (bf16[8,24,256]{2,1,0:T(8,128)(2,1)S(1)}, bf16[8,24,256]{2,1,0:T(8,128)(2,1)S(1)}, u32[]{:S(2)}, u32[]{:S(2)}) collective-permute-start(bf16[8,24,256]{2,1,0:T(8,128)(2,1)S(1)} %get-tuple-element.214), channel_id=1, source_target_pairs={{0,1},{1,0},{2,3},{3,2},{4,5},{5,4},{6,7},{7,6},{8,9},{9,8},{10,11... | collective-permute-start | bytes 294920 | tf_op jit(solution)/shard_map/ppermute | solution.py:923
  261.3 11.9 %collective-permute-start.25 = (bf16[4,128,384]{2,1,0:T(8,128)(2,1)S(1)}, bf16[4,128,384]{2,1,0:T(8,128)(2,1)S(1)}, u32[]{:S(2)}, u32[]{:S(2)}) collective-permute-start(bf16[4,128,384]{2,1,0:T(8,128)(2,1)S(1)} %copy-done.40), channel_id=1, source_target_pairs={{0,2},{2,0},{1,3},{3,1},{4,6},{6,4},{5,7},{7,5},{8,10},{10,8},{9,1... | collective-permute-start | bytes 1179656 | tf_op jit(solution)/shard_map/ppermute | solution.py:923
  262.8 26.9 %collective-permute-start.30 = (bf16[4,128,384]{2,1,0:T(8,128)(2,1)S(1)}, bf16[4,128,384]{2,1,0:T(8,128)(2,1)S(1)}, u32[]{:S(2)}, u32[]{:S(2)}) collective-permute-start(bf16[4,128,384]{2,1,0:T(8,128)(2,1)S(1)} %copy-done.39), channel_id=1, source_target_pairs={{0,2},{2,0},{1,3},{3,1},{4,6},{6,4},{5,7},{7,5},{8,10},{10,8},{9,1... | collective-permute-start | bytes 1179656 | tf_op jit(solution)/shard_map/ppermute | solution.py:923
  263.5 11.1 %copy-start.23 = (bf16[4,128,384]{2,1,0:T(8,128)(2,1)S(1)}, bf16[4,128,384]{2,1,0:T(8,128)(2,1)}, u32[]{:S(2)}) copy-start(bf16[4,128,384]{2,1,0:T(8,128)(2,1)} %get-tuple-element.146) | copy-start | bytes 1179652
  273.2 8.2 %collective-permute-start.26 = (bf16[1,2,4,24,704]{4,3,2,1,0:T(8,128)(2,1)S(1)}, bf16[1,2,4,24,704]{4,3,2,1,0:T(8,128)(2,1)S(1)}, u32[]{:S(2)}, u32[]{:S(2)}) collective-permute-start(bf16[1,2,4,24,704]{4,3,2,1,0:T(8,128)(2,1)S(1)} %get-tuple-element.151), channel_id=1, source_target_pairs={{0,16},{16,0},{1,17},{17,1},{2,18},{18,2},{3,19},{19,3},{4,20},{20... | collective-permute-start | bytes 811016 | tf_op jit(solution)/shard_map/ppermute | solution.py:923
  274.8 15.5 %copy-start.22 = (bf16[4,128,384]{2,1,0:T(8,128)(2,1)S(1)}, bf16[4,128,384]{2,1,0:T(8,128)(2,1)}, u32[]{:S(2)}) copy-start(bf16[4,128,384]{2,1,0:T(8,128)(2,1)} %get-tuple-element.161) | copy-start | bytes 1179652
  281.4 27.0 %collective-permute-start.27 = (bf16[128,384]{1,0:T(8,128)(2,1)S(1)}, bf16[128,384]{1,0:T(8,128)(2,1)S(1)}, u32[]{:S(2)}, u32[]{:S(2)}) collective-permute-start(bf16[128,384]{1,0:T(8,128)(2,1)S(1)} %get-tuple-element.153), channel_id=1, source_target_pairs={{0,4},{4,8},{8,12},{12,0},{1,5},{5,9},{9,13},{13,1},{2,6},{6,10},{... | collective-permute-start | bytes 294920 | tf_op jit(solution)/shard_map/ppermute | solution.py:946
  287.1 21.3 %collective-permute-start.28 = (bf16[128,384]{1,0:T(8,128)(2,1)S(1)}, bf16[128,384]{1,0:T(8,128)(2,1)S(1)}, u32[]{:S(2)}, u32[]{:S(2)}) collective-permute-start(bf16[128,384]{1,0:T(8,128)(2,1)S(1)} %get-tuple-element.154), channel_id=1, source_target_pairs={{0,8},{4,12},{8,0},{12,4},{1,9},{5,13},{9,1},{13,5},{2,10},{6,14},... | collective-permute-start | bytes 294920 | tf_op jit(solution)/shard_map/ppermute | solution.py:946
  287.2 21.3 %collective-permute-start.29 = (bf16[128,384]{1,0:T(8,128)(2,1)S(1)}, bf16[128,384]{1,0:T(8,128)(2,1)S(1)}, u32[]{:S(2)}, u32[]{:S(2)}) collective-permute-start(bf16[128,384]{1,0:T(8,128)(2,1)S(1)} %get-tuple-element.155), channel_id=1, source_target_pairs={{0,12},{4,0},{8,4},{12,8},{1,13},{5,1},{9,5},{13,9},{2,14},{6,2},{... | collective-permute-start | bytes 294920 | tf_op jit(solution)/shard_map/ppermute | solution.py:946
  289.7 17.9 %collective-permute-start.31 = (bf16[1,4,24,1472]{3,2,1,0:T(8,128)(2,1)S(1)}, bf16[1,4,24,1472]{3,2,1,0:T(8,128)(2,1)S(1)}, u32[]{:S(2)}, u32[]{:S(2)}) collective-permute-start(bf16[1,4,24,1472]{3,2,1,0:T(8,128)(2,1)S(1)} %get-tuple-element.163), channel_id=1, source_target_pairs={{0,8},{8,0},{1,9},{9,1},{2,10},{10,2},{3,11},{11,3},{4,12},{12,4},... | collective-permute-start | bytes 847880 | tf_op jit(solution)/shard_map/ppermute | solution.py:923
  308.4 17.4 %all-to-all-start.3 = ((bf16[4,24,1472]{2,1,0:T(8,128)(2,1)}), bf16[4,24,1472]{2,1,0:T(8,128)(2,1)S(1)}, u32[]{:S(2)}, u32[]{:S(2)}) async-start(bf16[4,24,1472]{2,1,0:T(8,128)(2,1)} %fusion.13), calls=%async_computation.3 | async-start | bytes 589824 | tf_op jit(solution)/shard_map/all_to_all | solution.py:1229
  313.1 8.8 %collective-permute-start.32 = (bf16[128,384]{1,0:T(8,128)(2,1)S(1)}, bf16[128,384]{1,0:T(8,128)(2,1)S(1)}, u32[]{:S(2)}, u32[]{:S(2)}) collective-permute-start(bf16[128,384]{1,0:T(8,128)(2,1)S(1)} %get-tuple-element.170), channel_id=1, source_target_pairs={{0,4},{4,8},{8,12},{12,0},{1,5},{5,9},{9,13},{13,1},{2,6},{6,10},{... | collective-permute-start | bytes 294920 | tf_op jit(solution)/shard_map/ppermute | solution.py:946
  315.1 8.6 %collective-permute-start.33 = (bf16[128,384]{1,0:T(8,128)(2,1)S(1)}, bf16[128,384]{1,0:T(8,128)(2,1)S(1)}, u32[]{:S(2)}, u32[]{:S(2)}) collective-permute-start(bf16[128,384]{1,0:T(8,128)(2,1)S(1)} %get-tuple-element.171), channel_id=1, source_target_pairs={{0,8},{4,12},{8,0},{12,4},{1,9},{5,13},{9,1},{13,5},{2,10},{6,14},... | collective-permute-start | bytes 294920 | tf_op jit(solution)/shard_map/ppermute | solution.py:946
  316.8 7.0 %collective-permute-start.34 = (bf16[128,384]{1,0:T(8,128)(2,1)S(1)}, bf16[128,384]{1,0:T(8,128)(2,1)S(1)}, u32[]{:S(2)}, u32[]{:S(2)}) collective-permute-start(bf16[128,384]{1,0:T(8,128)(2,1)S(1)} %get-tuple-element.172), channel_id=1, source_target_pairs={{0,12},{4,0},{8,4},{12,8},{1,13},{5,1},{9,5},{13,9},{2,14},{6,2},{... | collective-permute-start | bytes 294920 | tf_op jit(solution)/shard_map/ppermute | solution.py:946
  (36 other events, 125.1 us)
Sparse Core Ops, SparseCore 0:
  15.3 117.9 all-gather.1

commit v3 on v2

--- a/solution.py
+++ b/solution.py
@@ -329,17 +329,17 @@
                 near = pl.multiple_of((2 * b + parity) * BLOCK, BLOCK)
                 far = pl.multiple_of((2 * b + 1 - parity) * BLOCK, BLOCK)
                 lanes = slice(b * BLOCK, (b + 1) * BLOCK)
-                own_grad_ref[0, rows, lanes] = sums[:, pl.ds(near, BLOCK)]
+                own_grad_ref[0, rows, lanes] = sums[:, pl.ds(near, BLOCK)].astype(bf16)
                 other_grad_ref[0, rows, lanes] = sums[:, pl.ds(far, BLOCK)].astype(bf16)
 
 
-def attend_back(place, grad, kept, inverse, probs, query, own, other, hot, first, count):
-    unused, rows, width = query.shape
+def attend_back(place, grad, kept, inverse, probs, query, own, other, hot):
+    count, rows, width = query.shape
     own_rows = own.shape[1]
     key_count = 2 * own_rows
     span = key_count * 2
     tile, chunk = 512, 512
-    pairs = pl.BlockSpec((1, own_rows, 2 * width), lambda h, i, s: (h + first, 0, 0))
+    pairs = pl.BlockSpec((1, own_rows, 2 * width), lambda h, i, s: (h, 0, 0))
     return pl.pallas_call(
         functools.partial(attend_back_kernel, tile, chunk),
         grid_spec=pltpu.PrefetchScalarGridSpec(
@@ -347,12 +347,12 @@
             grid=(count, rows // tile),
             in_specs=[
                 pl.BlockSpec(
-                    (tile // BLOCK, width, BLOCK), lambda h, i, s: (i, h + first, 0)
+                    (tile // BLOCK, width, BLOCK), lambda h, i, s: (i, h, 0)
                 ),
-                pl.BlockSpec((1, tile, 2 * width), lambda h, i, s: (h + first, i, 0)),
-                pl.BlockSpec((1, tile // BLOCK, 1, BLOCK), lambda h, i, s: (h + first, i, 0, 0)),
-                pl.BlockSpec((1, tile, key_count), lambda h, i, s: (h + first, i, 0)),
-                pl.BlockSpec((1, tile, width), lambda h, i, s: (h + first, i, 0)),
+                pl.BlockSpec((1, tile, 2 * width), lambda h, i, s: (h, i, 0)),
+                pl.BlockSpec((1, tile // BLOCK, 1, BLOCK), lambda h, i, s: (h, i, 0, 0)),
+                pl.BlockSpec((1, tile, key_count), lambda h, i, s: (h, i, 0)),
+                pl.BlockSpec((1, tile, width), lambda h, i, s: (h, i, 0)),
                 pairs,
                 pairs,
                 pl.BlockSpec(hot.shape, lambda h, i, s: (0, 0)),
@@ -373,7 +373,7 @@
         ),
         out_shape=[
             jax.ShapeDtypeStruct((count, rows, width), bf16),
-            jax.ShapeDtypeStruct((count, 2 * width, own_rows), f32),
+            jax.ShapeDtypeStruct((count, 2 * width, own_rows), bf16),
             jax.ShapeDtypeStruct((count, 2 * width, own_rows), bf16),
             jax.ShapeDtypeStruct((count, 1, hot.shape[1]), f32),
         ],
@@ -387,27 +387,31 @@
     )(place, grad, kept, inverse, probs, query, own, other, hot)
 
 
-def project_back_kernel(splits, place_ref, normed_ref, token_ref, weight_ref, *refs):
-    extra_ref, given = refs[0], refs[1:-9]
-    rows_refs, kept_ref, sent_ref, turned, sums, gains = (*[refs[-9:-5]], *refs[-5:])
+def project_back_kernel(
+    place_ref,
+    normed_ref,
+    weight_ref,
+    extra_ref,
+    query_grad_ref,
+    own_ref,
+    came_ref,
+    kept_rows,
+    sent_rows,
+    kept_ref,
+    sent_ref,
+    turned,
+    sums,
+    gains,
+):
     step = pl.program_id(0)
-    query_grads = given[: len(splits)]
-    owns = given[len(splits) : 2 * len(splits)]
-    came = given[2 * len(splits) :]
-    heads = sum(splits)
-    width = query_grads[0].shape[2]
+    heads, unused, width = query_grad_ref.shape
     part = heads * width
-    head = 0
-    for k, count in enumerate(splits):
-        for h in range(count):
-            turned[head * width : (head + 1) * width, :] = (
-                query_grads[k][h].astype(f32).T.astype(bf16)
-            )
-            both = (owns[k][h] + came[k][h].astype(f32)).astype(bf16)
-            for side in range(2):
-                at = part * (side + 1) + head * width
-                turned[at : at + width, :] = both[side * width : (side + 1) * width]
-            head += 1
+    for head in range(heads):
+        turned[head * width : (head + 1) * width, :] = query_grad_ref[head].T
+        both = (own_ref[head].astype(f32) + came_ref[head].astype(f32)).astype(bf16)
+        for side in range(2):
+            at = part * (side + 1) + head * width
+            turned[at : at + width, :] = both[side * width : (side + 1) * width]
     grads = turned[...]
     normed_grad = lax.dot_general(
         grads,
@@ -416,19 +420,15 @@
         preferred_element_type=f32,
     )
     low = normed_grad.astype(bf16)
-    half, model = low.shape[0] // 2, low.shape[1]
+    half = low.shape[0] // 2
     for k in range(2):
 
         @pl.when(place_ref[0] == k)
         def store():
-            for share in range(2):
-                lanes = slice(share * model // 2, (share + 1) * model // 2)
-                rows_refs[share][0] = low[k * half : (k + 1) * half, lanes]
-                rows_refs[2 + share][0] = low[(1 - k) * half : (2 - k) * half, lanes]
-
-    tokens = token_ref[...].astype(f32)
-    scale = lax.rsqrt(jnp.mean(tokens * tokens, axis=-1, keepdims=True) + epsilon)
-    gain = jnp.sum(normed_grad * (tokens * scale), axis=0, keepdims=True)
+            kept_rows[0] = low[k * half : (k + 1) * half]
+            sent_rows[0] = low[(1 - k) * half : (2 - k) * half]
+
+    gain = jnp.sum(normed_grad * normed_ref[...].astype(f32), axis=0, keepdims=True)
     update = jnp.dot(grads, normed_ref[...], preferred_element_type=f32)
 
     @pl.when(step == 0)
@@ -440,11 +440,12 @@
     def more():
         sums[...] += update
 
-    gains[0:1, :] += gain
+    gains[0:1, :] += gain / extra_ref[3:4, :]
 
     @pl.when(step == pl.num_programs(0) - 1)
     def finish():
         update = sums[...].T
+        model = update.shape[0]
         extras = jnp.concatenate(
             [gains[...], jnp.zeros((BLOCK - gains.shape[0], model), f32)], axis=0
         ).T
@@ -460,70 +461,63 @@
                         ref[owner, :, 3 * part :] = extras[at].astype(bf16)
 
 
-def project_back(place, query_grads, owns, came, normed, tokens, weight, extra, weight_rows):
-    rows, model = tokens.shape
-    splits = tuple(value.shape[0] for value in query_grads)
-    width = query_grads[0].shape[2]
-    part = sum(splits) * width
+def project_back(place, query_grad, own, came, normed, weight, extra, weight_rows):
+    rows, model = normed.shape
+    heads, unused, width = query_grad.shape
+    part = heads * width
     tile = 2 * BLOCK
     steps = rows // tile
-    by_rows = pl.BlockSpec((tile, model), lambda i, s: (i, 0))
     whole = lambda shape: pl.BlockSpec(shape, lambda i, s: (0, 0))
-    pairs = [pl.BlockSpec((count, 2 * width, tile), lambda i, s: (0, 0, i)) for count in splits]
-    share = (1, BLOCK, model // 2)
+    pairs = pl.BlockSpec((heads, 2 * width, tile), lambda i, s: (0, 0, i))
+    share = pl.BlockSpec((1, BLOCK, model), lambda i, s: (i, 0, 0))
     packed = (model // (2 * weight_rows), weight_rows, 3 * part + BLOCK)
     return pl.pallas_call(
-        functools.partial(project_back_kernel, splits),
+        project_back_kernel,
         grid_spec=pltpu.PrefetchScalarGridSpec(
             num_scalar_prefetch=1,
             grid=(steps,),
-            in_specs=[by_rows, by_rows, whole(weight.shape), whole(extra.shape)]
-            + [pl.BlockSpec((count, tile, width), lambda i, s: (0, i, 0)) for count in splits]
-            + pairs
-            + pairs,
-            out_specs=[pl.BlockSpec(share, lambda i, s: (i, 0, 0))] * 4
-            + [pl.BlockSpec(packed, lambda i, s: (0, 0, 0))] * 2,
+            in_specs=[
+                pl.BlockSpec((tile, model), lambda i, s: (i, 0)),
+                whole(weight.shape),
+                whole(extra.shape),
+                pl.BlockSpec((heads, tile, width), lambda i, s: (0, i, 0)),
+                pairs,
+                pairs,
+            ],
+            out_specs=[share] * 2 + [pl.BlockSpec(packed, lambda i, s: (0, 0, 0))] * 2,
             scratch_shapes=[
                 pltpu.VMEM((3 * part, tile), bf16),
                 pltpu.VMEM((3 * part, model), f32),
                 pltpu.VMEM(extra.shape, f32),
             ],
         ),
-        out_shape=[jax.ShapeDtypeStruct((steps, *share[1:]), bf16)] * 4
+        out_shape=[jax.ShapeDtypeStruct((steps, BLOCK, model), bf16)] * 2
         + [jax.ShapeDtypeStruct(packed, bf16)] * 2,
         compiler_params=vmem_limit(60),
         cost_estimate=pl.CostEstimate(
             flops=12 * rows * model * part, bytes_accessed=12 * rows * model, transcendentals=0
         ),
         name="project_back",
-    )(place, normed, tokens, weight, extra, *query_grads, *owns, *came)
-
-
-def rows_kernel(place_ref, token_ref, residual_ref, gain_ref, *refs):
-    terms, grad_ref = refs[:-1], refs[-1]
-    per_share = len(terms) // 2
+    )(place, normed, weight, extra, query_grad, own, came)
+
+
+def rows_kernel(place_ref, token_ref, residual_ref, gain_ref, own_ref, other_ref, grad_ref):
     seqs, local_rows, model = token_ref.shape
-    for seq in range(seqs):
-        shares = []
-        for share in range(2):
-            total = jnp.zeros((local_rows, model // 2), f32)
-            for shift in range(per_share):
-                term = terms[share * per_share + shift][...].astype(f32)
-                total = total + jnp.where(place_ref[shift] == seq, term, 0.0)
-            shares.append(total)
-        weighted = jnp.concatenate(shares, axis=1) * gain_ref[...]
+    for k, normed_ref in enumerate((own_ref, other_ref)):
+        seq = place_ref[0] ^ k
+        weighted = normed_ref[...].astype(f32) * gain_ref[...]
         tokens = token_ref[seq].astype(f32)
         scale = lax.rsqrt(jnp.mean(tokens * tokens, axis=-1, keepdims=True) + epsilon)
         inner = jnp.mean(weighted * tokens, axis=-1, keepdims=True)
-        rows = slice(seq * local_rows, (seq + 1) * local_rows)
+        rows = pl.ds(pl.multiple_of(seq * local_rows, local_rows), local_rows)
         grad_ref[seq] = (
             residual_ref[rows] + scale * weighted - tokens * (scale * scale * scale * inner)
         )
 
 
-def rows_stage(place, tokens, residual_grad, gain_row, terms):
+def rows_stage(place, tokens, residual_grad, gain_row, own, other):
     whole = lambda array: pl.BlockSpec(array.shape, lambda i, s: (0,) * array.ndim)
-    given = (tokens, residual_grad, gain_row, *terms)
+    given = (tokens, residual_grad, gain_row, own, other)
     return pl.pallas_call(
         rows_kernel,
         grid_spec=pltpu.PrefetchScalarGridSpec(
@@ -575,25 +569,22 @@
             jax.ShapeDtypeStruct((seqs * local_rows, model), f32),
             jax.ShapeDtypeStruct((seqs * local_rows, model), bf16),
         ],
-        compiler_params=vmem_limit(60),
+        compiler_params=vmem_limit(40),
         cost_estimate=pl.CostEstimate(
             flops=2 * seqs * local_rows * model * model,
             bytes_accessed=2 * model * model,
             transcendentals=0,
         ),
         name="output_stage",
-    )(context, tokens, gain_row, *[everything] * len(shape.output_specs()))
-
-
-def hidden_kernel(
-    shape, place_ref, normed_own, normed_other, down_own, down_other, gate_w, upper_w, *refs
-):
-    panels = shape.model // PANEL
+    )(context, tokens, gain_row, *[everything] * shape.panels)
+
+
+def hidden_kernel(shape, normed_own, normed_other, down_own, down_other, gate_w, upper_w, *refs):
+    panels = shape.panels
     down_w = refs[:panels]
-    out_own, out_other, norm_own, norm_other = refs[panels : panels + 4]
-    grad_refs, (normed, downs, outs, norms) = refs[panels + 4 : -4], refs[-4:]
+    norm_own, norm_other, hidden_ref, gate_ref, upper_ref = refs[panels : panels + 5]
+    normed, downs, lows, sides, pres = refs[panels + 5 :]
     step = pl.program_id(0)
-    x, dp = place_ref[0], place_ref[1]
     half = normed_own.shape[0]
 
     @pl.when(step == 0)
@@ -603,82 +594,101 @@
         downs[:half] = down_own[...]
         downs[half:] = down_other[...]
 
-    rows, grad = normed[...], downs[...]
-    gate = gate_w[...].reshape(shape.model, PANEL)
-    upper = upper_w[...].reshape(shape.model, PANEL)
-    gate_pre = jnp.dot(rows, gate, preferred_element_type=f32)
-    up_pre = jnp.dot(rows, upper, preferred_element_type=f32)
-    hidden_grad = None
+    across = (((1,), (1,)), ((), ()))
+    weights = []
+    for side, weight_ref in enumerate((gate_w, upper_w)):
+        weight = weight_ref[...].reshape(shape.model, PANEL)
+        sides[side, step] = weight
+        pres[side] = jnp.dot(normed[...], weight, preferred_element_type=f32)
+    down = jnp.concatenate([ref[...].reshape(PANEL, PANEL) for ref in down_w], axis=1)
+    pres[2] = lax.dot_general(downs[...], down, across, preferred_element_type=f32)
+    slope = 0.7978845608028654
+    tile = 64
+
+    def bend_rows(k, carried):
+        rows = pl.ds(pl.multiple_of(k * tile, tile), tile)
+        gate_pre, up_pre, hidden_grad = pres[0, rows], pres[1, rows], pres[2, rows]
+        square = gate_pre * gate_pre
+        bend = jnp.tanh(slope * gate_pre * (1.0 + 0.044715 * square))
+        share = 0.5 * (1.0 + bend)
+        curved = gate_pre * share
+        steep = share + 0.5 * gate_pre * (1.0 - bend * bend) * (
+            slope * (1.0 + 3.0 * 0.044715 * square)
+        )
+        hidden_ref[rows] = (curved * up_pre).astype(bf16)
+        gate_low = (hidden_grad * up_pre * steep).astype(bf16)
+        up_low = (hidden_grad * curved).astype(bf16)
+        gate_ref[rows], upper_ref[rows] = gate_low, up_low
+        lows[0, step, rows], lows[1, step, rows] = gate_low, up_low
+        return carried
+
+    lax.fori_loop(0, 2 * half // tile, bend_rows, 0)
+
+    @pl.when(step == shape.steps - 1)
+    def finish():
+        for rows, ref in ((slice(0, half), norm_own), (slice(half, 2 * half), norm_other)):
+            total = None
+            for side in range(2):
+                for k in range(shape.steps):
+                    more = lax.dot_general(
+                        lows[side, k, rows], sides[side, k], across, preferred_element_type=f32
+                    )
+                    total = more if total is None else total + more
+            ref[...] = total.astype(ref.dtype)
+
+
+def hidden_back_kernel(
+    shape,
+    place_ref,
+    normed_own,
+    normed_other,
+    down_own,
+    down_other,
+    hidden_ref,
+    gate_ref,
+    upper_ref,
+    output_ref,
+    *refs,
+):
+    panels = shape.panels
+    down_w = refs[:panels]
+    out_own, out_other = refs[panels : panels + 2]
+    grad_refs, (turned, downs, outs) = refs[panels + 2 : -3], refs[-3:]
+    step = pl.program_id(0)
+    x, dp = place_ref[0], place_ref[1]
+    half = normed_own.shape[0]
+
+    @pl.when(step == 0)
+    def gather():
+        turned[:, :half] = normed_own[...].T
+        turned[:, half:] = normed_other[...].T
+        downs[:half] = down_own[...]
+        downs[half:] = down_other[...]
+        shape.store_output(grad_refs, output_ref, x)
+
+    hidden = hidden_ref[...]
+    down = jnp.concatenate([ref[...].reshape(PANEL, PANEL) for ref in down_w], axis=1)
+    product = jnp.dot(hidden, down, preferred_element_type=f32)
+
+    @pl.when(step == 0)
+    def first_out():
+        outs[...] = product
+
+    @pl.when(step != 0)
+    def later_out():
+        outs[...] += product
+
+    for side, ref in enumerate((gate_ref, upper_ref)):
+        grad = jnp.dot(turned[...], ref[...], preferred_element_type=f32)
+        shape.store_side(grad_refs, step, side, grad, x, dp)
+    grad = jnp.dot(hidden.T, downs[...], preferred_element_type=f32)
     for p in range(panels):
-        product = lax.dot_general(
-            grad[:, p * PANEL : (p + 1) * PANEL],
-            down_w[p][...].reshape(PANEL, PANEL),
-            (((1,), (1,)), ((), ())),
-            preferred_element_type=f32,
-        )
-        hidden_grad = product if hidden_grad is None else hidden_grad + product
-    slope = 0.7978845608028654
-    square = gate_pre * gate_pre
-    bend = jnp.tanh(slope * gate_pre * (1.0 + 0.044715 * square))
-    share = 0.5 * (1.0 + bend)
-    curved = gate_pre * share
-    hidden = (curved * up_pre).astype(bf16)
-    steep = share + 0.5 * gate_pre * (1.0 - bend * bend) * (
-        slope * (1.0 + 3.0 * 0.044715 * square)
-    )
-    gate_low = (hidden_grad * up_pre * steep).astype(bf16)
-    up_low = (hidden_grad * curved).astype(bf16)
-    across = (((1,), (1,)), ((), ()))
-    norm_part = lax.dot_general(gate_low, gate, across, preferred_element_type=f32)
-    norm_part += lax.dot_general(up_low, upper, across, preferred_element_type=f32)
-
-    @pl.when(step == 0)
-    def first():
-        norms[...] = norm_part
-
-    @pl.when(step != 0)
-    def later():
-        norms[...] += norm_part
-
-    along = (((0,), (0,)), ((), ()))
-    for p in range(panels):
-        lanes = slice(p * PANEL, (p + 1) * PANEL)
-        product = jnp.dot(
-            hidden, down_w[p][...].reshape(PANEL, PANEL), preferred_element_type=f32
-        )
-
-        @pl.when(step == 0)
-        def first_out():
-            outs[:, lanes] = product
-
-        @pl.when(step != 0)
-        def later_out():
-            outs[:, lanes] += product
-
-        shape.store_down(
-            grad_refs,
-            step,
-            p,
-            lax.dot_general(hidden, grad[:, lanes], along, preferred_element_type=f32),
-            x,
-            dp,
-        )
-    for side, low in enumerate((gate_low, up_low)):
-        shape.store_side(
-            grad_refs,
-            step,
-            side,
-            lax.dot_general(rows, low, along, preferred_element_type=f32),
-            x,
-            dp,
-        )
+        shape.store_down(grad_refs, step, p, grad[:, p * PANEL : (p + 1) * PANEL], x, dp)
 
     @pl.when(step == shape.steps - 1)
     def finish():
         out_own[...] = outs[:half]
         out_other[...] = outs[half:].astype(bf16)
-        norm_own[...] = norms[:half]
-        norm_other[...] = norms[half:].astype(bf16)
 
 
 class PackedWeights:
@@ -720,9 +730,28 @@
         if self.pieces == 1:
             return [(1, self.grad_rows, PANEL)]
         side = self.steps * self.side
-        first = (self.pieces // 2, side + self.deep, PANEL)
+        first = (self.pieces // 2, side + self.deep + self.panels * 32, PANEL)
         second = (self.pieces // 2, side + (self.panels - 1) * self.deep, PANEL)
         return [first, first, second, second]
+
+    def store_output(self, refs, output_ref, x):
+        if self.pieces == 1:
+            return
+        owners, rows, model = output_ref.shape
+        pairs = output_ref[...].reshape(owners // 2, 2, rows, model)
+        start = self.steps * self.side + self.deep
+        short = jnp.zeros((owners // 2, 32 - rows, PANEL), bf16)
+        for k in range(2):
+
+            @pl.when(x == k)
+            def store():
+                for p in range(self.panels):
+                    lanes = slice(p * PANEL, (p + 1) * PANEL)
+                    at = slice(start + 32 * p, start + 32 * (p + 1))
+                    for slot, side in ((0, k), (1, 1 - k)):
+                        refs[slot][:, at, :] = jnp.concatenate(
+                            [pairs[:, side, :, lanes], short], axis=1
+                        )
 
     def store_side(self, refs, step, side, value, x, dp):
         low = value.astype(bf16).reshape(self.pieces, self.side, PANEL)
@@ -777,43 +806,76 @@
                     refs[slot][spots, first : first + self.deep, :] = pieces
 
 
-def hidden_stage(place, normed, normed_other, down, down_other, everything, shape):
+def hidden_stage(normed, normed_other, down, down_other, everything, shape):
+    half, model = normed.shape
+    whole = pl.BlockSpec((half, model), lambda j: (0, 0))
+    panel = pl.BlockSpec((2 * half, PANEL), lambda j: (0, j))
+    units = shape.steps * PANEL
+    return pl.pallas_call(
+        functools.partial(hidden_kernel, shape),
+        grid=(shape.steps,),
+        in_specs=[whole] * 4
+        + [shape.side_spec(0), shape.side_spec(shape.steps)]
+        + shape.down_specs(),
+        out_specs=[whole] * 2 + [panel] * 3,
+        out_shape=[
+            jax.ShapeDtypeStruct((half, model), f32),
+            jax.ShapeDtypeStruct((half, model), bf16),
+        ]
+        + [jax.ShapeDtypeStruct((2 * half, units), bf16)] * 3,
+        scratch_shapes=[
+            pltpu.VMEM((2 * half, model), bf16),
+            pltpu.VMEM((2 * half, model), bf16),
+            pltpu.VMEM((2, shape.steps, 2 * half, PANEL), bf16),
+            pltpu.VMEM((2, shape.steps, model, PANEL), bf16),
+            pltpu.VMEM((3, 2 * half, PANEL), f32),
+        ],
+        compiler_params=vmem_limit(40),
+        cost_estimate=pl.CostEstimate(
+            flops=10 * 2 * half * model * units, bytes_accessed=12 * model * units, transcendentals=0
+        ),
+        name="hidden_stage",
+    )(normed, normed_other, down, down_other, *[everything] * (2 + shape.panels))
+
+
+def hidden_back(place, normed, normed_other, down, down_other, lows, output, everything, shape):
     half, model = normed.shape
     whole = pl.BlockSpec((half, model), lambda j, s: (0, 0))
+    panel = pl.BlockSpec((2 * half, PANEL), lambda j, s: (0, j))
     with_place = lambda spec: pl.BlockSpec(
         spec.block_shape, lambda j, s, spec=spec: spec.index_map(j)
     )
     grads = shape.grad_shapes()
-    weights = [shape.side_spec(0), shape.side_spec(shape.steps)] + shape.down_specs()
+    units = shape.steps * PANEL
     return pl.pallas_call(
-        functools.partial(hidden_kernel, shape),
+        functools.partial(hidden_back_kernel, shape),
         grid_spec=pltpu.PrefetchScalarGridSpec(
             num_scalar_prefetch=1,
             grid=(shape.steps,),
-            in_specs=[whole] * 4 + [with_place(spec) for spec in weights],
-            out_specs=[whole] * 4 + [pl.BlockSpec(size, lambda j, s: (0, 0, 0)) for size in grads],
+            in_specs=[whole] * 4
+            + [panel] * 3
+            + [pl.BlockSpec(output.shape, lambda j, s: (0, 0, 0))]
+            + [with_place(spec) for spec in shape.down_specs()],
+            out_specs=[whole] * 2 + [pl.BlockSpec(size, lambda j, s: (0, 0, 0)) for size in grads],
             scratch_shapes=[
-                pltpu.VMEM((2 * half, model), bf16),
+                pltpu.VMEM((model, 2 * half), bf16),
                 pltpu.VMEM((2 * half, model), bf16),
                 pltpu.VMEM((2 * half, model), f32),
-                pltpu.VMEM((2 * half, model), f32),
             ],
         ),
         out_shape=[
-            jax.ShapeDtypeStruct((half, model), f32),
-            jax.ShapeDtypeStruct((half, model), bf16),
             jax.ShapeDtypeStruct((half, model), f32),
             jax.ShapeDtypeStruct((half, model), bf16),
         ]
         + [jax.ShapeDtypeStruct(size, bf16) for size in grads],
-        compiler_params=vmem_limit(60),
+        compiler_params=vmem_limit(40),
         cost_estimate=pl.CostEstimate(
-            flops=18 * 2 * half * model * shape.steps * PANEL,
-            bytes_accessed=12 * model * shape.steps * PANEL,
-            transcendentals=0,
-        ),
-        name="hidden_stage",
-    )(place, normed, normed_other, down, down_other, *[everything] * (2 + shape.panels))
+            flops=8 * 2 * half * model * units, bytes_accessed=12 * model * units, transcendentals=0
+        ),
+        name="hidden_back",
+    )(
+        place, normed, normed_other, down, down_other, *lows, output, *[everything] * shape.panels
+    )
 
 
 def output_back_kernel(norm_own, norm_other, residual_ref, down_ref, gain_ref, context_ref, *refs):
@@ -875,7 +937,7 @@
         in_specs=[whole(array) for array in given] + shape.output_specs(),
         out_specs=[whole(array) for array in out_shape],
         out_shape=out_shape,
-        compiler_params=vmem_limit(60),
+        compiler_params=vmem_limit(40),
         cost_estimate=pl.CostEstimate(
             flops=4 * rows * model * model, bytes_accessed=4 * model * model, transcendentals=0
         ),
@@ -885,24 +947,21 @@
 
 def owned_kernel(part, term_ref, *refs):
     groups, rows, columns = term_ref.shape
-    model = refs[0].shape[1]
-    total = None
+    extras = None
     for group in range(groups):
         term = term_ref[group].astype(f32)
         for k in range(3):
-            first = model + k * part
-            refs[k][:, group * part : (group + 1) * part] = term[:, first : first + part]
-        total = term if total is None else total + term
-    refs[3][...] = total[:, :model]
-    extras = total[:, model + 3 * part :]
+            refs[k][:, group * part : (group + 1) * part] = term[:, k * part : (k + 1) * part]
+        more = term[:, 3 * part :]
+        extras = more if extras is None else extras + more
     short = jnp.zeros((BLOCK - rows, BLOCK), f32)
-    refs[4][...] = jnp.concatenate([extras, short], axis=0).T[:8]
+    refs[3][...] = jnp.concatenate([extras, short], axis=0).T[:8]
 
 
 def owned_stage(terms, model, part):
     groups, rows, columns = terms.shape
     whole = lambda array: pl.BlockSpec(array.shape, lambda i: (0,) * array.ndim)
-    out_shape = [jax.ShapeDtypeStruct((rows, model), f32)] * 4 + [
+    out_shape = [jax.ShapeDtypeStruct((rows, model), f32)] * 3 + [
         jax.ShapeDtypeStruct((8, BLOCK), f32)
     ]
     return pl.pallas_call(
@@ -923,6 +982,10 @@
     return lax.ppermute(value, axis, [(0, 1), (1, 0)])
 
 
+def after(value, gate):
+    return lax.optimization_barrier((value, gate))[0]
+
+
 def pick(pair, index, axis):
     return lax.dynamic_index_in_dim(pair, index, axis, keepdims=False)
 
@@ -939,22 +1002,6 @@
 
 def halve(value, index, name, axis):
     return plus(pick(value, index, axis), swap(pick(value, 1 - index, axis), name))
-
-
-def turn(value, shift):
-    count = 2 * 2
-    return lax.ppermute(value, ("zh", "zl"), [(i, (i + shift) % count) for i in range(count)])
-
-
-def exchange(value, axes, index, axis):
-    count = value.shape[axis]
-    result = value
-    for mask in range(1, count):
-        came = lax.ppermute(
-            pick(value, index ^ mask, axis), axes, [(i, i ^ mask) for i in range(count)]
-        )
-        result = lax.dynamic_update_index_in_dim(result, came, index ^ mask, axis)
-    return result
 
 
 def columns_in_panels(weight):
@@ -1000,12 +1047,9 @@
     own_count = depth * 2 * local_rows
     token_count = seqs * local_rows
 
-    column = jnp.zeros((depth, local_rows, model), bf16)
-    column = lax.dynamic_update_index_in_dim(column, pick(inputs, zh, 0), z, 0)
-    for shift in range(1, depth):
-        arriving = turn(pick(inputs, (z + shift) % depth // 2, 0), shift)
-        column = lax.dynamic_update_index_in_dim(column, arriving, (z - shift) % depth, 0)
-    tokens_own = in_order(column, swap(column, "x"), x, 1).reshape(own_count, model)
+    near = in_order(pick(inputs, zh, 0), swap(pick(inputs, 1 - zh, 0), "zh"), zh, 0)
+    column = in_order(near, swap(near, "zl"), zl, 1)
+    tokens_own = in_order(column, swap(column, "x"), x, 2).reshape(own_count, model)
 
     blocks = [
         jnp.transpose(w.reshape(weight_rows, GROUPS, part), (1, 0, 2))
@@ -1083,6 +1127,7 @@
     other = swap(own, "c")
     biases = skew(vectors)
     place = jnp.stack([a * (own_count // BLOCK), c]).astype(jnp.int32)
+    place = after(place, hot)
     context_own, probs, kept, inverse = attend(place, query, own, other, biases)
     owners = ("zh", "zl", "x")
     context = lax.all_to_all(context_own, owners, 0, 0, tiled=True)
@@ -1092,90 +1137,63 @@
     residual, second = output_stage(context, inputs, gain_b, everything, shape)
     second_other = swap(second, "c")
     sides_place = jnp.stack([x, dp]).astype(jnp.int32)
-    out_own, out_other, norm_own, norm_other, *big_grads = hidden_stage(
-        sides_place, second, second_other, down_grad, down_other, everything, shape
+    norm_own, norm_other, *lows = hidden_stage(
+        second, second_other, down_grad, down_other, everything, shape
     )
     norm_came = swap(norm_other, "c")
+    residual_grad, gain_b_grad, context_sent, output_grad = output_back(
+        norm_own, norm_came, residual, down_grad, gain_b, context, everything, shape
+    )
+    *lows, output_grad, context_sent = lax.optimization_barrier(
+        (*lows, output_grad, context_sent)
+    )
+    context_grad = lax.all_to_all(context_sent, owners, 0, 0, tiled=True)
+    output_terms = halve(
+        output_grad.reshape(model // (2 * weight_rows), CORES, weight_rows, model), c, "c", 1
+    )
+    out_own, out_other, *big_grads = hidden_back(
+        sides_place,
+        second,
+        second_other,
+        down_grad,
+        down_other,
+        lows,
+        output_terms,
+        everything,
+        shape,
+    )
     out_came = swap(out_other, "c")
     outputs = (residual + out_own + out_came.astype(f32)).astype(bf16)
-    residual_grad, gain_b_grad, context_sent, output_grad = output_back(
-        norm_own, norm_came, residual, down_grad, gain_b, context, everything, shape
-    )
-    context_grad = lax.all_to_all(context_sent, owners, 0, 0, tiled=True)
+
     if along_a == 1:
         first_terms, first_sent, second_terms, second_sent = big_grads
         first_came = swap(first_sent, "x")
         second_came = swap(second_sent, "dp")
-    output_terms = output_grad.reshape(
-        along_dp, along_a, 2, GROUPS, CORES, weight_rows, model
-    )
-    output_terms = halve(output_terms, c, "c", 4)
-
-    if along_a == 1:
-        context_grad, first_came, second_came = lax.optimization_barrier(
-            (context_grad, first_came, second_came)
+    query_grad, own_grad, other_grad, bucket_sums = attend_back(
+        place, context_grad, kept, inverse, probs, query, own, other, hot
+    )
+    if along_a > 1:
+        own_grad, other_grad = (
+            lax.psum_scatter(value, "a", scatter_dimension=2, tiled=True)
+            for value in (own_grad, other_grad)
+        )
+    else:
+        first_came, second_came, query_grad, own_grad, other_grad, bucket_sums = (
+            lax.optimization_barrier(
+                (first_came, second_came, query_grad, own_grad, other_grad, bucket_sums)
+            )
         )
         first_terms = plus(first_terms, first_came).reshape(along_dp, depth, -1, PANEL)
         second_terms = plus(second_terms, second_came).reshape(depth, 2, -1, PANEL)
-        first_terms, second_terms, context_grad, output_terms = lax.optimization_barrier(
-            (first_terms, second_terms, context_grad, output_terms)
+        first_terms, second_terms, query_grad = lax.optimization_barrier(
+            (first_terms, second_terms, query_grad)
         )
         first_came = swap(pick(first_terms, 1 - dp, 0), "dp")
         second_came = swap(pick(second_terms, 1 - x, 1), "x")
-    output_came = swap(pick(output_terms, 1 - dp, 0), "dp")
-
-    query_grads, owns, came, offset_grads = [], [], [], []
-    for first, count in ((0, 1), (1, heads - 1)):
-        query_grad, own_grad, other_grad, offset_grad = attend_back(
-            place, context_grad, kept, inverse, probs, query, own, other, hot, first, count
-        )
-        if along_a > 1:
-            own_grad, other_grad = (
-                lax.psum_scatter(value, "a", scatter_dimension=2, tiled=True)
-                for value in (own_grad, other_grad)
-            )
-        elif first == 0:
-            first_came, second_came, output_came, query_grad, own_grad, other_grad, offset_grad = (
-                lax.optimization_barrier(
-                    (
-                        first_came,
-                        second_came,
-                        output_came,
-                        query_grad,
-                        own_grad,
-                        other_grad,
-                        offset_grad,
-                    )
-                )
-            )
-            terms = jnp.concatenate(
-                [
-                    plus(pick(first_terms, dp, 0), first_came),
-                    plus(pick(second_terms, x, 1), second_came),
-                ],
-                axis=1,
-            )
-            output_terms = plus(pick(output_terms, dp, 0), output_came)
-            terms, output_terms, context_grad = lax.optimization_barrier(
-                (terms, output_terms, context_grad)
-            )
-            column_came = [
-                turn(pick(terms, (z + shift) % depth, 0), shift) for shift in range(1, depth)
-            ]
-        else:
-            *column_came, query_grad, own_grad, other_grad, offset_grad = (
-                lax.optimization_barrier(
-                    (*column_came, query_grad, own_grad, other_grad, offset_grad)
-                )
-            )
-        query_grads.append(query_grad)
-        owns.append(own_grad)
-        came.append(swap(other_grad, "c"))
-        offset_grads.append(offset_grad)
-    if along_a > 1:
-        output_terms = plus(pick(output_terms, dp, 0), output_came)
+    came = swap(other_grad, "c")
+
     per_owner = bias_table.shape[0]
-    bucket_sums = jnp.concatenate(offset_grads, axis=0)[:, 0, :BUCKETS]
+    bucket_sums = bucket_sums[:, 0, :BUCKETS]
     spot = jnp.arange(model, dtype=jnp.int32)
     entry = spot // weight_rows * per_owner + spot % weight_rows
     entry = jnp.where(spot % weight_rows < per_owner, entry, -1)
@@ -1186,56 +1204,67 @@
         jnp.where(entry[None, :] % H == own_heads[:, None], table_rows, 0.0), axis=0
     )
     extra = jnp.stack(
-        [jnp.zeros((model,), f32), gain_b_grad.reshape(model), table_row]
-        + [jnp.zeros((model,), f32)] * 5
+        [jnp.zeros((model,), f32), gain_b_grad.reshape(model), table_row, gain_a.reshape(model)]
+        + [jnp.zeros((model,), f32)] * 4
     )
     core_place = jnp.stack([x, c]).astype(jnp.int32)
     *rows_grads, mixed, sent_c = project_back(
-        core_place, query_grads, owns, came, normed, tokens_own, columns, extra, weight_rows
-    )
+        core_place, query_grad, own_grad, came, normed, columns, extra, weight_rows
+    )
+    if along_a == 1:
+        first_came, second_came = (
+            after(value, sent_c) for value in (first_came, second_came)
+        )
 
     by_owner = (along_dp, along_a, 2, GROUPS, weight_rows, mixed.shape[2])
-    mixed, sent_c, sent = mixed.reshape(by_owner), sent_c.reshape(by_owner), rows_grads[2:]
-    came_x = [swap(value, "x") for value in sent]
-    came_c = swap(sent_c, "c")
-    mixed = plus(mixed, came_c)
-    sent_dp, mixed, came_x[0] = lax.optimization_barrier(
-        (pick(mixed, 1 - dp, 0), pick(mixed, dp, 0), came_x[0])
-    )
-    came_dp = swap(sent_dp, "dp")
-    arrived = []
-
-    def along_column(k):
-        share = plus(rows_grads[k], came_x[k])
-        return [pick(share, (z + shift) % depth, 0) for shift in range(depth)]
-
-    def turned(parts):
-        return [part if shift == 0 else turn(part, shift) for shift, part in enumerate(parts)]
-
-    *parts, came_dp = lax.optimization_barrier((*along_column(0), came_dp))
-    arrived += turned(parts)
-    mixed = jnp.concatenate([output_terms, plus(mixed, came_dp)], axis=4)
-    sent_zh, mixed, came_x[1] = lax.optimization_barrier(
-        (pick(mixed, 1 - zh, 1), pick(mixed, zh, 1), came_x[1])
-    )
-    came_zh = swap(sent_zh, "zh")
-    *parts, came_zh = lax.optimization_barrier((*along_column(1), came_zh))
-    arrived += turned(parts)
-    mixed = plus(mixed, came_zh)
+    mixed, sent_c = mixed.reshape(by_owner), sent_c.reshape(by_owner)
+    came_x = swap(rows_grads[1], "x")
+    mixed = plus(mixed, swap(sent_c, "c"))
+    if along_a == 1:
+        terms = jnp.concatenate(
+            [
+                plus(pick(first_terms, dp, 0), first_came),
+                plus(pick(second_terms, x, 1), second_came),
+            ],
+            axis=1,
+        )
+        terms = terms.reshape(2, 2, -1, PANEL)
+        column_came = swap(pick(terms, 1 - zl, 1), "zl")
+    came_dp = swap(pick(mixed, 1 - dp, 0), "dp")
+    mixed = plus(pick(mixed, dp, 0), came_dp)
+    came_zh = swap(pick(mixed, 1 - zh, 1), "zh")
+    share = plus(rows_grads[0], came_x).reshape(2, 2, local_rows, model)
+    share, sent = pick(share, zl, 1), pick(share, 1 - zl, 1)
+    came_zl = swap(sent, "zl")
+    if along_a == 1:
+        column_came = after(column_came, sent)
+        terms = plus(pick(terms, zl, 1), column_came)
+        sent = pick(terms, 1 - zh, 0)
+        column_came = swap(sent, "zh")
+    share = plus(share, after(came_zl, sent))
+    rows_own, sent = pick(share, zh, 0), pick(share, 1 - zh, 0)
+    rows_came = swap(sent, "zh")
+    came_zh = after(came_zh, sent)
+    mixed = plus(pick(mixed, zh, 1), came_zh)
     if along_a > 1:
         mixed = lax.psum_scatter(mixed, "a", scatter_dimension=0, tiled=True)
-    *early, terms_owned = lax.optimization_barrier((*arrived[:depth], mixed[0]))
-    arrived = early + arrived[depth:]
-    terms_owned = lax.all_to_all(terms_owned, ("zl", "x"), 0, 0, tiled=True)
-    origins = jnp.stack([(z - shift) % depth // 2 for shift in range(depth)]).astype(jnp.int32)
-    input_grad = rows_stage(origins, inputs, residual_grad, gain_a, arrived)
+    terms_owned = lax.all_to_all(mixed[0], ("zl", "x"), 0, 0, tiled=True)
+    input_grad = rows_stage(
+        zh.astype(jnp.int32)[None], inputs, residual_grad, gain_a, rows_own, rows_came
+    )
 
     if along_a == 1:
-        total = pick(terms, z, 0).astype(f32)
-        for arriving in column_came:
-            total = total + arriving.astype(f32)
+        column_came = after(column_came, mixed)
+        total = pick(terms, zh, 0).astype(f32) + column_came.astype(f32)
         side, deep = shape.steps * shape.side, shape.deep
-        sides = jnp.concatenate([total[:side], total[side + deep : 2 * side + deep]], axis=0)
+        rest = total[side + deep + shape.panels * 32 :]
+        output_owned = jnp.transpose(
+            total[side + deep : side + deep + shape.panels * 32].reshape(shape.panels, 32, PANEL)[
+                :, :weight_rows
+            ],
+            (1, 0, 2),
+        ).reshape(weight_rows, model)
+        sides = jnp.concatenate([total[:side], rest[:side]], axis=0)
         sides = sides.astype(bf16).reshape(-1, 2, weight_rows, PANEL)
         sides = in_order(pick(sides, c, 1), swap(pick(sides, 1 - c, 1), "c"), c, 0)
         sides = sides.reshape(2, 2, shape.steps, weight_rows, PANEL)
@@ -1244,7 +1273,7 @@
         ).reshape(2, weight_rows, hidden_units)
         gate_owned, upper_owned = sides[0].astype(f32), sides[1].astype(f32)
         down_owned = jnp.transpose(
-            jnp.concatenate([total[side : side + deep], total[2 * side + deep :]], axis=0).reshape(
+            jnp.concatenate([total[side : side + deep], rest[side:]], axis=0).reshape(
                 shape.panels, each, PANEL
             ),
             (1, 0, 2),
@@ -1262,6 +1291,12 @@
             big_grads[0][0, 2 * side :].reshape(shape.panels, -1, PANEL), (1, 0, 2)
         ).reshape(-1, 1, each, model)
         zero = jnp.zeros_like
+        output_owned = lax.psum_scatter(
+            in_order(output_terms, zero(output_terms), c, 1).reshape(model, model),
+            everyone,
+            scatter_dimension=0,
+            tiled=True,
+        ).astype(f32)
         gate_owned, upper_owned = (
             lax.psum_scatter(
                 in_order(half, zero(half), c, 2).reshape(model, hidden_units),
@@ -1283,6 +1318,7 @@
         outputs.reshape(seqs, local_rows, model),
         input_grad,
         *owned,
+        output_owned,
         gate_owned,
         upper_owned,
         down_owned,

time: 335 us -> 305 us (0.910)
  Pallas kernels: 99.8 us -> 84.5 us
  waiting for transfers between devices: 118 us -> 104 us
  starting transfers between devices: 60.3 us -> 47.3 us
  local copies, waits for them, and re-layouts: 24.2 us -> 32.4 us
  other arithmetic: 15.9 us -> 20.4 us
    ppermute x12 -> x0, starting transfers between devices: 23.5 us -> none  [turn(): lax.ppermute(value, ('zh', 'zl'), [(i, (i + shift) % count) for i in rang...]
    ppermute x12 -> x0, waiting for transfers between devices: 14.9 us -> none  [turn(): lax.ppermute(value, ('zh', 'zl'), [(i, (i + shift) % count) for i in rang...]
    ppermute x24 -> x27, starting transfers between devices: 14.1 us -> 27.1 us  [swap(): return lax.ppermute(value, axis, [(0, 1), (1, 0)])]
    unnamed x88 -> x82, local copies, waits for them, and re-layouts: 8.61 us -> 17.8 us
    all_to_all x1, waiting for transfers between devices: 20.1 us -> 12 us  [body(): context = lax.all_to_all(context_own, owners, 0, 0, tiled=True)]
    ppermute x24 -> x27, waiting for transfers between devices: 79.8 us -> 87 us  [swap(): return lax.ppermute(value, axis, [(0, 1), (1, 0)])]
    all_to_all x1, starting transfers between devices: 12.4 us -> 6.28 us  [body(): context = lax.all_to_all(context_own, owners, 0, 0, tiled=True)]
    pallas_call x2 -> x3, Pallas kernels: 36.2 us -> 30.2 us  [the longest x1 12.5 us: hidden_back(): pl.pallas_call(functools.partial(hidden_back_kernel, shape), grid_spec=pl...]
  transfers between devices with their start and end apart: 41 -> 32, of which waited for: 20 -> 18; matrix products, arithmetic and copies ran while one was open for 6% -> 9% of each run, Pallas kernels for 19% -> 24%
where the time goes in v3:
time: 305 us; the launch traced here: 304 us
  waiting for transfers between devices  104 us (34%)
  Pallas kernels  84.5 us (28%)
  starting transfers between devices  47.3 us (16%)
  local copies, waits for them, and re-layouts  32.4 us (11%)
  other arithmetic  20.4 us (7%)
  between operations  15 us (5%)
    ppermute x27, waiting for transfers between devices, swap(): return lax.ppermute(value, axis, [(0, 1), (1, 0)])  87 us
    ppermute x27, starting transfers between devices, swap(): return lax.ppermute(value, axis, [(0, 1), (1, 0)])  27.1 us
    pallas_call x1, Pallas kernels, attend_back(): pl.pallas_call(functools.partial(attend_back_kernel, tile, chunk), grid_s...  24.5 us
    pallas_call x1, Pallas kernels, attend(): pl.pallas_call(functools.partial(attend_kernel, tile, chunk), grid_spec=p...  19.9 us
    unnamed x82, local copies, waits for them, and re-layouts  17.8 us
    pallas_call x1, Pallas kernels, hidden_back(): pl.pallas_call(functools.partial(hidden_back_kernel, shape), grid_spec=pl...  12.5 us
    all_to_all x1, waiting for transfers between devices, body(): context = lax.all_to_all(context_own, owners, 0, 0, tiled=True)  12 us
    pallas_call x1, Pallas kernels, project_back(): pl.pallas_call(project_back_kernel, grid_spec=pltpu.PrefetchScalarGridSpe...  9.93 us
  transfers between devices with their start and end apart: 32, of which 18 were waited for; matrix products, arithmetic and copies ran while one was open for 9% of the time, Pallas kernels for 24%

profile of v3, /device:TPU:0, one launch (start us, length us, event | category | flops | bytes accessed | tf_op | source)
XLA Modules:
  0.0 303.7 jit_solution(7878101373494895505)
XLA Ops:
  9.5 2.5 dynamic-slice_reduce_fusion.2
  16.6 5.1 %all-to-all-start = ((bf16[4,24,704]{2,1,0:T(8,128)(2,1)}), bf16[4,24,704]{2,1,0:T(8,128)(2,1)S(1)}, u32[]{:S(2)}, u32[]{:S(2)}) async-start(bf16[4,24,704]{2,1,0:T(8,128)(2,1)} %pad_maximum_fusion.6), calls=%async_computation | async-start | bytes 294912 | tf_op jit(solution)/shard_map/all_to_all | solution.py:1062
  21.8 2.7 collective-permute-start
  24.4 4.2 %all-to-all-done = bf16[4,24,704]{2,1,0:T(8,128)(2,1)S(1)} async-done(((bf16[4,24,704]{2,1,0:T(8,128)(2,1)}), bf16[4,24,704]{2,1,0:T(8,128)(2,1)S(1)}, u32[]{:S(2)}, u32[]{:S(2)}) %all-to-all-start) | async-done | bytes 135200 | tf_op jit(solution)/shard_map/all_to_all | solution.py:1062
  29.8 13.6 %collective-permute-done = bf16[128,768]{1,0:T(8,128)(2,1)S(1)} collective-permute-done((bf16[128,768]{1,0:T(8,128)(2,1)S(1)}, bf16[128,768]{1,0:T(8,128)(2,1)S(1)}, u32[]{:S(2)}, u32[]{:S(2)}) %collective-permute-start) | collective-permute-done | bytes 196640 | tf_op jit(solution)/shard_map/ppermute | solution.py:982
  43.6 4.3 %collective-permute-done.3 = bf16[4,24,704]{2,1,0:T(8,128)(2,1)S(1)} collective-permute-done((bf16[4,24,704]{2,1,0:T(8,128)(2,1)S(1)}, bf16[4,24,704]{2,1,0:T(8,128)(2,1)S(1)}, u32[]{:S(2)}, u32[]{:S(2)}) %collective-permute-start.3) | collective-permute-done | bytes 135200 | tf_op jit(solution)/shard_map/ppermute | solution.py:982
  48.0 1.6 collective-permute-start.4
  49.7 10.0 %collective-permute-done.1 = bf16[2,128,768]{2,1,0:T(8,128)(2,1)S(1)} collective-permute-done((bf16[2,128,768]{2,1,0:T(8,128)(2,1)S(1)}, bf16[2,128,768]{2,1,0:T(8,128)(2,1)S(1)}, u32[]{:S(2)}, u32[]{:S(2)}) %collective-permute-start.1) | collective-permute-done | bytes 393248 | tf_op jit(solution)/shard_map/ppermute | solution.py:982
  59.8 4.8 %collective-permute-start.2 = (bf16[2,2,128,768]{3,2,0,1:T(8,128)(2,1)S(1)}, bf16[2,2,128,768]{3,2,0,1:T(8,128)(2,1)S(1)}, u32[]{:S(2)}, u32[]{:S(2)}) collective-permute-start(bf16[2,2,128,768]{3,2,0,1:T(8,128)(2,1)S(1)} %maximum_select_fusion.3), channel_id=1, source_target_pairs={{0,2},{2,0},{1,3},{3,1},{4,6},{6,4},{5,7},{7,5},{8,10},{10,8},{9,1... | collective-permute-start | bytes 2359304 | tf_op jit(solution)/shard_map/ppermute | solution.py:982
  65.9 1.9 collective-permute-done.5
  67.8 1.4 maximum_select_fusion.1
  69.6 12.8 %collective-permute-done.2 = bf16[2,2,128,768]{3,2,0,1:T(8,128)(2,1)S(1)} collective-permute-done((bf16[2,2,128,768]{3,2,0,1:T(8,128)(2,1)S(1)}, bf16[2,2,128,768]{3,2,0,1:T(8,128)(2,1)S(1)}, u32[]{:S(2)}, u32[]{:S(2)}) %collective-permute-start.2) | collective-permute-done | bytes 786464 | tf_op jit(solution)/shard_map/ppermute | solution.py:982
  82.8 2.7 project.1
  86.7 2.7 fusion.hot_ref
  91.0 2.0 skew.1.table
  93.0 1.7 copy-done.4
  94.7 19.9 %attend.1 = (bf16[8,192,128]{2,1,0:T(8,128)(2,1)}, bf16[3,1024,2048]{2,1,0:T(8,128)(2,1)}, f32[3,1024,128]{2,1,0:T(8,128)}, f32[3,8,1,128]{3,2,1,0:T(1,128)}) custom-call(s32[2]{0:T(128)} %pad_add_fusion.place_ref, bf16[3,1024,64]{2,1,0:T(8,128)(2,1)} %copy-done.23, bf16[3,1024,128]{2,1,0:T(8,128)(2,1)} %copy-done.20, ...), custom_call_target="tpu_custom_call" | custom-call | flops 6442450944 | bytes 12582912 | tf_op jit(solution)/shard_map/attend/pallas_call | solution.py:207
  114.6 6.3 %all-to-all-start.1 = ((bf16[8,192,128]{2,1,0:T(8,128)(2,1)}), bf16[8,192,128]{2,1,0:T(8,128)(2,1)S(1)}, u32[]{:S(2)}, u32[]{:S(2)}) async-start(bf16[8,192,128]{2,1,0:T(8,128)(2,1)} %get-tuple-element.72), calls=%async_computation.1 | async-start | bytes 786432 | tf_op jit(solution)/shard_map/all_to_all | solution.py:1133
  121.1 12.0 %all-to-all-done.1.context_ref = bf16[8,192,128]{2,1,0:T(8,128)(2,1)S(1)} async-done(((bf16[8,192,128]{2,1,0:T(8,128)(2,1)}), bf16[8,192,128]{2,1,0:T(8,128)(2,1)S(1)}, u32[]{:S(2)}, u32[]{:S(2)}) %all-to-all-start.1) | async-done | bytes 393248 | tf_op jit(solution)/shard_map/all_to_all | solution.py:1133
  133.1 2.7 copy-done
  136.6 1.7 collective-permute-done.8.normed_other
  138.5 7.8 %hidden_stage.1 = (f32[256,768]{1,0:T(8,128)S(1)}, bf16[256,768]{1,0:T(8,128)(2,1)S(1)}, bf16[512,1024]{1,0:T(8,128)(2,1)S(1)}, bf16[512,1024]{1,0:T(8,128)(2,1)S(1)}, bf16[512,1024]{1,0:T(8,128)(2,1)S(1)}) custom-call(bf16[256,768]{1,0:T(8,128)(2,1)S(1)} %get-tuple-element.74.normed_own, bf16[256,768]{1,0:T(8,128)(2,1)S(1)} %collective-permute-done.8.normed_other, ...), custom_call_target="tpu_custom_call" | custom-call | flops 4026531840 | bytes 9437184 | tf_op jit(solution)/shard_map/hidden_stage/pallas_call | solution.py:814
  149.2 1.7 collective-permute-done.10.norm_other
  150.9 2.4 output_back.1
  154.9 4.1 %all-to-all-start.2 = ((bf16[8,192,128]{2,1,0:T(8,128)(2,1)}), bf16[8,192,128]{2,1,0:T(8,128)(2,1)}, u32[]{:S(2)}, u32[]{:S(2)}) async-start(bf16[8,192,128]{2,1,0:T(8,128)(2,1)} %get-tuple-element.93), calls=%async_computation.2 | async-start | bytes 786432 | tf_op jit(solution)/shard_map/all_to_all | solution.py:1150
  159.0 1.5 fusion.6.output_ref
  163.0 12.5 %hidden_back.1 = (f32[256,768]{1,0:T(8,128)S(1)}, bf16[256,768]{1,0:T(8,128)(2,1)S(1)}, bf16[8,352,256]{2,1,0:T(8,128)(2,1)S(1)}, bf16[8,352,256]{2,1,0:T(8,128)...) custom-call(s32[2]{0:T(128)S(1)} %pad_add_fusion.1.place_ref, ...), custom_call_target="tpu_custom_call" | custom-call | flops 3221225472 | bytes 9437184 | tf_op jit(solution)/shard_map/hidden_back/pallas_call | solution.py:850
  179.6 1.9 collective-permute-start.13
  181.5 1.7 collective-permute-start.14
  183.8 24.5 %attend_back.1 = (bf16[3,1024,64]{2,1,0:T(8,128)(2,1)}, bf16[3,128,1024]{2,1,0:T(8,128)(2,1)}, bf16[3,128,1024]{2,1,0:T(8,128)(2,1)}, f32[3,1,128]{2,1,0:T(1,128)}) custom-call(s32[2]{0:T(128)} %pad_add_fusion.place_ref, bf16[8,192,128]{2,1,0:T(8,128)(2,1)} %all-to-all-done.2.grad_ref, f32[3,1024,128]{2,1,0:T(8,128)} %get-tuple-element.94.kept_ref, ...), custom_call_target="tpu_custom_call" | custom-call | flops 12884901888 | bytes 12582912 | tf_op jit(solution)/shard_map/attend_back/pallas_call | solution.py:343
  208.2 4.1 %collective-permute-done.14 = bf16[8,320,256]{2,1,0:T(8,128)(2,1)} collective-permute-done((bf16[8,320,256]{2,1,0:T(8,128)(2,1)}, bf16[8,320,256]{2,1,0:T(8,128)(2,1)}, u32[]{:S(2)}, u32[]{:S(2)}) %collective-permute-start.14) | collective-permute-done | bytes 1310752 | tf_op jit(solution)/shard_map/ppermute | solution.py:982
  212.4 1.2 collective-permute-done.13
  214.7 1.8 add_convert_fusion
  216.6 1.6 add_convert_fusion.1
  219.3 1.6 collective-permute-start.19
  221.8 1.6 collective-permute-start.18
  223.4 1.9 add_convert_fusion.3
  226.2 9.9 %project_back.1 = (bf16[4,128,768]{2,1,0:T(8,128)(2,1)}, bf16[4,128,768]{2,1,0:T(8,128)(2,1)}, bf16[16,24,704]{2,1,0:T(8,128)(2,1)}, bf16[16,24,704]{2,1,0:T(8,128)(2,1)}) custom-call(s32[2]{0:T(128)} %pad_add_fusion.2.place_ref, bf16[1024,768]{1,0:T(8,128)(2,1)} %copy-done.22, bf16[768,704]{1,0:T(8,128)(2,1)} %bitcast.170, f32[8,768]{1,0:T(8,128)} %stack.227.extra_ref, ...), custom_call_target="tpu_custom_call" | custom-call | flops 1811939328 | bytes 9437184 | tf_op jit(solution)/shard_map/project_back/pallas_call | solution.py:474
  237.3 1.3 fusion.4
  239.3 1.3 fusion.2
  240.8 1.5 collective-permute-start.20
  242.6 1.7 collective-permute-start.23
  244.2 12.1 %collective-permute-done.16 = bf16[4,128,768]{2,1,0:T(8,128)(2,1)S(1)} collective-permute-done((bf16[4,128,768]{2,1,0:T(8,128)(2,1)}, bf16[4,128,768]{2,1,0:T(8,128)(2,1)S(1)}, u32[]{:S(2)}, u32[]{:S(2)}) %collective-permute-start.16) | collective-permute-done | bytes 786464 | tf_op jit(solution)/shard_map/ppermute | solution.py:982
  256.6 1.5 collective-permute-start.17
  258.4 2.5 collective-permute-start.25
  261.6 13.7 %collective-permute-done.17 = bf16[2,128,768]{2,1,0:T(8,128)(2,1)S(1)} collective-permute-done((bf16[2,128,768]{2,1,0:T(8,128)(2,1)S(1)}, bf16[2,128,768]{2,1,0:T(8,128)(2,1)S(1)}, u32[]{:S(2)}, u32[]{:S(2)}) %collective-permute-start.17) | collective-permute-done | bytes 393248 | tf_op jit(solution)/shard_map/ppermute | solution.py:982
  275.4 7.0 %collective-permute-done.24 = bf16[1,4,24,704]{3,2,1,0:T(8,128)(2,1)S(1)} collective-permute-done((bf16[1,4,24,704]{3,2,1,0:T(8,128)(2,1)S(1)}, bf16[1,4,24,704]{3,2,1,0:T(8,128)(2,1)S(1)}, u32[]{:S(2)}, u32[]{:S(2)}) %collective-permute-start.24) | collective-permute-done | bytes 135200 | tf_op jit(solution)/shard_map/ppermute | solution.py:982
  285.0 4.6 %all-to-all-start.3 = ((bf16[4,24,704]{2,1,0:T(8,128)(2,1)}), bf16[4,24,704]{2,1,0:T(8,128)(2,1)S(1)}, u32[]{:S(2)}, u32[]{:S(2)}) async-start(bf16[4,24,704]{2,1,0:T(8,128)(2,1)} %bitcast.66), calls=%async_computation.3 | async-start | bytes 294912 | tf_op jit(solution)/shard_map/all_to_all | solution.py:1251
  (215 shorter events, 42.8 us)
Async XLA Ops:
  7.2 5.4 %copy-start.33 = (bf16[24,768]{1,0:T(8,128)(2,1)S(1)}, bf16[24,768]{1,0:T(8,128)(2,1)}, u32[]{:S(2)}) copy-start(bf16[24,768]{1,0:T(8,128)(2,1)} %param.17) | copy-start | bytes 110596
  7.2 125.9 %all-gather.2.cloned.1.call-start = ((), (), s32[]{:S(2)}) async-start(), calls=%async_computation.4 | async-start | bytes 6266880 | tf_op jit(solution)/shard_map/all_gather | solution.py:1099
  7.2 5.9 %copy-start.29 = (bf16[64,768]{1,0:T(8,128)(2,1)S(1)}, bf16[64,768]{1,0:T(8,128)(2,1)}, u32[]{:S(2)}) copy-start(bf16[64,768]{1,0:T(8,128)(2,1)} %param.20) | copy-start | bytes 294916
  12.6 1.5 collective-permute-start.7
  14.4 7.3 %copy-start.3 = (bf16[2,128,768]{2,1,0:T(8,128)(2,1)S(1)}, bf16[2,128,768]{2,1,0:T(8,128)(2,1)}, u32[]{:S(2)}) copy-start(bf16[2,128,768]{2,1,0:T(8,128)(2,1)} %token_ref.3) | copy-start | bytes 1179652
  16.6 12.0 %all-to-all-start = ((bf16[4,24,704]{2,1,0:T(8,128)(2,1)}), bf16[4,24,704]{2,1,0:T(8,128)(2,1)S(1)}, u32[]{:S(2)}, u32[]{:S(2)}) async-start(bf16[4,24,704]{2,1,0:T(8,128)(2,1)} %pad_maximum_fusion.6), calls=%async_computation | async-start | bytes 294912 | tf_op jit(solution)/shard_map/all_to_all | solution.py:1062
  21.8 21.7 %collective-permute-start = (bf16[128,768]{1,0:T(8,128)(2,1)S(1)}, bf16[128,768]{1,0:T(8,128)(2,1)S(1)}, u32[]{:S(2)}, u32[]{:S(2)}) collective-permute-start(bf16[128,768]{1,0:T(8,128)(2,1)S(1)} %get-tuple-element.139), channel_id=1, source_target_pairs={{0,8},{8,0},{1,9},{9,1},{2,10},{10,2},{3,11},{11,3},{4,12},{12,4},... | collective-permute-start | bytes 589832 | tf_op jit(solution)/shard_map/ppermute | solution.py:982
  28.6 19.3 %collective-permute-start.3 = (bf16[4,24,704]{2,1,0:T(8,128)(2,1)S(1)}, bf16[4,24,704]{2,1,0:T(8,128)(2,1)S(1)}, u32[]{:S(2)}, u32[]{:S(2)}) collective-permute-start(bf16[4,24,704]{2,1,0:T(8,128)(2,1)S(1)} %all-to-all-done), channel_id=1, source_target_pairs={{0,8},{8,0},{1,9},{9,1},{2,10},{10,2},{3,11},{11,3},{4,12},{12,4},... | collective-permute-start | bytes 405512 | tf_op jit(solution)/shard_map/ppermute | solution.py:982
  43.5 16.2 %collective-permute-start.1 = (bf16[2,128,768]{2,1,0:T(8,128)(2,1)S(1)}, bf16[2,128,768]{2,1,0:T(8,128)(2,1)S(1)}, u32[]{:S(2)}, u32[]{:S(2)}) collective-permute-start(bf16[2,128,768]{2,1,0:T(8,128)(2,1)S(1)} %maximum_select_fusion.6), channel_id=1, source_target_pairs={{0,4},{4,0},{1,5},{5,1},{2,6},{6,2},{3,7},{7,3},{8,12},{12,8},{9,1... | collective-permute-start | bytes 1179656 | tf_op jit(solution)/shard_map/ppermute | solution.py:982
  48.0 16.6 %collective-permute-start.4 = (bf16[2,4,24,704]{3,2,1,0:T(8,128)(2,1)S(1)}, bf16[2,4,24,704]{3,2,1,0:T(8,128)(2,1)S(1)}, u32[]{:S(2)}, u32[]{:S(2)}) collective-permute-start(bf16[2,4,24,704]{3,2,1,0:T(8,128)(2,1)S(1)} %maximum_select_fusion.9), channel_id=1, source_target_pairs={{0,16},{16,0},{1,17},{17,1},{2,18},{18,2},{3,19},{19,3},{4,20},{20... | collective-permute-start | bytes 811016 | tf_op jit(solution)/shard_map/ppermute | solution.py:982
  59.7 5.8 %copy-start.34 = (s32[4095]{0:T(1024)S(1)}, s32[4095]{0:T(1024)}, u32[]{:S(2)}) copy-start(s32[4095]{0:T(1024)} %param.24) | copy-start | bytes 49144
  59.8 22.6 %collective-permute-start.2 = (bf16[2,2,128,768]{3,2,0,1:T(8,128)(2,1)S(1)}, bf16[2,2,128,768]{3,2,0,1:T(8,128)(2,1)S(1)}, u32[]{:S(2)}, u32[]{:S(2)}) collective-permute-start(bf16[2,2,128,768]{3,2,0,1:T(8,128)(2,1)S(1)} %maximum_select_fusion.3), channel_id=1, source_target_pairs={{0,2},{2,0},{1,3},{3,1},{4,6},{6,4},{5,7},{7,5},{8,10},{10,8},{9,1... | collective-permute-start | bytes 2359304 | tf_op jit(solution)/shard_map/ppermute | solution.py:982
  65.5 2.3 collective-permute-start.5
  69.3 20.8 %copy-start.5 = (bf16[2,2,4,2,24,704]{5,4,3,2,1,0:T(8,128)(2,1)}, bf16[2,2,4,2,24,704]{5,4,3,2,1,0:T(8,128)(2,1)S(1)}, u32[]{:S(2)}) copy-start(bf16[2,2,4,2,24,704]{5,4,3,2,1,0:T(8,128)(2,1)S(1)} %maximum_select_fusion.1) | copy-start | bytes 3244036
  86.7 6.2 %copy-start.20 = (bf16[3,1024,128]{2,1,0:T(8,128)(2,1)}, bf16[3,1024,128]{2,1,0:T(8,128)(2,1)S(1)}, u32[]{:S(2)}) copy-start(bf16[3,1024,128]{2,1,0:T(8,128)(2,1)S(1)} %get-tuple-element.71.pair_own) | copy-start | bytes 2359300
  86.7 6.2 %copy-start.23 = (bf16[3,1024,64]{2,1,0:T(8,128)(2,1)}, bf16[3,1024,64]{2,1,0:T(8,128)(2,1)S(1)}, u32[]{:S(2)}) copy-start(bf16[3,1024,64]{2,1,0:T(8,128)(2,1)S(1)} %get-tuple-element.70.query_ref) | copy-start | bytes 1179652
  86.7 8.0 %collective-permute-start.6 = (bf16[3,1024,128]{2,1,0:T(8,128)(2,1)S(1)}, bf16[3,1024,128]{2,1,0:T(8,128)(2,1)}, u32[]{:S(2)}, u32[]{:S(2)}) collective-permute-start(bf16[3,1024,128]{2,1,0:T(8,128)(2,1)S(1)} %get-tuple-element.71.pair_own), channel_id=1, source_target_pairs={{0,1},{1,0},{2,3},{3,2},{4,5},{5,4},{6,7},{7,6},{8,9},{9,8},{10,11... | collective-permute-start | bytes 2359304 | tf_op jit(solution)/shard_map/ppermute | solution.py:982
  94.7 26.2 %copy-start.2 = (bf16[2,128,768]{2,1,0:T(8,128)(2,1)S(1)}, bf16[2,128,768]{2,1,0:T(8,128)(2,1)}, u32[]{:S(2)}) copy-start(bf16[2,128,768]{2,1,0:T(8,128)(2,1)} %param.25) | copy-start | bytes 1179652
  114.6 18.5 %all-to-all-start.1 = ((bf16[8,192,128]{2,1,0:T(8,128)(2,1)}), bf16[8,192,128]{2,1,0:T(8,128)(2,1)S(1)}, u32[]{:S(2)}, u32[]{:S(2)}) async-start(bf16[8,192,128]{2,1,0:T(8,128)(2,1)} %get-tuple-element.72), calls=%async_computation.1 | async-start | bytes 786432 | tf_op jit(solution)/shard_map/all_to_all | solution.py:1133
  120.9 15.7 %collective-permute-start.9 = (bf16[256,768]{1,0:T(8,128)(2,1)S(1)}, bf16[256,768]{1,0:T(8,128)(2,1)S(1)}, u32[]{:S(2)}, u32[]{:S(2)}) collective-permute-start(bf16[256,768]{1,0:T(8,128)(2,1)S(1)} %bitcast.163), channel_id=1, source_target_pairs={{0,1},{1,0},{2,3},{3,2},{4,5},{5,4},{6,7},{7,6},{8,9},{9,8},{10,11... | collective-permute-start | bytes 1179656 | tf_op jit(solution)/shard_map/ppermute | solution.py:982
  133.1 2.7 copy-start
  135.8 2.7 copy-start.1
  136.5 1.8 collective-permute-start.8
  149.2 1.7 collective-permute-start.10
  154.6 4.3 %collective-permute-start.11 = (bf16[16,24,768]{2,1,0:T(8,128)(2,1)S(1)}, bf16[16,24,768]{2,1,0:T(8,128)(2,1)}, u32[]{:S(2)}, u32[]{:S(2)}) collective-permute-start(bf16[16,24,768]{2,1,0:T(8,128)(2,1)S(1)} %dynamic-slice_bitcast_fusion.3), channel_id=1, source_target_pairs={{0,1},{1,0},{2,3},{3,2},{4,5},{5,4},{6,7},{7,6},{8,9},{9,8},{10,11... | collective-permute-start | bytes 1769480 | tf_op jit(solution)/shard_map/ppermute | solution.py:982
  154.9 28.9 %all-to-all-start.2 = ((bf16[8,192,128]{2,1,0:T(8,128)(2,1)}), bf16[8,192,128]{2,1,0:T(8,128)(2,1)}, u32[]{:S(2)}, u32[]{:S(2)}) async-start(bf16[8,192,128]{2,1,0:T(8,128)(2,1)} %get-tuple-element.93), calls=%async_computation.2 | async-start | bytes 786432 | tf_op jit(solution)/shard_map/all_to_all | solution.py:1150
  179.6 34.1 %collective-permute-start.13 = (bf16[8,352,256]{2,1,0:T(8,128)(2,1)}, bf16[8,352,256]{2,1,0:T(8,128)(2,1)S(1)}, u32[]{:S(2)}, u32[]{:S(2)}) collective-permute-start(bf16[8,352,256]{2,1,0:T(8,128)(2,1)} %get-tuple-element.91), channel_id=1, source_target_pairs={{0,2},{2,0},{1,3},{3,1},{4,6},{6,4},{5,7},{7,5},{8,10},{10,8},{9,1... | collective-permute-start | bytes 4325384 | tf_op jit(solution)/shard_map/ppermute | solution.py:982
  181.5 30.9 %collective-permute-start.14 = (bf16[8,320,256]{2,1,0:T(8,128)(2,1)}, bf16[8,320,256]{2,1,0:T(8,128)(2,1)}, u32[]{:S(2)}, u32[]{:S(2)}) collective-permute-start(bf16[8,320,256]{2,1,0:T(8,128)(2,1)} %copy-done.19), channel_id=1, source_target_pairs={{0,16},{16,0},{1,17},{17,1},{2,18},{18,2},{3,19},{19,3},{4,20},{20... | collective-permute-start | bytes 3932168 | tf_op jit(solution)/shard_map/ppermute | solution.py:982
  183.8 39.7 %collective-permute-start.12 = (bf16[256,768]{1,0:T(8,128)(2,1)}, bf16[256,768]{1,0:T(8,128)(2,1)}, u32[]{:S(2)}, u32[]{:S(2)}) collective-permute-start(bf16[256,768]{1,0:T(8,128)(2,1)} %copy-done.21), channel_id=1, source_target_pairs={{0,1},{1,0},{2,3},{3,2},{4,5},{5,4},{6,7},{7,6},{8,9},{9,8},{10,11... | collective-permute-start | bytes 1179656 | tf_op jit(solution)/shard_map/ppermute | solution.py:982
  183.8 31.0 %copy-start.7 = (bf16[8,352,256]{2,1,0:T(8,128)(2,1)S(1)}, bf16[8,352,256]{2,1,0:T(8,128)(2,1)}, u32[]{:S(2)}) copy-start(bf16[8,352,256]{2,1,0:T(8,128)(2,1)} %copy-done.6) | copy-start | bytes 4325380
  213.6 12.5 %collective-permute-start.15 = (bf16[3,128,1024]{2,1,0:T(8,128)(2,1)}, bf16[3,128,1024]{2,1,0:T(8,128)(2,1)}, u32[]{:S(2)}, u32[]{:S(2)}) collective-permute-start(bf16[3,128,1024]{2,1,0:T(8,128)(2,1)} %get-tuple-element.109), channel_id=1, source_target_pairs={{0,1},{1,0},{2,3},{3,2},{4,5},{5,4},{6,7},{7,6},{8,9},{9,8},{10,11... | collective-permute-start | bytes 2359304 | tf_op jit(solution)/shard_map/ppermute | solution.py:982
  218.2 3.6 %copy-start.24 = (bf16[8,320,256]{2,1,0:T(8,128)(2,1)}, bf16[8,320,256]{2,1,0:T(8,128)(2,1)S(1)}, u32[]{:S(2)}) copy-start(bf16[8,320,256]{2,1,0:T(8,128)(2,1)S(1)} %add_convert_fusion.1) | copy-start | bytes 3932164
  219.3 16.9 %collective-permute-start.19 = (bf16[4,320,256]{2,1,0:T(8,128)(2,1)}, bf16[4,320,256]{2,1,0:T(8,128)(2,1)}, u32[]{:S(2)}, u32[]{:S(2)}) collective-permute-start(bf16[4,320,256]{2,1,0:T(8,128)(2,1)} %dynamic-slice_bitcast_fusion.2), channel_id=1, source_target_pairs={{0,2},{2,0},{1,3},{3,1},{4,6},{6,4},{5,7},{7,5},{8,10},{10,8},{9,1... | collective-permute-start | bytes 1966088 | tf_op jit(solution)/shard_map/ppermute | solution.py:982
  221.8 3.5 %copy-start.35 = (f32[3,1,128]{2,1,0:T(1,128)S(1)}, f32[3,1,128]{2,1,0:T(1,128)}, u32[]{:S(2)}) copy-start(f32[3,1,128]{2,1,0:T(1,128)} %get-tuple-element.101) | copy-start | bytes 4612
  221.8 17.5 %collective-permute-start.18 = (bf16[4,352,256]{2,1,0:T(8,128)(2,1)}, bf16[4,352,256]{2,1,0:T(8,128)(2,1)}, u32[]{:S(2)}, u32[]{:S(2)}) collective-permute-start(bf16[4,352,256]{2,1,0:T(8,128)(2,1)} %dynamic-slice_bitcast_fusion), channel_id=1, source_target_pairs={{0,16},{16,0},{1,17},{17,1},{2,18},{18,2},{3,19},{19,3},{4,20},{20... | collective-permute-start | bytes 2162696 | tf_op jit(solution)/shard_map/ppermute | solution.py:982
  226.2 11.1 %copy-start.25 = (bf16[8,320,256]{2,1,0:T(8,128)(2,1)S(1)}, bf16[8,320,256]{2,1,0:T(8,128)(2,1)}, u32[]{:S(2)}) copy-start(bf16[8,320,256]{2,1,0:T(8,128)(2,1)} %copy-done.24) | copy-start | bytes 3932164
  236.1 6.3 %collective-permute-start.22 = (bf16[2,1,2,4,24,704]{5,4,3,2,1,0:T(8,128)(2,1)}, bf16[2,1,2,4,24,704]{5,4,3,2,1,0:T(8,128)(2,1)S(1)}, u32[]{:S(2)}, u32[]{:S(2)}) collective-permute-start(bf16[2,1,2,4,24,704]{5,4,3,2,1,0:T(8,128)(2,1)} %bitcast.219), channel_id=1, source_target_pairs={{0,1},{1,0},{2,3},{3,2},{4,5},{5,4},{6,7},{7,6},{8,9},{9,8},{10,11... | collective-permute-start | bytes 1622024 | tf_op jit(solution)/shard_map/ppermute | solution.py:982
  236.2 20.2 %collective-permute-start.16 = (bf16[4,128,768]{2,1,0:T(8,128)(2,1)}, bf16[4,128,768]{2,1,0:T(8,128)(2,1)S(1)}, u32[]{:S(2)}, u32[]{:S(2)}) collective-permute-start(bf16[4,128,768]{2,1,0:T(8,128)(2,1)} %get-tuple-element.111), channel_id=1, source_target_pairs={{0,2},{2,0},{1,3},{3,1},{4,6},{6,4},{5,7},{7,5},{8,10},{10,8},{9,1... | collective-permute-start | bytes 2359304 | tf_op jit(solution)/shard_map/ppermute | solution.py:982
  240.8 15.5 %copy-start.27 = (bf16[4,128,768]{2,1,0:T(8,128)(2,1)S(1)}, bf16[4,128,768]{2,1,0:T(8,128)(2,1)}, u32[]{:S(2)}) copy-start(bf16[4,128,768]{2,1,0:T(8,128)(2,1)} %get-tuple-element.110) | copy-start | bytes 2359300
  240.8 17.3 %collective-permute-start.20 = (bf16[2,672,256]{2,1,0:T(8,128)(2,1)S(1)}, bf16[2,672,256]{2,1,0:T(8,128)(2,1)S(1)}, u32[]{:S(2)}, u32[]{:S(2)}) collective-permute-start(bf16[2,672,256]{2,1,0:T(8,128)(2,1)S(1)} %dynamic-slice_bitcast_fusion.1), channel_id=1, source_target_pairs={{0,4},{4,0},{1,5},{5,1},{2,6},{6,2},{3,7},{7,3},{8,12},{12,8},{9,1... | collective-permute-start | bytes 2064392 | tf_op jit(solution)/shard_map/ppermute | solution.py:982
  242.6 18.3 %collective-permute-start.23 = (bf16[1,2,4,24,704]{4,3,2,1,0:T(8,128)(2,1)S(1)}, bf16[1,2,4,24,704]{4,3,2,1,0:T(8,128)(2,1)S(1)}, u32[]{:S(2)}, u32[]{:S(2)}) collective-permute-start(bf16[1,2,4,24,704]{4,3,2,1,0:T(8,128)(2,1)S(1)} %dynamic-slice_bitcast_fusion.6), channel_id=1, source_target_pairs={{0,16},{16,0},{1,17},{17,1},{2,18},{18,2},{3,19},{19,3},{4,20},{20... | collective-permute-start | bytes 811016 | tf_op jit(solution)/shard_map/ppermute | solution.py:982
  256.6 18.6 %collective-permute-start.17 = (bf16[2,128,768]{2,1,0:T(8,128)(2,1)S(1)}, bf16[2,128,768]{2,1,0:T(8,128)(2,1)S(1)}, u32[]{:S(2)}, u32[]{:S(2)}) collective-permute-start(bf16[2,128,768]{2,1,0:T(8,128)(2,1)S(1)} %dynamic-slice_bitcast_fusion.4), channel_id=1, source_target_pairs={{0,4},{4,0},{1,5},{5,1},{2,6},{6,2},{3,7},{7,3},{8,12},{12,8},{9,1... | collective-permute-start | bytes 1179656 | tf_op jit(solution)/shard_map/ppermute | solution.py:982
  258.4 24.7 %collective-permute-start.25 = (bf16[672,256]{1,0:T(8,128)(2,1)S(1)}, bf16[672,256]{1,0:T(8,128)(2,1)S(1)}, u32[]{:S(2)}, u32[]{:S(2)}) collective-permute-start(bf16[672,256]{1,0:T(8,128)(2,1)S(1)} %dynamic-slice_bitcast_fusion.5), channel_id=1, source_target_pairs={{0,8},{8,0},{1,9},{9,1},{2,10},{10,2},{3,11},{11,3},{4,12},{12,4},... | collective-permute-start | bytes 1032200 | tf_op jit(solution)/shard_map/ppermute | solution.py:982
  260.9 21.5 %collective-permute-start.24 = (bf16[1,4,24,704]{3,2,1,0:T(8,128)(2,1)S(1)}, bf16[1,4,24,704]{3,2,1,0:T(8,128)(2,1)S(1)}, u32[]{:S(2)}, u32[]{:S(2)}) collective-permute-start(bf16[1,4,24,704]{3,2,1,0:T(8,128)(2,1)S(1)} %dynamic-slice_bitcast_fusion.10), channel_id=1, source_target_pairs={{0,8},{8,0},{1,9},{9,1},{2,10},{10,2},{3,11},{11,3},{4,12},{12,4},... | collective-permute-start | bytes 405512 | tf_op jit(solution)/shard_map/ppermute | solution.py:982
  283.2 10.3 %collective-permute-start.21 = (bf16[128,768]{1,0:T(8,128)(2,1)S(1)}, bf16[128,768]{1,0:T(8,128)(2,1)S(1)}, u32[]{:S(2)}, u32[]{:S(2)}) collective-permute-start(bf16[128,768]{1,0:T(8,128)(2,1)S(1)} %get-tuple-element.136), channel_id=1, source_target_pairs={{0,8},{8,0},{1,9},{9,1},{2,10},{10,2},{3,11},{11,3},{4,12},{12,4},... | collective-permute-start | bytes 589832 | tf_op jit(solution)/shard_map/ppermute | solution.py:982
  283.4 6.2 %collective-permute-start.26 = (bf16[8,24,256]{2,1,0:T(8,128)(2,1)S(1)}, bf16[8,24,256]{2,1,0:T(8,128)(2,1)S(1)}, u32[]{:S(2)}, u32[]{:S(2)}) collective-permute-start(bf16[8,24,256]{2,1,0:T(8,128)(2,1)S(1)} %get-tuple-element.143), channel_id=1, source_target_pairs={{0,1},{1,0},{2,3},{3,2},{4,5},{5,4},{6,7},{7,6},{8,9},{9,8},{10,11... | collective-permute-start | bytes 294920 | tf_op jit(solution)/shard_map/ppermute | solution.py:982
  285.0 10.0 %all-to-all-start.3 = ((bf16[4,24,704]{2,1,0:T(8,128)(2,1)}), bf16[4,24,704]{2,1,0:T(8,128)(2,1)S(1)}, u32[]{:S(2)}, u32[]{:S(2)}) async-start(bf16[4,24,704]{2,1,0:T(8,128)(2,1)} %bitcast.66), calls=%async_computation.3 | async-start | bytes 294912 | tf_op jit(solution)/shard_map/all_to_all | solution.py:1251
  290.0 3.5 %copy-start.18 = (f32[256,768]{1,0:T(8,128)S(1)}, f32[256,768]{1,0:T(8,128)}, u32[]{:S(2)}) copy-start(f32[256,768]{1,0:T(8,128)} %copy-done.17) | copy-start | bytes 2359300
  (23 other events, 28.5 us)
Sparse Core Ops, SparseCore 0:
  15.4 105.3 all-gather.1

commit v4 on v3

--- a/solution.py
+++ b/solution.py
@@ -868,7 +868,7 @@
             jax.ShapeDtypeStruct((half, model), bf16),
         ]
         + [jax.ShapeDtypeStruct(size, bf16) for size in grads],
-        compiler_params=vmem_limit(40),
+        compiler_params=vmem_limit(60),
         cost_estimate=pl.CostEstimate(
             flops=8 * 2 * half * model * units, bytes_accessed=12 * model * units, transcendentals=0
         ),

time: 305 us -> 299 us (0.980)
  local copies, waits for them, and re-layouts: 32.4 us -> 27 us
    unnamed x82 -> x78, local copies, waits for them, and re-layouts: 17.8 us -> 12.4 us
  transfers between devices with their start and end apart: 32 -> 32, of which waited for: 18 -> 18; matrix products, arithmetic and copies ran while one was open for 9% -> 9% of each run, Pallas kernels for 24% -> 25%
where the time goes in v4:
time: 299 us; the launch traced here: 298 us
  waiting for transfers between devices  101 us (34%)
  Pallas kernels  86.7 us (29%)
  starting transfers between devices  48.2 us (16%)
  local copies, waits for them, and re-layouts  27 us (9%)
  other arithmetic  19.5 us (7%)
  between operations  15 us (5%)
    ppermute x27, waiting for transfers between devices, swap(): return lax.ppermute(value, axis, [(0, 1), (1, 0)])  84.3 us
    ppermute x27, starting transfers between devices, swap(): return lax.ppermute(value, axis, [(0, 1), (1, 0)])  28 us
    pallas_call x1, Pallas kernels, attend_back(): pl.pallas_call(functools.partial(attend_back_kernel, tile, chunk), grid_s...  24.5 us
    pallas_call x1, Pallas kernels, attend(): pl.pallas_call(functools.partial(attend_kernel, tile, chunk), grid_spec=p...  19.9 us
    pallas_call x1, Pallas kernels, hidden_back(): pl.pallas_call(functools.partial(hidden_back_kernel, shape), grid_spec=pl...  15 us
    unnamed x78, local copies, waits for them, and re-layouts  12.4 us
    all_to_all x1, waiting for transfers between devices, body(): context = lax.all_to_all(context_own, owners, 0, 0, tiled=True)  12 us
    pallas_call x1, Pallas kernels, project_back(): pl.pallas_call(project_back_kernel, grid_spec=pltpu.PrefetchScalarGridSpe...  9.77 us
  transfers between devices with their start and end apart: 32, of which 18 were waited for; matrix products, arithmetic and copies ran while one was open for 9% of the time, Pallas kernels for 25%

profile of v4, /device:TPU:0, one launch (start us, length us, event | category | flops | bytes accessed | tf_op | source)
XLA Modules:
  0.0 298.4 jit_solution(9158722914736039842)
XLA Ops:
  9.5 2.5 dynamic-slice_reduce_fusion.2
  16.6 5.1 %all-to-all-start = ((bf16[4,24,704]{2,1,0:T(8,128)(2,1)}), bf16[4,24,704]{2,1,0:T(8,128)(2,1)S(1)}, u32[]{:S(2)}, u32[]{:S(2)}) async-start(bf16[4,24,704]{2,1,0:T(8,128)(2,1)} %pad_maximum_fusion.6), calls=%async_computation | async-start | bytes 294912 | tf_op jit(solution)/shard_map/all_to_all | solution.py:1062
  21.8 2.7 collective-permute-start
  24.4 4.2 %all-to-all-done = bf16[4,24,704]{2,1,0:T(8,128)(2,1)S(1)} async-done(((bf16[4,24,704]{2,1,0:T(8,128)(2,1)}), bf16[4,24,704]{2,1,0:T(8,128)(2,1)S(1)}, u32[]{:S(2)}, u32[]{:S(2)}) %all-to-all-start) | async-done | bytes 135200 | tf_op jit(solution)/shard_map/all_to_all | solution.py:1062
  28.6 1.2 collective-permute-start.3
  29.8 13.6 %collective-permute-done = bf16[128,768]{1,0:T(8,128)(2,1)S(1)} collective-permute-done((bf16[128,768]{1,0:T(8,128)(2,1)S(1)}, bf16[128,768]{1,0:T(8,128)(2,1)S(1)}, u32[]{:S(2)}, u32[]{:S(2)}) %collective-permute-start) | collective-permute-done | bytes 196640 | tf_op jit(solution)/shard_map/ppermute | solution.py:982
  43.6 4.3 %collective-permute-done.3 = bf16[4,24,704]{2,1,0:T(8,128)(2,1)S(1)} collective-permute-done((bf16[4,24,704]{2,1,0:T(8,128)(2,1)S(1)}, bf16[4,24,704]{2,1,0:T(8,128)(2,1)S(1)}, u32[]{:S(2)}, u32[]{:S(2)}) %collective-permute-start.3) | collective-permute-done | bytes 135200 | tf_op jit(solution)/shard_map/ppermute | solution.py:982
  48.0 1.6 collective-permute-start.4
  49.6 10.0 %collective-permute-done.1 = bf16[2,128,768]{2,1,0:T(8,128)(2,1)S(1)} collective-permute-done((bf16[2,128,768]{2,1,0:T(8,128)(2,1)S(1)}, bf16[2,128,768]{2,1,0:T(8,128)(2,1)S(1)}, u32[]{:S(2)}, u32[]{:S(2)}) %collective-permute-start.1) | collective-permute-done | bytes 393248 | tf_op jit(solution)/shard_map/ppermute | solution.py:982
  59.8 4.8 %collective-permute-start.2 = (bf16[2,2,128,768]{3,2,0,1:T(8,128)(2,1)S(1)}, bf16[2,2,128,768]{3,2,0,1:T(8,128)(2,1)S(1)}, u32[]{:S(2)}, u32[]{:S(2)}) collective-permute-start(bf16[2,2,128,768]{3,2,0,1:T(8,128)(2,1)S(1)} %maximum_select_fusion.3), channel_id=1, source_target_pairs={{0,2},{2,0},{1,3},{3,1},{4,6},{6,4},{5,7},{7,5},{8,10},{10,8},{9,1... | collective-permute-start | bytes 2359304 | tf_op jit(solution)/shard_map/ppermute | solution.py:982
  65.9 1.9 collective-permute-done.5
  67.8 1.5 maximum_select_fusion.1
  69.6 12.8 %collective-permute-done.2 = bf16[2,2,128,768]{3,2,0,1:T(8,128)(2,1)S(1)} collective-permute-done((bf16[2,2,128,768]{3,2,0,1:T(8,128)(2,1)S(1)}, bf16[2,2,128,768]{3,2,0,1:T(8,128)(2,1)S(1)}, u32[]{:S(2)}, u32[]{:S(2)}) %collective-permute-start.2) | collective-permute-done | bytes 786464 | tf_op jit(solution)/shard_map/ppermute | solution.py:982
  82.8 2.7 project.1
  87.6 2.7 fusion.hot_ref
  91.8 2.0 skew.1.table
  93.8 1.7 copy-done.4
  96.4 19.9 %attend.1 = (bf16[8,192,128]{2,1,0:T(8,128)(2,1)}, bf16[3,1024,2048]{2,1,0:T(8,128)(2,1)}, f32[3,1024,128]{2,1,0:T(8,128)}, f32[3,8,1,128]{3,2,1,0:T(1,128)}) custom-call(s32[2]{0:T(128)} %pad_add_fusion.place_ref, bf16[3,1024,64]{2,1,0:T(8,128)(2,1)} %copy-done.16, bf16[3,1024,128]{2,1,0:T(8,128)(2,1)} %copy-done.14, bf16[3,1024,128]{2,1,0:T(8,128)(2,1)} %copy-done.34, ...), custom_call_target="tpu_custom_call" | custom-call | flops 6442450944 | bytes 12582912 | tf_op jit(solution)/shard_map/attend/pallas_call | solution.py:207
  116.3 6.3 %all-to-all-start.1 = ((bf16[8,192,128]{2,1,0:T(8,128)(2,1)}), bf16[8,192,128]{2,1,0:T(8,128)(2,1)S(1)}, u32[]{:S(2)}, u32[]{:S(2)}) async-start(bf16[8,192,128]{2,1,0:T(8,128)(2,1)} %get-tuple-element.72), calls=%async_computation.1 | async-start | bytes 786432 | tf_op jit(solution)/shard_map/all_to_all | solution.py:1133
  122.8 12.0 %all-to-all-done.1.context_ref = bf16[8,192,128]{2,1,0:T(8,128)(2,1)S(1)} async-done(((bf16[8,192,128]{2,1,0:T(8,128)(2,1)}), bf16[8,192,128]{2,1,0:T(8,128)(2,1)S(1)}, u32[]{:S(2)}, u32[]{:S(2)}) %all-to-all-start.1) | async-done | bytes 393248 | tf_op jit(solution)/shard_map/all_to_all | solution.py:1133
  134.9 2.7 copy-done
  138.4 1.7 collective-permute-done.8.normed_other
  140.5 7.8 %hidden_stage.1 = (f32[256,768]{1,0:T(8,128)S(1)}, bf16[256,768]{1,0:T(8,128)(2,1)S(1)}, bf16[512,1024]{1,0:T(8,128)(2,1)S(1)}, bf16[512,1024]{1,0:T(8,128)(2,1)S(1)}, bf16[512,1024]{1,0:T(8,128)(2,1)S(1)}) custom-call(bf16[256,768]{1,0:T(8,128)(2,1)S(1)} %get-tuple-element.74.normed_own, bf16[256,768]{1,0:T(8,128)(2,1)S(1)} %collective-permute-done.8.normed_other, ...), custom_call_target="tpu_custom_call" | custom-call | flops 4026531840 | bytes 9437184 | tf_op jit(solution)/shard_map/hidden_stage/pallas_call | solution.py:814
  150.2 1.7 collective-permute-done.10.norm_other
  152.0 2.4 output_back.1
  156.1 3.6 %all-to-all-start.2 = ((bf16[8,192,128]{2,1,0:T(8,128)(2,1)}), bf16[8,192,128]{2,1,0:T(8,128)(2,1)S(1)}, u32[]{:S(2)}, u32[]{:S(2)}) async-start(bf16[8,192,128]{2,1,0:T(8,128)(2,1)} %get-tuple-element.93), calls=%async_computation.2 | async-start | bytes 786432 | tf_op jit(solution)/shard_map/all_to_all | solution.py:1150
  159.8 2.1 fusion.6.output_ref
  161.8 15.0 %hidden_back.1 = (f32[256,768]{1,0:T(8,128)}, bf16[256,768]{1,0:T(8,128)(2,1)}, bf16[8,352,256]{2,1,0:T(8,128)(2,1)}, bf16[8,352,256]{2,1,0:T(8,128)(2,1)}, bf16...) custom-call(s32[2]{0:T(128)} %pad_add_fusion.1.place_ref, bf16[256,768]{1,0:T(8,128)(2,1)} %copy-done.7, ...), custom_call_target="tpu_custom_call" | custom-call | flops 3221225472 | bytes 9437184 | tf_op jit(solution)/shard_map/hidden_back/pallas_call | solution.py:850
  176.8 2.0 collective-permute-start.13
  179.4 1.6 collective-permute-start.14
  182.4 24.5 %attend_back.1 = (bf16[3,1024,64]{2,1,0:T(8,128)(2,1)}, bf16[3,128,1024]{2,1,0:T(8,128)(2,1)}, bf16[3,128,1024]{2,1,0:T(8,128)(2,1)}, f32[3,1,128]{2,1,0:T(1,128)}) custom-call(s32[2]{0:T(128)} %pad_add_fusion.place_ref, bf16[8,192,128]{2,1,0:T(8,128)(2,1)} %copy-done.24, f32[3,1024,128]{2,1,0:T(8,128)} %get-tuple-element.94.kept_ref, ...), custom_call_target="tpu_custom_call" | custom-call | flops 12884901888 | bytes 12582912 | tf_op jit(solution)/shard_map/attend_back/pallas_call | solution.py:343
  206.8 3.1 %collective-permute-done.14 = bf16[8,320,256]{2,1,0:T(8,128)(2,1)} collective-permute-done((bf16[8,320,256]{2,1,0:T(8,128)(2,1)}, bf16[8,320,256]{2,1,0:T(8,128)(2,1)}, u32[]{:S(2)}, u32[]{:S(2)}) %collective-permute-start.14) | collective-permute-done | bytes 1310752 | tf_op jit(solution)/shard_map/ppermute | solution.py:982
  212.0 1.6 add_convert_fusion.1
  214.6 1.6 collective-permute-start.19
  217.2 1.6 collective-permute-start.18
  218.8 1.9 add_convert_fusion.3
  221.5 9.8 %project_back.1 = (bf16[4,128,768]{2,1,0:T(8,128)(2,1)}, bf16[4,128,768]{2,1,0:T(8,128)(2,1)}, bf16[16,24,704]{2,1,0:T(8,128)(2,1)}, bf16[16,24,704]{2,1,0:T(8,128)(2,1)}) custom-call(s32[2]{0:T(128)} %pad_add_fusion.2.place_ref, bf16[1024,768]{1,0:T(8,128)(2,1)} %copy-done.15, bf16[768,704]{1,0:T(8,128)(2,1)} %bitcast.170, f32[8,768]{1,0:T(8,128)} %stack.227.extra_ref, ...), custom_call_target="tpu_custom_call" | custom-call | flops 1811939328 | bytes 9437184 | tf_op jit(solution)/shard_map/project_back/pallas_call | solution.py:474
  232.1 1.6 collective-permute-start.16
  233.7 1.3 fusion.4
  236.1 1.5 collective-permute-start.20
  237.8 1.7 collective-permute-start.23
  239.4 12.1 %collective-permute-done.16 = bf16[4,128,768]{2,1,0:T(8,128)(2,1)S(1)} collective-permute-done((bf16[4,128,768]{2,1,0:T(8,128)(2,1)}, bf16[4,128,768]{2,1,0:T(8,128)(2,1)S(1)}, u32[]{:S(2)}, u32[]{:S(2)}) %collective-permute-start.16) | collective-permute-done | bytes 786464 | tf_op jit(solution)/shard_map/ppermute | solution.py:982
  251.8 1.6 collective-permute-start.17
  253.7 2.5 collective-permute-start.25
  256.8 12.8 %collective-permute-done.17 = bf16[2,128,768]{2,1,0:T(8,128)(2,1)S(1)} collective-permute-done((bf16[2,128,768]{2,1,0:T(8,128)(2,1)S(1)}, bf16[2,128,768]{2,1,0:T(8,128)(2,1)S(1)}, u32[]{:S(2)}, u32[]{:S(2)}) %collective-permute-start.17) | collective-permute-done | bytes 393248 | tf_op jit(solution)/shard_map/ppermute | solution.py:982
  269.8 7.1 %collective-permute-done.24 = bf16[1,4,24,704]{3,2,1,0:T(8,128)(2,1)S(1)} collective-permute-done((bf16[1,4,24,704]{3,2,1,0:T(8,128)(2,1)S(1)}, bf16[1,4,24,704]{3,2,1,0:T(8,128)(2,1)S(1)}, u32[]{:S(2)}, u32[]{:S(2)}) %collective-permute-start.24) | collective-permute-done | bytes 135200 | tf_op jit(solution)/shard_map/ppermute | solution.py:982
  279.5 5.1 %all-to-all-start.3 = ((bf16[4,24,704]{2,1,0:T(8,128)(2,1)}), bf16[4,24,704]{2,1,0:T(8,128)(2,1)S(1)}, u32[]{:S(2)}, u32[]{:S(2)}) async-start(bf16[4,24,704]{2,1,0:T(8,128)(2,1)} %bitcast.66), calls=%async_computation.3 | async-start | bytes 294912 | tf_op jit(solution)/shard_map/all_to_all | solution.py:1251
  287.6 1.2 rows_stage.1
  (211 shorter events, 36.6 us)
Async XLA Ops:
  7.2 5.4 %copy-start.29 = (bf16[24,768]{1,0:T(8,128)(2,1)S(1)}, bf16[24,768]{1,0:T(8,128)(2,1)}, u32[]{:S(2)}) copy-start(bf16[24,768]{1,0:T(8,128)(2,1)} %param.17) | copy-start | bytes 110596
  7.2 127.7 %all-gather.2.cloned.1.call-start = ((), (), s32[]{:S(2)}) async-start(), calls=%async_computation.4 | async-start | bytes 6266880 | tf_op jit(solution)/shard_map/all_gather | solution.py:1099
  7.2 5.9 %copy-start.25 = (bf16[64,768]{1,0:T(8,128)(2,1)S(1)}, bf16[64,768]{1,0:T(8,128)(2,1)}, u32[]{:S(2)}) copy-start(bf16[64,768]{1,0:T(8,128)(2,1)} %param.20) | copy-start | bytes 294916
  12.6 1.5 collective-permute-start.7
  14.4 7.3 %copy-start.3 = (bf16[2,128,768]{2,1,0:T(8,128)(2,1)S(1)}, bf16[2,128,768]{2,1,0:T(8,128)(2,1)}, u32[]{:S(2)}) copy-start(bf16[2,128,768]{2,1,0:T(8,128)(2,1)} %token_ref.3) | copy-start | bytes 1179652
  16.6 12.0 %all-to-all-start = ((bf16[4,24,704]{2,1,0:T(8,128)(2,1)}), bf16[4,24,704]{2,1,0:T(8,128)(2,1)S(1)}, u32[]{:S(2)}, u32[]{:S(2)}) async-start(bf16[4,24,704]{2,1,0:T(8,128)(2,1)} %pad_maximum_fusion.6), calls=%async_computation | async-start | bytes 294912 | tf_op jit(solution)/shard_map/all_to_all | solution.py:1062
  21.8 21.7 %collective-permute-start = (bf16[128,768]{1,0:T(8,128)(2,1)S(1)}, bf16[128,768]{1,0:T(8,128)(2,1)S(1)}, u32[]{:S(2)}, u32[]{:S(2)}) collective-permute-start(bf16[128,768]{1,0:T(8,128)(2,1)S(1)} %get-tuple-element.139), channel_id=1, source_target_pairs={{0,8},{8,0},{1,9},{9,1},{2,10},{10,2},{3,11},{11,3},{4,12},{12,4},... | collective-permute-start | bytes 589832 | tf_op jit(solution)/shard_map/ppermute | solution.py:982
  28.6 19.3 %collective-permute-start.3 = (bf16[4,24,704]{2,1,0:T(8,128)(2,1)S(1)}, bf16[4,24,704]{2,1,0:T(8,128)(2,1)S(1)}, u32[]{:S(2)}, u32[]{:S(2)}) collective-permute-start(bf16[4,24,704]{2,1,0:T(8,128)(2,1)S(1)} %all-to-all-done), channel_id=1, source_target_pairs={{0,8},{8,0},{1,9},{9,1},{2,10},{10,2},{3,11},{11,3},{4,12},{12,4},... | collective-permute-start | bytes 405512 | tf_op jit(solution)/shard_map/ppermute | solution.py:982
  43.5 16.2 %collective-permute-start.1 = (bf16[2,128,768]{2,1,0:T(8,128)(2,1)S(1)}, bf16[2,128,768]{2,1,0:T(8,128)(2,1)S(1)}, u32[]{:S(2)}, u32[]{:S(2)}) collective-permute-start(bf16[2,128,768]{2,1,0:T(8,128)(2,1)S(1)} %maximum_select_fusion.6), channel_id=1, source_target_pairs={{0,4},{4,0},{1,5},{5,1},{2,6},{6,2},{3,7},{7,3},{8,12},{12,8},{9,1... | collective-permute-start | bytes 1179656 | tf_op jit(solution)/shard_map/ppermute | solution.py:982
  48.0 16.6 %collective-permute-start.4 = (bf16[2,4,24,704]{3,2,1,0:T(8,128)(2,1)S(1)}, bf16[2,4,24,704]{3,2,1,0:T(8,128)(2,1)S(1)}, u32[]{:S(2)}, u32[]{:S(2)}) collective-permute-start(bf16[2,4,24,704]{3,2,1,0:T(8,128)(2,1)S(1)} %maximum_select_fusion.9), channel_id=1, source_target_pairs={{0,16},{16,0},{1,17},{17,1},{2,18},{18,2},{3,19},{19,3},{4,20},{20... | collective-permute-start | bytes 811016 | tf_op jit(solution)/shard_map/ppermute | solution.py:982
  59.7 5.8 %copy-start.30 = (s32[4095]{0:T(1024)S(1)}, s32[4095]{0:T(1024)}, u32[]{:S(2)}) copy-start(s32[4095]{0:T(1024)} %param.24) | copy-start | bytes 49144
  59.8 22.6 %collective-permute-start.2 = (bf16[2,2,128,768]{3,2,0,1:T(8,128)(2,1)S(1)}, bf16[2,2,128,768]{3,2,0,1:T(8,128)(2,1)S(1)}, u32[]{:S(2)}, u32[]{:S(2)}) collective-permute-start(bf16[2,2,128,768]{3,2,0,1:T(8,128)(2,1)S(1)} %maximum_select_fusion.3), channel_id=1, source_target_pairs={{0,2},{2,0},{1,3},{3,1},{4,6},{6,4},{5,7},{7,5},{8,10},{10,8},{9,1... | collective-permute-start | bytes 2359304 | tf_op jit(solution)/shard_map/ppermute | solution.py:982
  65.5 2.3 collective-permute-start.5
  69.3 21.6 %copy-start.5 = (bf16[2,2,4,2,24,704]{5,4,3,2,1,0:T(8,128)(2,1)}, bf16[2,2,4,2,24,704]{5,4,3,2,1,0:T(8,128)(2,1)S(1)}, u32[]{:S(2)}) copy-start(bf16[2,2,4,2,24,704]{5,4,3,2,1,0:T(8,128)(2,1)S(1)} %maximum_select_fusion.1) | copy-start | bytes 3244036
  87.6 6.2 %copy-start.14 = (bf16[3,1024,128]{2,1,0:T(8,128)(2,1)}, bf16[3,1024,128]{2,1,0:T(8,128)(2,1)S(1)}, u32[]{:S(2)}) copy-start(bf16[3,1024,128]{2,1,0:T(8,128)(2,1)S(1)} %get-tuple-element.71.pair_own) | copy-start | bytes 2359300
  87.6 7.9 %collective-permute-start.6 = (bf16[3,1024,128]{2,1,0:T(8,128)(2,1)S(1)}, bf16[3,1024,128]{2,1,0:T(8,128)(2,1)S(1)}, u32[]{:S(2)}, u32[]{:S(2)}) collective-permute-start(bf16[3,1024,128]{2,1,0:T(8,128)(2,1)S(1)} %get-tuple-element.71.pair_own), channel_id=1, source_target_pairs={{0,1},{1,0},{2,3},{3,2},{4,5},{5,4},{6,7},{7,6},{8,9},{9,8},{10,11... | collective-permute-start | bytes 2359304 | tf_op jit(solution)/shard_map/ppermute | solution.py:982
  96.4 26.1 %copy-start.2 = (bf16[2,128,768]{2,1,0:T(8,128)(2,1)S(1)}, bf16[2,128,768]{2,1,0:T(8,128)(2,1)}, u32[]{:S(2)}) copy-start(bf16[2,128,768]{2,1,0:T(8,128)(2,1)} %param.25) | copy-start | bytes 1179652
  116.3 18.6 %all-to-all-start.1 = ((bf16[8,192,128]{2,1,0:T(8,128)(2,1)}), bf16[8,192,128]{2,1,0:T(8,128)(2,1)S(1)}, u32[]{:S(2)}, u32[]{:S(2)}) async-start(bf16[8,192,128]{2,1,0:T(8,128)(2,1)} %get-tuple-element.72), calls=%async_computation.1 | async-start | bytes 786432 | tf_op jit(solution)/shard_map/all_to_all | solution.py:1133
  122.5 15.8 %collective-permute-start.9 = (bf16[256,768]{1,0:T(8,128)(2,1)S(1)}, bf16[256,768]{1,0:T(8,128)(2,1)S(1)}, u32[]{:S(2)}, u32[]{:S(2)}) collective-permute-start(bf16[256,768]{1,0:T(8,128)(2,1)S(1)} %bitcast.164), channel_id=1, source_target_pairs={{0,1},{1,0},{2,3},{3,2},{4,5},{5,4},{6,7},{7,6},{8,9},{9,8},{10,11... | collective-permute-start | bytes 1179656 | tf_op jit(solution)/shard_map/ppermute | solution.py:982
  138.3 10.0 %copy-start.7 = (bf16[256,768]{1,0:T(8,128)(2,1)}, bf16[256,768]{1,0:T(8,128)(2,1)S(1)}, u32[]{:S(2)}) copy-start(bf16[256,768]{1,0:T(8,128)(2,1)S(1)} %get-tuple-element.74.normed_own) | copy-start | bytes 1179652
  138.3 1.8 collective-permute-start.8
  138.4 9.9 %copy-start.6 = (bf16[256,768]{1,0:T(8,128)(2,1)}, bf16[256,768]{1,0:T(8,128)(2,1)S(1)}, u32[]{:S(2)}) copy-start(bf16[256,768]{1,0:T(8,128)(2,1)S(1)} %collective-permute-done.9.down_other) | copy-start | bytes 1179652
  140.5 7.8 %copy-start.8 = (bf16[256,768]{1,0:T(8,128)(2,1)}, bf16[256,768]{1,0:T(8,128)(2,1)S(1)}, u32[]{:S(2)}) copy-start(bf16[256,768]{1,0:T(8,128)(2,1)S(1)} %collective-permute-done.8.normed_other) | copy-start | bytes 1179652
  150.2 4.1 %copy-start.11 = (bf16[512,1024]{1,0:T(8,128)(2,1)}, bf16[512,1024]{1,0:T(8,128)(2,1)S(1)}, u32[]{:S(2)}) copy-start(bf16[512,1024]{1,0:T(8,128)(2,1)S(1)} %get-tuple-element.84.upper_ref) | copy-start | bytes 3145732
  150.2 1.7 collective-permute-start.10
  155.3 4.4 %collective-permute-start.11 = (bf16[16,24,768]{2,1,0:T(8,128)(2,1)S(1)}, bf16[16,24,768]{2,1,0:T(8,128)(2,1)}, u32[]{:S(2)}, u32[]{:S(2)}) collective-permute-start(bf16[16,24,768]{2,1,0:T(8,128)(2,1)S(1)} %dynamic-slice_bitcast_fusion.3), channel_id=1, source_target_pairs={{0,1},{1,0},{2,3},{3,2},{4,5},{5,4},{6,7},{7,6},{8,9},{9,8},{10,11... | collective-permute-start | bytes 1769480 | tf_op jit(solution)/shard_map/ppermute | solution.py:982
  156.1 25.5 %all-to-all-start.2 = ((bf16[8,192,128]{2,1,0:T(8,128)(2,1)}), bf16[8,192,128]{2,1,0:T(8,128)(2,1)S(1)}, u32[]{:S(2)}, u32[]{:S(2)}) async-start(bf16[8,192,128]{2,1,0:T(8,128)(2,1)} %get-tuple-element.93), calls=%async_computation.2 | async-start | bytes 786432 | tf_op jit(solution)/shard_map/all_to_all | solution.py:1150
  176.8 33.9 %collective-permute-start.13 = (bf16[8,352,256]{2,1,0:T(8,128)(2,1)}, bf16[8,352,256]{2,1,0:T(8,128)(2,1)S(1)}, u32[]{:S(2)}, u32[]{:S(2)}) collective-permute-start(bf16[8,352,256]{2,1,0:T(8,128)(2,1)} %get-tuple-element.91), channel_id=1, source_target_pairs={{0,2},{2,0},{1,3},{3,1},{4,6},{6,4},{5,7},{7,5},{8,10},{10,8},{9,1... | collective-permute-start | bytes 4325384 | tf_op jit(solution)/shard_map/ppermute | solution.py:982
  179.4 30.6 %collective-permute-start.14 = (bf16[8,320,256]{2,1,0:T(8,128)(2,1)}, bf16[8,320,256]{2,1,0:T(8,128)(2,1)}, u32[]{:S(2)}, u32[]{:S(2)}) collective-permute-start(bf16[8,320,256]{2,1,0:T(8,128)(2,1)} %get-tuple-element.92), channel_id=1, source_target_pairs={{0,16},{16,0},{1,17},{17,1},{2,18},{18,2},{3,19},{19,3},{4,20},{20... | collective-permute-start | bytes 3932168 | tf_op jit(solution)/shard_map/ppermute | solution.py:982
  181.6 37.2 %collective-permute-start.12 = (bf16[256,768]{1,0:T(8,128)(2,1)}, bf16[256,768]{1,0:T(8,128)(2,1)}, u32[]{:S(2)}, u32[]{:S(2)}) collective-permute-start(bf16[256,768]{1,0:T(8,128)(2,1)} %get-tuple-element.87), channel_id=1, source_target_pairs={{0,1},{1,0},{2,3},{3,2},{4,5},{5,4},{6,7},{7,6},{8,9},{9,8},{10,11... | collective-permute-start | bytes 1179656 | tf_op jit(solution)/shard_map/ppermute | solution.py:982
  182.4 28.3 %copy-start.19 = (bf16[8,352,256]{2,1,0:T(8,128)(2,1)S(1)}, bf16[8,352,256]{2,1,0:T(8,128)(2,1)}, u32[]{:S(2)}) copy-start(bf16[8,352,256]{2,1,0:T(8,128)(2,1)} %get-tuple-element.102) | copy-start | bytes 4325380
  210.7 10.8 %collective-permute-start.15 = (bf16[3,128,1024]{2,1,0:T(8,128)(2,1)}, bf16[3,128,1024]{2,1,0:T(8,128)(2,1)}, u32[]{:S(2)}, u32[]{:S(2)}) collective-permute-start(bf16[3,128,1024]{2,1,0:T(8,128)(2,1)} %get-tuple-element.109), channel_id=1, source_target_pairs={{0,1},{1,0},{2,3},{3,2},{4,5},{5,4},{6,7},{7,6},{8,9},{9,8},{10,11... | collective-permute-start | bytes 2359304 | tf_op jit(solution)/shard_map/ppermute | solution.py:982
  211.1 5.1 %copy-start.17 = (bf16[8,352,256]{2,1,0:T(8,128)(2,1)}, bf16[8,352,256]{2,1,0:T(8,128)(2,1)S(1)}, u32[]{:S(2)}) copy-start(bf16[8,352,256]{2,1,0:T(8,128)(2,1)S(1)} %add_convert_fusion) | copy-start | bytes 4325380
  213.7 5.1 %copy-start.21 = (f32[256,768]{1,0:T(8,128)S(1)}, f32[256,768]{1,0:T(8,128)}, u32[]{:S(2)}) copy-start(f32[256,768]{1,0:T(8,128)} %get-tuple-element.86) | copy-start | bytes 2359300
  214.6 17.5 %collective-permute-start.19 = (bf16[4,320,256]{2,1,0:T(8,128)(2,1)}, bf16[4,320,256]{2,1,0:T(8,128)(2,1)}, u32[]{:S(2)}, u32[]{:S(2)}) collective-permute-start(bf16[4,320,256]{2,1,0:T(8,128)(2,1)} %dynamic-slice_bitcast_fusion.2), channel_id=1, source_target_pairs={{0,2},{2,0},{1,3},{3,1},{4,6},{6,4},{5,7},{7,5},{8,10},{10,8},{9,1... | collective-permute-start | bytes 1966088 | tf_op jit(solution)/shard_map/ppermute | solution.py:982
  217.2 18.5 %collective-permute-start.18 = (bf16[4,352,256]{2,1,0:T(8,128)(2,1)}, bf16[4,352,256]{2,1,0:T(8,128)(2,1)S(1)}, u32[]{:S(2)}, u32[]{:S(2)}) collective-permute-start(bf16[4,352,256]{2,1,0:T(8,128)(2,1)} %dynamic-slice_bitcast_fusion), channel_id=1, source_target_pairs={{0,16},{16,0},{1,17},{17,1},{2,18},{18,2},{3,19},{19,3},{4,20},{20... | collective-permute-start | bytes 2162696 | tf_op jit(solution)/shard_map/ppermute | solution.py:982
  231.3 4.4 %copy-start.18 = (bf16[8,352,256]{2,1,0:T(8,128)(2,1)S(1)}, bf16[8,352,256]{2,1,0:T(8,128)(2,1)}, u32[]{:S(2)}) copy-start(bf16[8,352,256]{2,1,0:T(8,128)(2,1)} %copy-done.17) | copy-start | bytes 4325380
  231.3 6.3 %collective-permute-start.22 = (bf16[2,1,2,4,24,704]{5,4,3,2,1,0:T(8,128)(2,1)}, bf16[2,1,2,4,24,704]{5,4,3,2,1,0:T(8,128)(2,1)S(1)}, u32[]{:S(2)}, u32[]{:S(2)}) collective-permute-start(bf16[2,1,2,4,24,704]{5,4,3,2,1,0:T(8,128)(2,1)} %bitcast.219), channel_id=1, source_target_pairs={{0,1},{1,0},{2,3},{3,2},{4,5},{5,4},{6,7},{7,6},{8,9},{9,8},{10,11... | collective-permute-start | bytes 1622024 | tf_op jit(solution)/shard_map/ppermute | solution.py:982
  232.1 19.4 %collective-permute-start.16 = (bf16[4,128,768]{2,1,0:T(8,128)(2,1)}, bf16[4,128,768]{2,1,0:T(8,128)(2,1)S(1)}, u32[]{:S(2)}, u32[]{:S(2)}) collective-permute-start(bf16[4,128,768]{2,1,0:T(8,128)(2,1)} %get-tuple-element.111), channel_id=1, source_target_pairs={{0,2},{2,0},{1,3},{3,1},{4,6},{6,4},{5,7},{7,5},{8,10},{10,8},{9,1... | collective-permute-start | bytes 2359304 | tf_op jit(solution)/shard_map/ppermute | solution.py:982
  236.0 15.5 %copy-start.22 = (bf16[4,128,768]{2,1,0:T(8,128)(2,1)S(1)}, bf16[4,128,768]{2,1,0:T(8,128)(2,1)}, u32[]{:S(2)}) copy-start(bf16[4,128,768]{2,1,0:T(8,128)(2,1)} %get-tuple-element.110) | copy-start | bytes 2359300
  236.1 17.4 %collective-permute-start.20 = (bf16[2,672,256]{2,1,0:T(8,128)(2,1)S(1)}, bf16[2,672,256]{2,1,0:T(8,128)(2,1)S(1)}, u32[]{:S(2)}, u32[]{:S(2)}) collective-permute-start(bf16[2,672,256]{2,1,0:T(8,128)(2,1)S(1)} %dynamic-slice_bitcast_fusion.1), channel_id=1, source_target_pairs={{0,4},{4,0},{1,5},{5,1},{2,6},{6,2},{3,7},{7,3},{8,12},{12,8},{9,1... | collective-permute-start | bytes 2064392 | tf_op jit(solution)/shard_map/ppermute | solution.py:982
  237.8 18.3 %collective-permute-start.23 = (bf16[1,2,4,24,704]{4,3,2,1,0:T(8,128)(2,1)S(1)}, bf16[1,2,4,24,704]{4,3,2,1,0:T(8,128)(2,1)S(1)}, u32[]{:S(2)}, u32[]{:S(2)}) collective-permute-start(bf16[1,2,4,24,704]{4,3,2,1,0:T(8,128)(2,1)S(1)} %dynamic-slice_bitcast_fusion.6), channel_id=1, source_target_pairs={{0,16},{16,0},{1,17},{17,1},{2,18},{18,2},{3,19},{19,3},{4,20},{20... | collective-permute-start | bytes 811016 | tf_op jit(solution)/shard_map/ppermute | solution.py:982
  251.8 17.9 %collective-permute-start.17 = (bf16[2,128,768]{2,1,0:T(8,128)(2,1)S(1)}, bf16[2,128,768]{2,1,0:T(8,128)(2,1)S(1)}, u32[]{:S(2)}, u32[]{:S(2)}) collective-permute-start(bf16[2,128,768]{2,1,0:T(8,128)(2,1)S(1)} %dynamic-slice_bitcast_fusion.4), channel_id=1, source_target_pairs={{0,4},{4,0},{1,5},{5,1},{2,6},{6,2},{3,7},{7,3},{8,12},{12,8},{9,1... | collective-permute-start | bytes 1179656 | tf_op jit(solution)/shard_map/ppermute | solution.py:982
  253.7 23.9 %collective-permute-start.25 = (bf16[672,256]{1,0:T(8,128)(2,1)S(1)}, bf16[672,256]{1,0:T(8,128)(2,1)S(1)}, u32[]{:S(2)}, u32[]{:S(2)}) collective-permute-start(bf16[672,256]{1,0:T(8,128)(2,1)S(1)} %dynamic-slice_bitcast_fusion.5), channel_id=1, source_target_pairs={{0,8},{8,0},{1,9},{9,1},{2,10},{10,2},{3,11},{11,3},{4,12},{12,4},... | collective-permute-start | bytes 1032200 | tf_op jit(solution)/shard_map/ppermute | solution.py:982
  256.2 20.7 %collective-permute-start.24 = (bf16[1,4,24,704]{3,2,1,0:T(8,128)(2,1)S(1)}, bf16[1,4,24,704]{3,2,1,0:T(8,128)(2,1)S(1)}, u32[]{:S(2)}, u32[]{:S(2)}) collective-permute-start(bf16[1,4,24,704]{3,2,1,0:T(8,128)(2,1)S(1)} %dynamic-slice_bitcast_fusion.10), channel_id=1, source_target_pairs={{0,8},{8,0},{1,9},{9,1},{2,10},{10,2},{3,11},{11,3},{4,12},{12,4},... | collective-permute-start | bytes 405512 | tf_op jit(solution)/shard_map/ppermute | solution.py:982
  277.7 9.8 %collective-permute-start.21 = (bf16[128,768]{1,0:T(8,128)(2,1)S(1)}, bf16[128,768]{1,0:T(8,128)(2,1)S(1)}, u32[]{:S(2)}, u32[]{:S(2)}) collective-permute-start(bf16[128,768]{1,0:T(8,128)(2,1)S(1)} %get-tuple-element.136), channel_id=1, source_target_pairs={{0,8},{8,0},{1,9},{9,1},{2,10},{10,2},{3,11},{11,3},{4,12},{12,4},... | collective-permute-start | bytes 589832 | tf_op jit(solution)/shard_map/ppermute | solution.py:982
  277.9 6.7 %collective-permute-start.26 = (bf16[8,24,256]{2,1,0:T(8,128)(2,1)S(1)}, bf16[8,24,256]{2,1,0:T(8,128)(2,1)S(1)}, u32[]{:S(2)}, u32[]{:S(2)}) collective-permute-start(bf16[8,24,256]{2,1,0:T(8,128)(2,1)S(1)} %get-tuple-element.143), channel_id=1, source_target_pairs={{0,1},{1,0},{2,3},{3,2},{4,5},{5,4},{6,7},{7,6},{8,9},{9,8},{10,11... | collective-permute-start | bytes 294920 | tf_op jit(solution)/shard_map/ppermute | solution.py:982
  279.5 10.2 %all-to-all-start.3 = ((bf16[4,24,704]{2,1,0:T(8,128)(2,1)}), bf16[4,24,704]{2,1,0:T(8,128)(2,1)S(1)}, u32[]{:S(2)}, u32[]{:S(2)}) async-start(bf16[4,24,704]{2,1,0:T(8,128)(2,1)} %bitcast.66), calls=%async_computation.3 | async-start | bytes 294912 | tf_op jit(solution)/shard_map/all_to_all | solution.py:1251
  (21 other events, 34.0 us)
Sparse Core Ops, SparseCore 0:
  15.4 105.3 all-gather.1

commit v5 on v4

--- a/solution.py
+++ b/solution.py
@@ -569,7 +569,7 @@
             jax.ShapeDtypeStruct((seqs * local_rows, model), f32),
             jax.ShapeDtypeStruct((seqs * local_rows, model), bf16),
         ],
-        compiler_params=vmem_limit(40),
+        compiler_params=vmem_limit(16),
         cost_estimate=pl.CostEstimate(
             flops=2 * seqs * local_rows * model * model,
             bytes_accessed=2 * model * model,
@@ -830,7 +830,7 @@
             pltpu.VMEM((2, shape.steps, model, PANEL), bf16),
             pltpu.VMEM((3, 2 * half, PANEL), f32),
         ],
-        compiler_params=vmem_limit(40),
+        compiler_params=vmem_limit(26),
         cost_estimate=pl.CostEstimate(
             flops=10 * 2 * half * model * units, bytes_accessed=12 * model * units, transcendentals=0
         ),
@@ -937,7 +937,7 @@
         in_specs=[whole(array) for array in given] + shape.output_specs(),
         out_specs=[whole(array) for array in out_shape],
         out_shape=out_shape,
-        compiler_params=vmem_limit(40),
+        compiler_params=vmem_limit(16),
         cost_estimate=pl.CostEstimate(
             flops=4 * rows * model * model, bytes_accessed=4 * model * model, transcendentals=0
         ),

time: 299 us -> 298 us (level)
  transfers between devices with their start and end apart: 32 -> 32, of which waited for: 18 -> 18; matrix products, arithmetic and copies ran while one was open for 9% -> 9% of each run, Pallas kernels for 25% -> 26%
where the time goes in v5:
time: 298 us; the launch traced here: 297 us
  waiting for transfers between devices  101 us (34%)
  Pallas kernels  86.7 us (29%)
  starting transfers between devices  48.3 us (16%)
  local copies, waits for them, and re-layouts  25 us (8%)
  other arithmetic  19.5 us (7%)
  between operations  15 us (5%)
    ppermute x27, waiting for transfers between devices, swap(): return lax.ppermute(value, axis, [(0, 1), (1, 0)])  84.3 us
    ppermute x27, starting transfers between devices, swap(): return lax.ppermute(value, axis, [(0, 1), (1, 0)])  28 us
    pallas_call x1, Pallas kernels, attend_back(): pl.pallas_call(functools.partial(attend_back_kernel, tile, chunk), grid_s...  24.4 us
    pallas_call x1, Pallas kernels, attend(): pl.pallas_call(functools.partial(attend_kernel, tile, chunk), grid_spec=p...  19.9 us
    pallas_call x1, Pallas kernels, hidden_back(): pl.pallas_call(functools.partial(hidden_back_kernel, shape), grid_spec=pl...  15 us
    all_to_all x1, waiting for transfers between devices, body(): context = lax.all_to_all(context_own, owners, 0, 0, tiled=True)  12 us
    unnamed x78, local copies, waits for them, and re-layouts  10.5 us
    pallas_call x1, Pallas kernels, project_back(): pl.pallas_call(project_back_kernel, grid_spec=pltpu.PrefetchScalarGridSpe...  9.77 us
  transfers between devices with their start and end apart: 32, of which 18 were waited for; matrix products, arithmetic and copies ran while one was open for 9% of the time, Pallas kernels for 26%

profile of v5, /device:TPU:0, one launch (start us, length us, event | category | flops | bytes accessed | tf_op | source)
XLA Modules:
  0.0 296.5 jit_solution(8190891169471466631)
XLA Ops:
  9.5 2.5 dynamic-slice_reduce_fusion.2
  16.6 5.1 %all-to-all-start = ((bf16[4,24,704]{2,1,0:T(8,128)(2,1)}), bf16[4,24,704]{2,1,0:T(8,128)(2,1)S(1)}, u32[]{:S(2)}, u32[]{:S(2)}) async-start(bf16[4,24,704]{2,1,0:T(8,128)(2,1)} %pad_maximum_fusion.6), calls=%async_computation | async-start | bytes 294912 | tf_op jit(solution)/shard_map/all_to_all | solution.py:1062
  21.8 2.7 collective-permute-start
  24.4 4.2 %all-to-all-done = bf16[4,24,704]{2,1,0:T(8,128)(2,1)S(1)} async-done(((bf16[4,24,704]{2,1,0:T(8,128)(2,1)}), bf16[4,24,704]{2,1,0:T(8,128)(2,1)S(1)}, u32[]{:S(2)}, u32[]{:S(2)}) %all-to-all-start) | async-done | bytes 135200 | tf_op jit(solution)/shard_map/all_to_all | solution.py:1062
  28.6 1.2 collective-permute-start.3
  29.8 13.6 %collective-permute-done = bf16[128,768]{1,0:T(8,128)(2,1)S(1)} collective-permute-done((bf16[128,768]{1,0:T(8,128)(2,1)S(1)}, bf16[128,768]{1,0:T(8,128)(2,1)S(1)}, u32[]{:S(2)}, u32[]{:S(2)}) %collective-permute-start) | collective-permute-done | bytes 196640 | tf_op jit(solution)/shard_map/ppermute | solution.py:982
  43.6 4.3 %collective-permute-done.3 = bf16[4,24,704]{2,1,0:T(8,128)(2,1)S(1)} collective-permute-done((bf16[4,24,704]{2,1,0:T(8,128)(2,1)S(1)}, bf16[4,24,704]{2,1,0:T(8,128)(2,1)S(1)}, u32[]{:S(2)}, u32[]{:S(2)}) %collective-permute-start.3) | collective-permute-done | bytes 135200 | tf_op jit(solution)/shard_map/ppermute | solution.py:982
  48.0 1.6 collective-permute-start.4
  49.6 10.0 %collective-permute-done.1 = bf16[2,128,768]{2,1,0:T(8,128)(2,1)S(1)} collective-permute-done((bf16[2,128,768]{2,1,0:T(8,128)(2,1)S(1)}, bf16[2,128,768]{2,1,0:T(8,128)(2,1)S(1)}, u32[]{:S(2)}, u32[]{:S(2)}) %collective-permute-start.1) | collective-permute-done | bytes 393248 | tf_op jit(solution)/shard_map/ppermute | solution.py:982
  59.8 4.8 %collective-permute-start.2 = (bf16[2,2,128,768]{3,2,0,1:T(8,128)(2,1)S(1)}, bf16[2,2,128,768]{3,2,0,1:T(8,128)(2,1)S(1)}, u32[]{:S(2)}, u32[]{:S(2)}) collective-permute-start(bf16[2,2,128,768]{3,2,0,1:T(8,128)(2,1)S(1)} %maximum_select_fusion.3), channel_id=1, source_target_pairs={{0,2},{2,0},{1,3},{3,1},{4,6},{6,4},{5,7},{7,5},{8,10},{10,8},{9,1... | collective-permute-start | bytes 2359304 | tf_op jit(solution)/shard_map/ppermute | solution.py:982
  65.9 1.9 collective-permute-done.5
  67.8 1.5 maximum_select_fusion.1
  69.6 12.8 %collective-permute-done.2 = bf16[2,2,128,768]{3,2,0,1:T(8,128)(2,1)S(1)} collective-permute-done((bf16[2,2,128,768]{3,2,0,1:T(8,128)(2,1)S(1)}, bf16[2,2,128,768]{3,2,0,1:T(8,128)(2,1)S(1)}, u32[]{:S(2)}, u32[]{:S(2)}) %collective-permute-start.2) | collective-permute-done | bytes 786464 | tf_op jit(solution)/shard_map/ppermute | solution.py:982
  82.8 2.7 project.1
  87.6 2.7 fusion.hot_ref
  91.8 2.0 skew.1.table
  93.8 1.7 copy-done.4
  96.4 19.9 %attend.1 = (bf16[8,192,128]{2,1,0:T(8,128)(2,1)}, bf16[3,1024,2048]{2,1,0:T(8,128)(2,1)}, f32[3,1024,128]{2,1,0:T(8,128)}, f32[3,8,1,128]{3,2,1,0:T(1,128)}) custom-call(s32[2]{0:T(128)} %pad_add_fusion.place_ref, bf16[3,1024,64]{2,1,0:T(8,128)(2,1)} %copy-done.16, bf16[3,1024,128]{2,1,0:T(8,128)(2,1)} %copy-done.14, bf16[3,1024,128]{2,1,0:T(8,128)(2,1)} %copy-done.34, ...), custom_call_target="tpu_custom_call" | custom-call | flops 6442450944 | bytes 12582912 | tf_op jit(solution)/shard_map/attend/pallas_call | solution.py:207
  116.3 6.3 %all-to-all-start.1 = ((bf16[8,192,128]{2,1,0:T(8,128)(2,1)}), bf16[8,192,128]{2,1,0:T(8,128)(2,1)S(1)}, u32[]{:S(2)}, u32[]{:S(2)}) async-start(bf16[8,192,128]{2,1,0:T(8,128)(2,1)} %get-tuple-element.72), calls=%async_computation.1 | async-start | bytes 786432 | tf_op jit(solution)/shard_map/all_to_all | solution.py:1133
  122.8 12.0 %all-to-all-done.1.context_ref = bf16[8,192,128]{2,1,0:T(8,128)(2,1)S(1)} async-done(((bf16[8,192,128]{2,1,0:T(8,128)(2,1)}), bf16[8,192,128]{2,1,0:T(8,128)(2,1)S(1)}, u32[]{:S(2)}, u32[]{:S(2)}) %all-to-all-start.1) | async-done | bytes 393248 | tf_op jit(solution)/shard_map/all_to_all | solution.py:1133
  134.9 2.7 copy-done
  138.4 1.7 collective-permute-done.8.normed_other
  140.5 7.8 %hidden_stage.1 = (f32[256,768]{1,0:T(8,128)S(1)}, bf16[256,768]{1,0:T(8,128)(2,1)S(1)}, bf16[512,1024]{1,0:T(8,128)(2,1)S(1)}, bf16[512,1024]{1,0:T(8,128)(2,1)S(1)}, bf16[512,1024]{1,0:T(8,128)(2,1)S(1)}) custom-call(bf16[256,768]{1,0:T(8,128)(2,1)S(1)} %get-tuple-element.74.normed_own, bf16[256,768]{1,0:T(8,128)(2,1)S(1)} %collective-permute-done.8.normed_other, ...), custom_call_target="tpu_custom_call" | custom-call | flops 4026531840 | bytes 9437184 | tf_op jit(solution)/shard_map/hidden_stage/pallas_call | solution.py:814
  148.4 1.7 collective-permute-done.10.norm_other
  150.1 2.4 output_back.1
  154.2 3.6 %all-to-all-start.2 = ((bf16[8,192,128]{2,1,0:T(8,128)(2,1)}), bf16[8,192,128]{2,1,0:T(8,128)(2,1)S(1)}, u32[]{:S(2)}, u32[]{:S(2)}) async-start(bf16[8,192,128]{2,1,0:T(8,128)(2,1)} %get-tuple-element.93), calls=%async_computation.2 | async-start | bytes 786432 | tf_op jit(solution)/shard_map/all_to_all | solution.py:1150
  157.9 2.1 fusion.6.output_ref
  160.0 15.0 %hidden_back.1 = (f32[256,768]{1,0:T(8,128)}, bf16[256,768]{1,0:T(8,128)(2,1)}, bf16[8,352,256]{2,1,0:T(8,128)(2,1)}, bf16[8,352,256]{2,1,0:T(8,128)(2,1)}, bf16...) custom-call(s32[2]{0:T(128)} %pad_add_fusion.1.place_ref, bf16[256,768]{1,0:T(8,128)(2,1)} %copy-done.7, ...), custom_call_target="tpu_custom_call" | custom-call | flops 3221225472 | bytes 9437184 | tf_op jit(solution)/shard_map/hidden_back/pallas_call | solution.py:850
  175.0 2.0 collective-permute-start.13
  177.5 1.6 collective-permute-start.14
  180.5 24.4 %attend_back.1 = (bf16[3,1024,64]{2,1,0:T(8,128)(2,1)}, bf16[3,128,1024]{2,1,0:T(8,128)(2,1)}, bf16[3,128,1024]{2,1,0:T(8,128)(2,1)}, f32[3,1,128]{2,1,0:T(1,128)}) custom-call(s32[2]{0:T(128)} %pad_add_fusion.place_ref, bf16[8,192,128]{2,1,0:T(8,128)(2,1)} %copy-done.24, f32[3,1024,128]{2,1,0:T(8,128)} %get-tuple-element.94.kept_ref, ...), custom_call_target="tpu_custom_call" | custom-call | flops 12884901888 | bytes 12582912 | tf_op jit(solution)/shard_map/attend_back/pallas_call | solution.py:343
  205.0 3.2 %collective-permute-done.14 = bf16[8,320,256]{2,1,0:T(8,128)(2,1)} collective-permute-done((bf16[8,320,256]{2,1,0:T(8,128)(2,1)}, bf16[8,320,256]{2,1,0:T(8,128)(2,1)}, u32[]{:S(2)}, u32[]{:S(2)}) %collective-permute-start.14) | collective-permute-done | bytes 1310752 | tf_op jit(solution)/shard_map/ppermute | solution.py:982
  210.2 1.6 add_convert_fusion.1
  212.8 1.6 collective-permute-start.19
  215.3 1.6 collective-permute-start.18
  216.9 1.9 add_convert_fusion.3
  219.6 9.8 %project_back.1 = (bf16[4,128,768]{2,1,0:T(8,128)(2,1)}, bf16[4,128,768]{2,1,0:T(8,128)(2,1)}, bf16[16,24,704]{2,1,0:T(8,128)(2,1)}, bf16[16,24,704]{2,1,0:T(8,128)(2,1)}) custom-call(s32[2]{0:T(128)} %pad_add_fusion.2.place_ref, bf16[1024,768]{1,0:T(8,128)(2,1)} %copy-done.15, bf16[768,704]{1,0:T(8,128)(2,1)} %bitcast.170, f32[8,768]{1,0:T(8,128)} %stack.227.extra_ref, ...), custom_call_target="tpu_custom_call" | custom-call | flops 1811939328 | bytes 9437184 | tf_op jit(solution)/shard_map/project_back/pallas_call | solution.py:474
  230.2 1.6 collective-permute-start.16
  231.9 1.3 fusion.4
  234.2 1.5 collective-permute-start.20
  235.9 1.6 collective-permute-start.23
  237.6 12.1 %collective-permute-done.16 = bf16[4,128,768]{2,1,0:T(8,128)(2,1)S(1)} collective-permute-done((bf16[4,128,768]{2,1,0:T(8,128)(2,1)}, bf16[4,128,768]{2,1,0:T(8,128)(2,1)S(1)}, u32[]{:S(2)}, u32[]{:S(2)}) %collective-permute-start.16) | collective-permute-done | bytes 786464 | tf_op jit(solution)/shard_map/ppermute | solution.py:982
  249.9 1.6 collective-permute-start.17
  251.8 2.5 collective-permute-start.25
  255.0 12.8 %collective-permute-done.17 = bf16[2,128,768]{2,1,0:T(8,128)(2,1)S(1)} collective-permute-done((bf16[2,128,768]{2,1,0:T(8,128)(2,1)S(1)}, bf16[2,128,768]{2,1,0:T(8,128)(2,1)S(1)}, u32[]{:S(2)}, u32[]{:S(2)}) %collective-permute-start.17) | collective-permute-done | bytes 393248 | tf_op jit(solution)/shard_map/ppermute | solution.py:982
  267.9 7.1 %collective-permute-done.24 = bf16[1,4,24,704]{3,2,1,0:T(8,128)(2,1)S(1)} collective-permute-done((bf16[1,4,24,704]{3,2,1,0:T(8,128)(2,1)S(1)}, bf16[1,4,24,704]{3,2,1,0:T(8,128)(2,1)S(1)}, u32[]{:S(2)}, u32[]{:S(2)}) %collective-permute-start.24) | collective-permute-done | bytes 135200 | tf_op jit(solution)/shard_map/ppermute | solution.py:982
  277.6 5.1 %all-to-all-start.3 = ((bf16[4,24,704]{2,1,0:T(8,128)(2,1)}), bf16[4,24,704]{2,1,0:T(8,128)(2,1)S(1)}, u32[]{:S(2)}, u32[]{:S(2)}) async-start(bf16[4,24,704]{2,1,0:T(8,128)(2,1)} %bitcast.66), calls=%async_computation.3 | async-start | bytes 294912 | tf_op jit(solution)/shard_map/all_to_all | solution.py:1251
  285.7 1.2 rows_stage.1
  (211 shorter events, 34.8 us)
Async XLA Ops:
  7.2 5.4 %copy-start.29 = (bf16[24,768]{1,0:T(8,128)(2,1)S(1)}, bf16[24,768]{1,0:T(8,128)(2,1)}, u32[]{:S(2)}) copy-start(bf16[24,768]{1,0:T(8,128)(2,1)} %param.17) | copy-start | bytes 110596
  7.2 127.7 %all-gather.2.cloned.1.call-start = ((), (), s32[]{:S(2)}) async-start(), calls=%async_computation.4 | async-start | bytes 6266880 | tf_op jit(solution)/shard_map/all_gather | solution.py:1099
  7.2 5.9 %copy-start.25 = (bf16[64,768]{1,0:T(8,128)(2,1)S(1)}, bf16[64,768]{1,0:T(8,128)(2,1)}, u32[]{:S(2)}) copy-start(bf16[64,768]{1,0:T(8,128)(2,1)} %param.20) | copy-start | bytes 294916
  12.6 1.5 collective-permute-start.7
  14.4 7.3 %copy-start.3 = (bf16[2,128,768]{2,1,0:T(8,128)(2,1)S(1)}, bf16[2,128,768]{2,1,0:T(8,128)(2,1)}, u32[]{:S(2)}) copy-start(bf16[2,128,768]{2,1,0:T(8,128)(2,1)} %token_ref.3) | copy-start | bytes 1179652
  16.6 12.0 %all-to-all-start = ((bf16[4,24,704]{2,1,0:T(8,128)(2,1)}), bf16[4,24,704]{2,1,0:T(8,128)(2,1)S(1)}, u32[]{:S(2)}, u32[]{:S(2)}) async-start(bf16[4,24,704]{2,1,0:T(8,128)(2,1)} %pad_maximum_fusion.6), calls=%async_computation | async-start | bytes 294912 | tf_op jit(solution)/shard_map/all_to_all | solution.py:1062
  21.8 21.7 %collective-permute-start = (bf16[128,768]{1,0:T(8,128)(2,1)S(1)}, bf16[128,768]{1,0:T(8,128)(2,1)S(1)}, u32[]{:S(2)}, u32[]{:S(2)}) collective-permute-start(bf16[128,768]{1,0:T(8,128)(2,1)S(1)} %get-tuple-element.139), channel_id=1, source_target_pairs={{0,8},{8,0},{1,9},{9,1},{2,10},{10,2},{3,11},{11,3},{4,12},{12,4},... | collective-permute-start | bytes 589832 | tf_op jit(solution)/shard_map/ppermute | solution.py:982
  28.6 19.3 %collective-permute-start.3 = (bf16[4,24,704]{2,1,0:T(8,128)(2,1)S(1)}, bf16[4,24,704]{2,1,0:T(8,128)(2,1)S(1)}, u32[]{:S(2)}, u32[]{:S(2)}) collective-permute-start(bf16[4,24,704]{2,1,0:T(8,128)(2,1)S(1)} %all-to-all-done), channel_id=1, source_target_pairs={{0,8},{8,0},{1,9},{9,1},{2,10},{10,2},{3,11},{11,3},{4,12},{12,4},... | collective-permute-start | bytes 405512 | tf_op jit(solution)/shard_map/ppermute | solution.py:982
  43.5 16.2 %collective-permute-start.1 = (bf16[2,128,768]{2,1,0:T(8,128)(2,1)S(1)}, bf16[2,128,768]{2,1,0:T(8,128)(2,1)S(1)}, u32[]{:S(2)}, u32[]{:S(2)}) collective-permute-start(bf16[2,128,768]{2,1,0:T(8,128)(2,1)S(1)} %maximum_select_fusion.6), channel_id=1, source_target_pairs={{0,4},{4,0},{1,5},{5,1},{2,6},{6,2},{3,7},{7,3},{8,12},{12,8},{9,1... | collective-permute-start | bytes 1179656 | tf_op jit(solution)/shard_map/ppermute | solution.py:982
  48.0 16.6 %collective-permute-start.4 = (bf16[2,4,24,704]{3,2,1,0:T(8,128)(2,1)S(1)}, bf16[2,4,24,704]{3,2,1,0:T(8,128)(2,1)S(1)}, u32[]{:S(2)}, u32[]{:S(2)}) collective-permute-start(bf16[2,4,24,704]{3,2,1,0:T(8,128)(2,1)S(1)} %maximum_select_fusion.9), channel_id=1, source_target_pairs={{0,16},{16,0},{1,17},{17,1},{2,18},{18,2},{3,19},{19,3},{4,20},{20... | collective-permute-start | bytes 811016 | tf_op jit(solution)/shard_map/ppermute | solution.py:982
  59.7 5.8 %copy-start.30 = (s32[4095]{0:T(1024)S(1)}, s32[4095]{0:T(1024)}, u32[]{:S(2)}) copy-start(s32[4095]{0:T(1024)} %param.24) | copy-start | bytes 49144
  59.8 22.6 %collective-permute-start.2 = (bf16[2,2,128,768]{3,2,0,1:T(8,128)(2,1)S(1)}, bf16[2,2,128,768]{3,2,0,1:T(8,128)(2,1)S(1)}, u32[]{:S(2)}, u32[]{:S(2)}) collective-permute-start(bf16[2,2,128,768]{3,2,0,1:T(8,128)(2,1)S(1)} %maximum_select_fusion.3), channel_id=1, source_target_pairs={{0,2},{2,0},{1,3},{3,1},{4,6},{6,4},{5,7},{7,5},{8,10},{10,8},{9,1... | collective-permute-start | bytes 2359304 | tf_op jit(solution)/shard_map/ppermute | solution.py:982
  65.5 2.3 collective-permute-start.5
  69.3 21.6 %copy-start.5 = (bf16[2,2,4,2,24,704]{5,4,3,2,1,0:T(8,128)(2,1)}, bf16[2,2,4,2,24,704]{5,4,3,2,1,0:T(8,128)(2,1)S(1)}, u32[]{:S(2)}) copy-start(bf16[2,2,4,2,24,704]{5,4,3,2,1,0:T(8,128)(2,1)S(1)} %maximum_select_fusion.1) | copy-start | bytes 3244036
  87.6 6.2 %copy-start.14 = (bf16[3,1024,128]{2,1,0:T(8,128)(2,1)}, bf16[3,1024,128]{2,1,0:T(8,128)(2,1)S(1)}, u32[]{:S(2)}) copy-start(bf16[3,1024,128]{2,1,0:T(8,128)(2,1)S(1)} %get-tuple-element.71.pair_own) | copy-start | bytes 2359300
  87.6 7.9 %collective-permute-start.6 = (bf16[3,1024,128]{2,1,0:T(8,128)(2,1)S(1)}, bf16[3,1024,128]{2,1,0:T(8,128)(2,1)S(1)}, u32[]{:S(2)}, u32[]{:S(2)}) collective-permute-start(bf16[3,1024,128]{2,1,0:T(8,128)(2,1)S(1)} %get-tuple-element.71.pair_own), channel_id=1, source_target_pairs={{0,1},{1,0},{2,3},{3,2},{4,5},{5,4},{6,7},{7,6},{8,9},{9,8},{10,11... | collective-permute-start | bytes 2359304 | tf_op jit(solution)/shard_map/ppermute | solution.py:982
  96.4 26.1 %copy-start.2 = (bf16[2,128,768]{2,1,0:T(8,128)(2,1)S(1)}, bf16[2,128,768]{2,1,0:T(8,128)(2,1)}, u32[]{:S(2)}) copy-start(bf16[2,128,768]{2,1,0:T(8,128)(2,1)} %param.25) | copy-start | bytes 1179652
  116.3 18.6 %all-to-all-start.1 = ((bf16[8,192,128]{2,1,0:T(8,128)(2,1)}), bf16[8,192,128]{2,1,0:T(8,128)(2,1)S(1)}, u32[]{:S(2)}, u32[]{:S(2)}) async-start(bf16[8,192,128]{2,1,0:T(8,128)(2,1)} %get-tuple-element.72), calls=%async_computation.1 | async-start | bytes 786432 | tf_op jit(solution)/shard_map/all_to_all | solution.py:1133
  122.5 15.8 %collective-permute-start.9 = (bf16[256,768]{1,0:T(8,128)(2,1)S(1)}, bf16[256,768]{1,0:T(8,128)(2,1)S(1)}, u32[]{:S(2)}, u32[]{:S(2)}) collective-permute-start(bf16[256,768]{1,0:T(8,128)(2,1)S(1)} %bitcast.164), channel_id=1, source_target_pairs={{0,1},{1,0},{2,3},{3,2},{4,5},{5,4},{6,7},{7,6},{8,9},{9,8},{10,11... | collective-permute-start | bytes 1179656 | tf_op jit(solution)/shard_map/ppermute | solution.py:982
  138.3 10.0 %copy-start.7 = (bf16[256,768]{1,0:T(8,128)(2,1)}, bf16[256,768]{1,0:T(8,128)(2,1)S(1)}, u32[]{:S(2)}) copy-start(bf16[256,768]{1,0:T(8,128)(2,1)S(1)} %get-tuple-element.74.normed_own) | copy-start | bytes 1179652
  138.3 1.8 collective-permute-start.8
  138.4 9.9 %copy-start.6 = (bf16[256,768]{1,0:T(8,128)(2,1)}, bf16[256,768]{1,0:T(8,128)(2,1)S(1)}, u32[]{:S(2)}) copy-start(bf16[256,768]{1,0:T(8,128)(2,1)S(1)} %collective-permute-done.9.down_other) | copy-start | bytes 1179652
  140.5 7.8 %copy-start.8 = (bf16[256,768]{1,0:T(8,128)(2,1)}, bf16[256,768]{1,0:T(8,128)(2,1)S(1)}, u32[]{:S(2)}) copy-start(bf16[256,768]{1,0:T(8,128)(2,1)S(1)} %collective-permute-done.8.normed_other) | copy-start | bytes 1179652
  148.3 4.2 %copy-start.9 = (bf16[512,1024]{1,0:T(8,128)(2,1)}, bf16[512,1024]{1,0:T(8,128)(2,1)S(1)}, u32[]{:S(2)}) copy-start(bf16[512,1024]{1,0:T(8,128)(2,1)S(1)} %get-tuple-element.82.hidden_ref) | copy-start | bytes 3145732
  148.3 1.8 collective-permute-start.10
  153.5 4.4 %collective-permute-start.11 = (bf16[16,24,768]{2,1,0:T(8,128)(2,1)S(1)}, bf16[16,24,768]{2,1,0:T(8,128)(2,1)}, u32[]{:S(2)}, u32[]{:S(2)}) collective-permute-start(bf16[16,24,768]{2,1,0:T(8,128)(2,1)S(1)} %dynamic-slice_bitcast_fusion.3), channel_id=1, source_target_pairs={{0,1},{1,0},{2,3},{3,2},{4,5},{5,4},{6,7},{7,6},{8,9},{9,8},{10,11... | collective-permute-start | bytes 1769480 | tf_op jit(solution)/shard_map/ppermute | solution.py:982
  154.2 25.5 %all-to-all-start.2 = ((bf16[8,192,128]{2,1,0:T(8,128)(2,1)}), bf16[8,192,128]{2,1,0:T(8,128)(2,1)S(1)}, u32[]{:S(2)}, u32[]{:S(2)}) async-start(bf16[8,192,128]{2,1,0:T(8,128)(2,1)} %get-tuple-element.93), calls=%async_computation.2 | async-start | bytes 786432 | tf_op jit(solution)/shard_map/all_to_all | solution.py:1150
  175.0 33.9 %collective-permute-start.13 = (bf16[8,352,256]{2,1,0:T(8,128)(2,1)}, bf16[8,352,256]{2,1,0:T(8,128)(2,1)S(1)}, u32[]{:S(2)}, u32[]{:S(2)}) collective-permute-start(bf16[8,352,256]{2,1,0:T(8,128)(2,1)} %get-tuple-element.91), channel_id=1, source_target_pairs={{0,2},{2,0},{1,3},{3,1},{4,6},{6,4},{5,7},{7,5},{8,10},{10,8},{9,1... | collective-permute-start | bytes 4325384 | tf_op jit(solution)/shard_map/ppermute | solution.py:982
  177.5 30.6 %collective-permute-start.14 = (bf16[8,320,256]{2,1,0:T(8,128)(2,1)}, bf16[8,320,256]{2,1,0:T(8,128)(2,1)}, u32[]{:S(2)}, u32[]{:S(2)}) collective-permute-start(bf16[8,320,256]{2,1,0:T(8,128)(2,1)} %get-tuple-element.92), channel_id=1, source_target_pairs={{0,16},{16,0},{1,17},{17,1},{2,18},{18,2},{3,19},{19,3},{4,20},{20... | collective-permute-start | bytes 3932168 | tf_op jit(solution)/shard_map/ppermute | solution.py:982
  179.8 37.2 %collective-permute-start.12 = (bf16[256,768]{1,0:T(8,128)(2,1)}, bf16[256,768]{1,0:T(8,128)(2,1)}, u32[]{:S(2)}, u32[]{:S(2)}) collective-permute-start(bf16[256,768]{1,0:T(8,128)(2,1)} %get-tuple-element.87), channel_id=1, source_target_pairs={{0,1},{1,0},{2,3},{3,2},{4,5},{5,4},{6,7},{7,6},{8,9},{9,8},{10,11... | collective-permute-start | bytes 1179656 | tf_op jit(solution)/shard_map/ppermute | solution.py:982
  180.5 28.3 %copy-start.19 = (bf16[8,352,256]{2,1,0:T(8,128)(2,1)S(1)}, bf16[8,352,256]{2,1,0:T(8,128)(2,1)}, u32[]{:S(2)}) copy-start(bf16[8,352,256]{2,1,0:T(8,128)(2,1)} %get-tuple-element.102) | copy-start | bytes 4325380
  208.8 10.8 %collective-permute-start.15 = (bf16[3,128,1024]{2,1,0:T(8,128)(2,1)}, bf16[3,128,1024]{2,1,0:T(8,128)(2,1)}, u32[]{:S(2)}, u32[]{:S(2)}) collective-permute-start(bf16[3,128,1024]{2,1,0:T(8,128)(2,1)} %get-tuple-element.109), channel_id=1, source_target_pairs={{0,1},{1,0},{2,3},{3,2},{4,5},{5,4},{6,7},{7,6},{8,9},{9,8},{10,11... | collective-permute-start | bytes 2359304 | tf_op jit(solution)/shard_map/ppermute | solution.py:982
  209.3 5.1 %copy-start.17 = (bf16[8,352,256]{2,1,0:T(8,128)(2,1)}, bf16[8,352,256]{2,1,0:T(8,128)(2,1)S(1)}, u32[]{:S(2)}) copy-start(bf16[8,352,256]{2,1,0:T(8,128)(2,1)S(1)} %add_convert_fusion) | copy-start | bytes 4325380
  211.8 5.1 %copy-start.21 = (f32[256,768]{1,0:T(8,128)S(1)}, f32[256,768]{1,0:T(8,128)}, u32[]{:S(2)}) copy-start(f32[256,768]{1,0:T(8,128)} %get-tuple-element.86) | copy-start | bytes 2359300
  212.8 17.5 %collective-permute-start.19 = (bf16[4,320,256]{2,1,0:T(8,128)(2,1)}, bf16[4,320,256]{2,1,0:T(8,128)(2,1)}, u32[]{:S(2)}, u32[]{:S(2)}) collective-permute-start(bf16[4,320,256]{2,1,0:T(8,128)(2,1)} %dynamic-slice_bitcast_fusion.2), channel_id=1, source_target_pairs={{0,2},{2,0},{1,3},{3,1},{4,6},{6,4},{5,7},{7,5},{8,10},{10,8},{9,1... | collective-permute-start | bytes 1966088 | tf_op jit(solution)/shard_map/ppermute | solution.py:982
  215.3 18.5 %collective-permute-start.18 = (bf16[4,352,256]{2,1,0:T(8,128)(2,1)}, bf16[4,352,256]{2,1,0:T(8,128)(2,1)S(1)}, u32[]{:S(2)}, u32[]{:S(2)}) collective-permute-start(bf16[4,352,256]{2,1,0:T(8,128)(2,1)} %dynamic-slice_bitcast_fusion), channel_id=1, source_target_pairs={{0,16},{16,0},{1,17},{17,1},{2,18},{18,2},{3,19},{19,3},{4,20},{20... | collective-permute-start | bytes 2162696 | tf_op jit(solution)/shard_map/ppermute | solution.py:982
  229.4 4.4 %copy-start.18 = (bf16[8,352,256]{2,1,0:T(8,128)(2,1)S(1)}, bf16[8,352,256]{2,1,0:T(8,128)(2,1)}, u32[]{:S(2)}) copy-start(bf16[8,352,256]{2,1,0:T(8,128)(2,1)} %copy-done.17) | copy-start | bytes 4325380
  229.4 6.3 %collective-permute-start.22 = (bf16[2,1,2,4,24,704]{5,4,3,2,1,0:T(8,128)(2,1)}, bf16[2,1,2,4,24,704]{5,4,3,2,1,0:T(8,128)(2,1)S(1)}, u32[]{:S(2)}, u32[]{:S(2)}) collective-permute-start(bf16[2,1,2,4,24,704]{5,4,3,2,1,0:T(8,128)(2,1)} %bitcast.219), channel_id=1, source_target_pairs={{0,1},{1,0},{2,3},{3,2},{4,5},{5,4},{6,7},{7,6},{8,9},{9,8},{10,11... | collective-permute-start | bytes 1622024 | tf_op jit(solution)/shard_map/ppermute | solution.py:982
  230.2 19.4 %collective-permute-start.16 = (bf16[4,128,768]{2,1,0:T(8,128)(2,1)}, bf16[4,128,768]{2,1,0:T(8,128)(2,1)S(1)}, u32[]{:S(2)}, u32[]{:S(2)}) collective-permute-start(bf16[4,128,768]{2,1,0:T(8,128)(2,1)} %get-tuple-element.111), channel_id=1, source_target_pairs={{0,2},{2,0},{1,3},{3,1},{4,6},{6,4},{5,7},{7,5},{8,10},{10,8},{9,1... | collective-permute-start | bytes 2359304 | tf_op jit(solution)/shard_map/ppermute | solution.py:982
  234.2 15.5 %copy-start.22 = (bf16[4,128,768]{2,1,0:T(8,128)(2,1)S(1)}, bf16[4,128,768]{2,1,0:T(8,128)(2,1)}, u32[]{:S(2)}) copy-start(bf16[4,128,768]{2,1,0:T(8,128)(2,1)} %get-tuple-element.110) | copy-start | bytes 2359300
  234.2 17.4 %collective-permute-start.20 = (bf16[2,672,256]{2,1,0:T(8,128)(2,1)S(1)}, bf16[2,672,256]{2,1,0:T(8,128)(2,1)S(1)}, u32[]{:S(2)}, u32[]{:S(2)}) collective-permute-start(bf16[2,672,256]{2,1,0:T(8,128)(2,1)S(1)} %dynamic-slice_bitcast_fusion.1), channel_id=1, source_target_pairs={{0,4},{4,0},{1,5},{5,1},{2,6},{6,2},{3,7},{7,3},{8,12},{12,8},{9,1... | collective-permute-start | bytes 2064392 | tf_op jit(solution)/shard_map/ppermute | solution.py:982
  235.9 18.3 %collective-permute-start.23 = (bf16[1,2,4,24,704]{4,3,2,1,0:T(8,128)(2,1)S(1)}, bf16[1,2,4,24,704]{4,3,2,1,0:T(8,128)(2,1)S(1)}, u32[]{:S(2)}, u32[]{:S(2)}) collective-permute-start(bf16[1,2,4,24,704]{4,3,2,1,0:T(8,128)(2,1)S(1)} %dynamic-slice_bitcast_fusion.6), channel_id=1, source_target_pairs={{0,16},{16,0},{1,17},{17,1},{2,18},{18,2},{3,19},{19,3},{4,20},{20... | collective-permute-start | bytes 811016 | tf_op jit(solution)/shard_map/ppermute | solution.py:982
  249.9 17.9 %collective-permute-start.17 = (bf16[2,128,768]{2,1,0:T(8,128)(2,1)S(1)}, bf16[2,128,768]{2,1,0:T(8,128)(2,1)S(1)}, u32[]{:S(2)}, u32[]{:S(2)}) collective-permute-start(bf16[2,128,768]{2,1,0:T(8,128)(2,1)S(1)} %dynamic-slice_bitcast_fusion.4), channel_id=1, source_target_pairs={{0,4},{4,0},{1,5},{5,1},{2,6},{6,2},{3,7},{7,3},{8,12},{12,8},{9,1... | collective-permute-start | bytes 1179656 | tf_op jit(solution)/shard_map/ppermute | solution.py:982
  251.8 23.9 %collective-permute-start.25 = (bf16[672,256]{1,0:T(8,128)(2,1)S(1)}, bf16[672,256]{1,0:T(8,128)(2,1)S(1)}, u32[]{:S(2)}, u32[]{:S(2)}) collective-permute-start(bf16[672,256]{1,0:T(8,128)(2,1)S(1)} %dynamic-slice_bitcast_fusion.5), channel_id=1, source_target_pairs={{0,8},{8,0},{1,9},{9,1},{2,10},{10,2},{3,11},{11,3},{4,12},{12,4},... | collective-permute-start | bytes 1032200 | tf_op jit(solution)/shard_map/ppermute | solution.py:982
  254.4 20.7 %collective-permute-start.24 = (bf16[1,4,24,704]{3,2,1,0:T(8,128)(2,1)S(1)}, bf16[1,4,24,704]{3,2,1,0:T(8,128)(2,1)S(1)}, u32[]{:S(2)}, u32[]{:S(2)}) collective-permute-start(bf16[1,4,24,704]{3,2,1,0:T(8,128)(2,1)S(1)} %dynamic-slice_bitcast_fusion.10), channel_id=1, source_target_pairs={{0,8},{8,0},{1,9},{9,1},{2,10},{10,2},{3,11},{11,3},{4,12},{12,4},... | collective-permute-start | bytes 405512 | tf_op jit(solution)/shard_map/ppermute | solution.py:982
  275.9 9.9 %collective-permute-start.21 = (bf16[128,768]{1,0:T(8,128)(2,1)S(1)}, bf16[128,768]{1,0:T(8,128)(2,1)S(1)}, u32[]{:S(2)}, u32[]{:S(2)}) collective-permute-start(bf16[128,768]{1,0:T(8,128)(2,1)S(1)} %get-tuple-element.136), channel_id=1, source_target_pairs={{0,8},{8,0},{1,9},{9,1},{2,10},{10,2},{3,11},{11,3},{4,12},{12,4},... | collective-permute-start | bytes 589832 | tf_op jit(solution)/shard_map/ppermute | solution.py:982
  276.0 6.7 %collective-permute-start.26 = (bf16[8,24,256]{2,1,0:T(8,128)(2,1)S(1)}, bf16[8,24,256]{2,1,0:T(8,128)(2,1)S(1)}, u32[]{:S(2)}, u32[]{:S(2)}) collective-permute-start(bf16[8,24,256]{2,1,0:T(8,128)(2,1)S(1)} %get-tuple-element.143), channel_id=1, source_target_pairs={{0,1},{1,0},{2,3},{3,2},{4,5},{5,4},{6,7},{7,6},{8,9},{9,8},{10,11... | collective-permute-start | bytes 294920 | tf_op jit(solution)/shard_map/ppermute | solution.py:982
  277.6 10.2 %all-to-all-start.3 = ((bf16[4,24,704]{2,1,0:T(8,128)(2,1)}), bf16[4,24,704]{2,1,0:T(8,128)(2,1)S(1)}, u32[]{:S(2)}, u32[]{:S(2)}) async-start(bf16[4,24,704]{2,1,0:T(8,128)(2,1)} %bitcast.66), calls=%async_computation.3 | async-start | bytes 294912 | tf_op jit(solution)/shard_map/all_to_all | solution.py:1251
  (21 other events, 40.5 us)
Sparse Core Ops, SparseCore 0:
  15.4 105.3 all-gather.1
